TPU v7x, 256 devices: a whole 4x4x8 slice. The times are simulated.
256 devices in a mesh: particle: 16 (over z_hi, y), space: 16 (over x, z_lo, core).
Axes of the slice: x: 4, y: 4, z: 8 (z_hi: 4, z_lo: 2; z = z_hi * 2 + z_lo), core: 2. Of those that a mesh axis runs over, the one named last changes fastest.
Arguments:
- ensemble: float32 [16, 13, 512, 1024], P('particle', None, 'space'), may hold values from -6 to 6
- ancestors: int32 [16], replicated, may hold values from 0 to 15
- depth_levels: int32 [512, 1024], P('space'), may hold values from 0 to 4
- level_coefs: float32 [3, 4], replicated, may hold values from 0.25 to 1
- altimetry: float32 [3, 64, 512], P(None, 'particle', 'space'), may hold values from -6 to 6
- obs_rows: int32 [3, 64], replicated, may hold values from 0 to 1023, as said below
Outputs:
- forecast: float32 [16, 13, 512, 1024], P('particle', None, 'space')
Inputs may be any that keep to these rules, and one draw needn't show every extreme that they name: `obs_rows`: within one step the indices are distinct.
All inputs are finite; a program needn't handle non-finite values.
Results may differ from a plain program's by a relative error of at most 0.00013.
Values sent between devices are 32-bit elements; how exact they have to be, the bound alone decides.
A program may use at most 128 MiB of HBM per device.

v0:
```python
import jax
import jax.numpy as jnp
from jax import lax
from jax.sharding import PartitionSpec as P

STEPS = 3


DT = 0.2
CORIOLIS = 0.5
GRAVITY = 1.0
NUDGE = 0.5


def with_halo(block, sides, width):
    for axis, dim in sides:
        count = lax.axis_size(axis)
        forward = [(i, i + 1) for i in range(count - 1)]
        forward.append((count - 1, 0))
        backward = [(target, source) for source, target in forward]
        low = lax.ppermute(
            lax.slice_in_dim(block, block.shape[dim] - width, None, axis=dim), axis, forward
        )
        high = lax.ppermute(lax.slice_in_dim(block, 0, width, axis=dim), axis, backward)
        block = jnp.concatenate([low, block, high], axis=dim)
    return block


def pad_second(field):
    return jnp.pad(field, [(0, 0)] * (field.ndim - 1) + [(1, 1)])


def gradients(wide):
    center = wide[:, 1:-1]
    east = wide[:, 2:]
    west = wide[:, :-2]
    padded = pad_second(center)
    ddx = (east - west) * 0.5
    ddy = (padded[..., 2:] - padded[..., :-2]) * 0.5
    laplace = east + west + padded[..., 2:] + padded[..., :-2] - 4.0 * center
    return (center, ddx, ddy, laplace)


def widen_state(field):
    return with_halo(field, (("space", 1),), 1)


def widen_surface(field):
    return with_halo(field, (("space", 1),), 1)


def level_terms(coefs):
    thick = coefs[0][:, None, None]
    visc = 0.2 * coefs[1][:, None, None]
    kappa = 0.2 * coefs[2][:, None, None]
    return (thick, visc, kappa)


def finish(center, ddx, ddy, laplace, masks, visc, kappa, grad_x, grad_y, height_two):
    levels = masks.shape[0]
    east_vel = center[:levels]
    north_vel = center[levels : 2 * levels]
    temper = center[2 * levels : 3 * levels]
    east_new = masks * (
        east_vel + DT * (CORIOLIS * north_vel - GRAVITY * grad_x + visc * laplace[:levels])
    )
    north_new = masks * (
        north_vel
        + DT * (-CORIOLIS * east_vel - GRAVITY * grad_y + visc * laplace[levels : 2 * levels])
    )
    temper_new = masks * (
        temper
        + DT
        * (
            kappa * laplace[2 * levels : 3 * levels]
            - east_vel * ddx[2 * levels : 3 * levels]
            - north_vel * ddy[2 * levels : 3 * levels]
        )
    )
    return jnp.concatenate([east_new, north_new, temper_new, height_two[None]], axis=0)


def one_step(state, masks, coefs, target, hit):
    levels = masks.shape[0]
    surface = masks[0]
    center, ddx, ddy, laplace = gradients(widen_state(state))
    height = center[3 * levels]
    thick, visc, kappa = level_terms(coefs)
    spread = ddx[:levels] + ddy[levels : 2 * levels]
    height_one = surface * (height - DT * jnp.sum(thick * masks * spread, axis=0))
    height_two = surface * (height_one + NUDGE * hit * (target - height_one))
    unused, grad_x, grad_y, unused_lap = gradients(widen_surface(height_two[None]))
    return finish(center, ddx, ddy, laplace, masks, visc, kappa, grad_x, grad_y, height_two)


def per_device(ensemble, ancestors, depth_levels, level_coefs, altimetry, obs_rows):
    levels = level_coefs.shape[1]
    width_y = ensemble.shape[3]
    mine = ancestors[lax.axis_index("particle")]
    piece = lax.all_gather(ensemble, "particle", axis=0, tiled=True)
    count = piece.shape[0]
    inside = (mine >= 0) & (mine < count)
    chosen = lax.dynamic_index_in_dim(piece, jnp.clip(mine, 0, count - 1), 0, keepdims=False)
    state = jnp.where(inside, chosen, jnp.zeros(ensemble.shape[1:], jnp.float32))
    level_ids = jnp.arange(levels, dtype=jnp.int32)
    masks = (level_ids[:, None, None] < depth_levels[None]).astype(jnp.float32)
    full_mask = jnp.concatenate([masks, masks, masks, masks[:1]], axis=0)
    state = state * full_mask
    columns = jnp.arange(width_y, dtype=jnp.int32)
    for step in range(STEPS):
        lines = lax.all_gather(altimetry[step], "particle", axis=0, tiled=True)
        onehot = (obs_rows[step][:, None] == columns[None, :]).astype(jnp.float32)
        target = jnp.dot(
            lines.T, onehot, precision=lax.Precision.HIGHEST, preferred_element_type=jnp.float32
        )
        hit = jnp.sum(onehot, axis=0)[None, :]
        state = one_step(state, masks, level_coefs, target, hit)
    return state[None]


def solution(mesh):
    in_specs = (
        P("particle", None, "space", None),
        P(),
        P("space", None),
        P(),
        P(None, "particle", "space"),
        P(),
    )
    out_specs = P("particle", None, "space", None)
    return jax.shard_map(
        per_device, mesh=mesh, in_specs=in_specs, out_specs=out_specs, check_vma=False
    )
```

profile of v0, /device:TPU:24, one launch (start us, length us, event | category | flops | bytes accessed | tf_op | source)
XLA Modules:
  0.0 478.2 jit_solution(3686461918665860004)
XLA Ops:
  6.6 0.7 all-gather.5.cloned.1.call-update
  7.3 0.6 dynamic_slice.7
  9.9 0.1 convert_reduce_fusion.2
  10.1 311.8 %all-gather.5.cloned.1.call-done = f32[16,13,32,1024]{3,2,1,0:T(8,128)} async-done(((f32[1,13,32,1024]{3,2,1,0:T(8,128)}), f32[16,13,32,1024]{3,2,1,0:T(8,128)}) %all-gather.5.cloned.1.call-update) | async-done | bytes 27262992 | tf_op jit(solution)/shard_map/all_gather | solution.py:100
  321.9 1.7 maximum_multiply_fusion
  323.7 0.1 collective-permute-start
  323.8 0.5 collective-permute-start.1
  324.3 35.5 %all-gather = f32[1,64,32]{2,0,1:T(1,128)S(1)} all-gather(f32[1,4,32]{2,0,1:T(1,128)S(1)} %bitcast.108), channel_id=2, replica_groups=mesh['particle'=16,'space'=16] {'particle'}, dimensions={1}, use_global_device_ids=true | all-gather | bytes 8704 | tf_op jit(solution)/shard_map/all_gather | solution.py:111
  359.8 1.8 multiply_subtract_fusion.2
  361.7 0.2 fusion.13
  361.8 0.3 fusion.3
  362.1 0.1 collective-permute-start.2
  362.2 0.5 collective-permute-start.3
  362.7 0.1 convert_reduce_fusion.1
  362.8 0.7 collective-permute-done.2
  363.6 3.9 collective-permute-done.3
  367.5 0.1 fusion.73
  367.6 0.6 fusion.54
  368.2 0.2 pad_maximum_fusion.18
  368.5 0.1 collective-permute-start.4
  368.6 0.5 collective-permute-start.5
  369.1 43.4 %all-gather.1 = f32[1,64,32]{2,0,1:T(1,128)S(1)} all-gather(f32[1,4,32]{2,0,1:T(1,128)S(1)} %bitcast.107), channel_id=3, replica_groups=mesh['particle'=16,'space'=16] {'particle'}, dimensions={1}, use_global_device_ids=true | all-gather | bytes 8704 | tf_op jit(solution)/shard_map/all_gather | solution.py:111
  412.4 0.4 subtract_multiply_fusion.3
  412.9 2.1 multiply_subtract_fusion.1
  415.0 0.5 fusion.32
  415.5 0.3 fusion.7
  415.8 0.1 collective-permute-start.6
  415.9 0.5 collective-permute-start.7
  416.4 0.1 convert_reduce_fusion
  416.5 0.7 collective-permute-done.6
  417.3 4.1 collective-permute-done.7
  421.3 0.1 fusion.70
  421.5 0.4 fusion.41
  421.9 0.2 pad_maximum_fusion.19
  422.2 0.1 collective-permute-start.8
  422.3 0.5 collective-permute-start.9
  422.8 38.1 %all-gather.2 = f32[1,64,32]{2,0,1:T(1,128)S(1)} all-gather(f32[1,4,32]{2,0,1:T(1,128)S(1)} %bitcast.106), channel_id=4, replica_groups=mesh['particle'=16,'space'=16] {'particle'}, dimensions={1}, use_global_device_ids=true | all-gather | bytes 8704 | tf_op jit(solution)/shard_map/all_gather | solution.py:111
  460.9 0.4 subtract_multiply_fusion.1
  461.3 2.1 multiply_subtract_fusion
  463.4 0.5 fusion.19
  463.9 0.3 fusion.12
  464.2 0.1 collective-permute-start.10
  464.3 0.5 collective-permute-start.11
  464.8 0.8 collective-permute-done.10
  465.7 3.9 collective-permute-done.11
  469.6 0.1 fusion.67
  469.7 0.4 fusion.28
  470.1 1.3 maximum_bitcast_fusion
  (31 shorter events, 0.4 us)
Async XLA Ops:
  6.5 0.7 copy-start.4
  6.5 3.3 copy-start
  6.5 3.4 copy-start.2
  6.5 3.5 copy-start.1
  6.5 315.4 %all-gather.5.cloned.1.call-start = ((), (), s32[]{:S(2)}) async-start(), calls=%async_computation | async-start | bytes 28966912 | tf_op jit(solution)/shard_map/all_gather | solution.py:100
  321.9 2.4 copy-start.3
  323.7 36.1 %collective-permute-start = (f32[13,1,1024]{2,1,0:T(1,128)S(1)}, f32[13,1,1024]{2,1,0:T(1,128)S(1)}, u32[]{:S(2)}, u32[]{:S(2)}) collective-permute-start(f32[13,1,1024]{2,1,0:T(1,128)S(1)} %get-tuple-element.28), channel_id=1, source_target_pairs={{1,0},{2,1},{3,2},{4,3},{5,4},{6,5},{7,6},{8,7},{9,8},{10,9},{11,1... | collective-permute-start | bytes 159752 | tf_op jit(solution)/shard_map/ppermute | solution.py:24
  323.8 36.0 %collective-permute-start.1 = (f32[13,1,1024]{2,1,0:T(1,128)S(1)}, f32[13,1,1024]{2,1,0:T(1,128)S(1)}, u32[]{:S(2)}, u32[]{:S(2)}) collective-permute-start(f32[13,1,1024]{2,1,0:T(1,128)S(1)} %get-tuple-element.27), channel_id=1, source_target_pairs={{0,1},{1,2},{2,3},{3,4},{4,5},{5,6},{6,7},{7,8},{8,9},{9,10},{10,1... | collective-permute-start | bytes 159752 | tf_op jit(solution)/shard_map/ppermute | solution.py:21
  362.1 1.4 collective-permute-start.2
  362.2 5.2 %collective-permute-start.3 = (f32[1,1,1024]{2,1,0:T(1,128)S(1)}, f32[1,1,1024]{2,1,0:T(1,128)S(1)}, u32[]{:S(2)}, u32[]{:S(2)}) collective-permute-start(f32[1,1,1024]{2,1,0:T(1,128)S(1)} %get-tuple-element.40), channel_id=1, source_target_pairs={{0,1},{1,2},{2,3},{3,4},{4,5},{5,6},{6,7},{7,8},{8,9},{9,10},{10,1... | collective-permute-start | bytes 12296 | tf_op jit(solution)/shard_map/ppermute | solution.py:21
  368.5 43.9 %collective-permute-start.4 = (f32[13,1,1024]{2,1,0:T(1,128)S(1)}, f32[13,1,1024]{2,1,0:T(1,128)S(1)}, u32[]{:S(2)}, u32[]{:S(2)}) collective-permute-start(f32[13,1,1024]{2,1,0:T(1,128)S(1)} %get-tuple-element.25), channel_id=1, source_target_pairs={{1,0},{2,1},{3,2},{4,3},{5,4},{6,5},{7,6},{8,7},{9,8},{10,9},{11,1... | collective-permute-start | bytes 159752 | tf_op jit(solution)/shard_map/ppermute | solution.py:24
  368.6 43.9 %collective-permute-start.5 = (f32[13,1,1024]{2,1,0:T(1,128)S(1)}, f32[13,1,1024]{2,1,0:T(1,128)S(1)}, u32[]{:S(2)}, u32[]{:S(2)}) collective-permute-start(f32[13,1,1024]{2,1,0:T(1,128)S(1)} %get-tuple-element.24), channel_id=1, source_target_pairs={{0,1},{1,2},{2,3},{3,4},{4,5},{5,6},{6,7},{7,8},{8,9},{9,10},{10,1... | collective-permute-start | bytes 159752 | tf_op jit(solution)/shard_map/ppermute | solution.py:21
  415.8 1.4 collective-permute-start.6
  415.9 5.4 %collective-permute-start.7 = (f32[1,1,1024]{2,1,0:T(1,128)S(1)}, f32[1,1,1024]{2,1,0:T(1,128)S(1)}, u32[]{:S(2)}, u32[]{:S(2)}) collective-permute-start(f32[1,1,1024]{2,1,0:T(1,128)S(1)} %get-tuple-element.36), channel_id=1, source_target_pairs={{0,1},{1,2},{2,3},{3,4},{4,5},{5,6},{6,7},{7,8},{8,9},{9,10},{10,1... | collective-permute-start | bytes 12296 | tf_op jit(solution)/shard_map/ppermute | solution.py:21
  422.2 38.7 %collective-permute-start.8 = (f32[13,1,1024]{2,1,0:T(1,128)S(1)}, f32[13,1,1024]{2,1,0:T(1,128)S(1)}, u32[]{:S(2)}, u32[]{:S(2)}) collective-permute-start(f32[13,1,1024]{2,1,0:T(1,128)S(1)} %get-tuple-element.21), channel_id=1, source_target_pairs={{1,0},{2,1},{3,2},{4,3},{5,4},{6,5},{7,6},{8,7},{9,8},{10,9},{11,1... | collective-permute-start | bytes 159752 | tf_op jit(solution)/shard_map/ppermute | solution.py:24
  422.3 38.6 %collective-permute-start.9 = (f32[13,1,1024]{2,1,0:T(1,128)S(1)}, f32[13,1,1024]{2,1,0:T(1,128)S(1)}, u32[]{:S(2)}, u32[]{:S(2)}) collective-permute-start(f32[13,1,1024]{2,1,0:T(1,128)S(1)} %get-tuple-element.20), channel_id=1, source_target_pairs={{0,1},{1,2},{2,3},{3,4},{4,5},{5,6},{6,7},{7,8},{8,9},{9,10},{10,1... | collective-permute-start | bytes 159752 | tf_op jit(solution)/shard_map/ppermute | solution.py:21
  464.2 1.4 collective-permute-start.10
  464.3 5.2 %collective-permute-start.11 = (f32[1,1,1024]{2,1,0:T(1,128)S(1)}, f32[1,1,1024]{2,1,0:T(1,128)S(1)}, u32[]{:S(2)}, u32[]{:S(2)}) collective-permute-start(f32[1,1,1024]{2,1,0:T(1,128)S(1)} %get-tuple-element.32), channel_id=1, source_target_pairs={{0,1},{1,2},{2,3},{3,4},{4,5},{5,6},{6,7},{7,8},{8,9},{9,10},{10,1... | collective-permute-start | bytes 12296 | tf_op jit(solution)/shard_map/ppermute | solution.py:21
Sparse Core Ops, SparseCore 0:
  9.8 312.0 all-gather.4
where the time goes:
time: 483 us; the launch traced here: 478 us
  waiting for transfers between devices  327 us (68%)
  blocking collectives  117 us (24%)
  between operations  15.7 us (3%)
  other arithmetic  13.6 us (3%)
    all_gather x1, waiting for transfers between devices, per_device(): piece = lax.all_gather(ensemble, 'particle', axis=0, tiled=True)  312 us
    all_gather x3, blocking collectives, per_device(): lines = lax.all_gather(altimetry[step], 'particle', axis=0, tiled=True)  117 us
    ppermute x6, waiting for transfers between devices, with_halo(): lax.ppermute(lax.slice_in_dim(block, block.shape[dim] - width, None, axis...  11.9 us
  transfers between devices with their start and end apart: 13, of which 7 were waited for; matrix products, arithmetic and copies ran while one was open for 0% of the time, Pallas kernels for 0%

commit v1 on v0

--- a/solution.py
+++ b/solution.py
@@ -1,7 +1,13 @@
+import functools
+
 import jax
 import jax.numpy as jnp
 from jax import lax
+from jax.experimental import pallas as pl
+from jax.experimental.pallas import tpu as pltpu
 from jax.sharding import PartitionSpec as P
+
+MESH = pl.DeviceIdType.MESH
 
 STEPS = 3
 
@@ -93,22 +99,135 @@
     return finish(center, ddx, ddy, laplace, masks, visc, kappa, grad_x, grad_y, height_two)
 
 
+def window(source, grid_cols, rows, cols):
+    return (pl.ds((source // grid_cols) * rows, rows), pl.ds((source % grid_cols) * cols, cols))
+
+
+def exchange_kernel(
+    count, grid_cols, anc_ref, ens_ref, alt_ref, out_ref, lines_ref,
+    held, outgoing, send1, recv1, send2, recv2, send3, recv3, local,
+):
+    me = lax.axis_index("particle")
+    rows, cols = held.shape[2], held.shape[3]
+
+    barrier = pltpu.get_barrier_semaphore()
+    for offset in range(1, count):
+        peer = lax.rem(me + offset, count)
+        pl.semaphore_signal(barrier, inc=1, device_id={"particle": peer}, device_id_type=MESH)
+    pl.semaphore_wait(barrier, count - 1)
+
+    def chunk_of(dest):
+        r, c = window(dest, grid_cols, rows, cols)
+        return ens_ref.at[:, r, c]
+
+    own = pltpu.make_async_copy(chunk_of(me), held.at[me], local.at[0])
+    own.start()
+    own_lines = pltpu.make_async_copy(alt_ref, lines_ref.at[me], local.at[1])
+    own_lines.start()
+    first = []
+    for offset in range(1, count):
+        peer = lax.rem(me + offset, count)
+        copy = pltpu.make_async_remote_copy(
+            src_ref=chunk_of(peer), dst_ref=held.at[me], send_sem=send1.at[offset],
+            recv_sem=recv1.at[me], device_id={"particle": peer}, device_id_type=MESH,
+        )
+        copy.start()
+        lines = pltpu.make_async_remote_copy(
+            src_ref=alt_ref, dst_ref=lines_ref.at[me], send_sem=send3.at[offset],
+            recv_sem=recv3.at[me], device_id={"particle": peer}, device_id_type=MESH,
+        )
+        lines.start()
+        first.append((copy, lines))
+    own.wait()
+    own_lines.wait()
+    for offset, (copy, lines) in zip(range(1, count), first):
+        sender = lax.rem(me + count - offset, count)
+        copy.wait_send()
+        lines.wait_send()
+        pltpu.make_async_remote_copy(
+            src_ref=chunk_of(me), dst_ref=held.at[sender], send_sem=send1.at[offset],
+            recv_sem=recv1.at[sender], device_id={"particle": sender}, device_id_type=MESH,
+        ).wait_recv()
+        pltpu.make_async_remote_copy(
+            src_ref=alt_ref, dst_ref=lines_ref.at[sender], send_sem=send3.at[offset],
+            recv_sem=recv3.at[sender], device_id={"particle": sender}, device_id_type=MESH,
+        ).wait_recv()
+
+    for member in range(count):
+        source = jnp.clip(anc_ref[member], 0, count - 1)
+        outgoing[member] = held[source]
+
+    r_me, c_me = window(me, grid_cols, rows, cols)
+    mine = pltpu.make_async_copy(outgoing.at[me], out_ref.at[:, r_me, c_me], local.at[2])
+    mine.start()
+    second = []
+    for offset in range(1, count):
+        peer = lax.rem(me + offset, count)
+        copy = pltpu.make_async_remote_copy(
+            src_ref=outgoing.at[peer], dst_ref=out_ref.at[:, r_me, c_me],
+            send_sem=send2.at[offset], recv_sem=recv2.at[me],
+            device_id={"particle": peer}, device_id_type=MESH,
+        )
+        copy.start()
+        second.append(copy)
+    mine.wait()
+    for offset, copy in zip(range(1, count), second):
+        sender = lax.rem(me + count - offset, count)
+        r_s, c_s = window(sender, grid_cols, rows, cols)
+        copy.wait_send()
+        pltpu.make_async_remote_copy(
+            src_ref=outgoing.at[me], dst_ref=out_ref.at[:, r_s, c_s],
+            send_sem=send2.at[offset], recv_sem=recv2.at[sender],
+            device_id={"particle": sender}, device_id_type=MESH,
+        ).wait_recv()
+
+
+def resample(tile, ancestors, altimetry):
+    count = lax.axis_size("particle")
+    fields, height, width = tile.shape
+    grid_rows = 4
+    grid_cols = count // grid_rows
+    rows, cols = height // grid_rows, width // grid_cols
+    sems = pltpu.SemaphoreType.DMA((count,))
+    return pl.pallas_call(
+        functools.partial(exchange_kernel, count, grid_cols),
+        out_shape=(
+            jax.ShapeDtypeStruct(tile.shape, tile.dtype),
+            jax.ShapeDtypeStruct((count,) + altimetry.shape, altimetry.dtype),
+        ),
+        in_specs=[
+            pl.BlockSpec(memory_space=pltpu.SMEM),
+            pl.BlockSpec(memory_space=pl.ANY),
+            pl.BlockSpec(memory_space=pltpu.VMEM),
+        ],
+        out_specs=(
+            pl.BlockSpec(memory_space=pl.ANY),
+            pl.BlockSpec(memory_space=pltpu.VMEM),
+        ),
+        scratch_shapes=[
+            pltpu.VMEM((count, fields, rows, cols), tile.dtype),
+            pltpu.VMEM((count, fields, rows, cols), tile.dtype),
+            sems, sems, sems, sems, sems, sems,
+            pltpu.SemaphoreType.DMA((3,)),
+        ],
+        compiler_params=pltpu.CompilerParams(collective_id=0, has_side_effects=True),
+    )(ancestors, tile, altimetry)
+
+
 def per_device(ensemble, ancestors, depth_levels, level_coefs, altimetry, obs_rows):
     levels = level_coefs.shape[1]
     width_y = ensemble.shape[3]
-    mine = ancestors[lax.axis_index("particle")]
-    piece = lax.all_gather(ensemble, "particle", axis=0, tiled=True)
-    count = piece.shape[0]
-    inside = (mine >= 0) & (mine < count)
-    chosen = lax.dynamic_index_in_dim(piece, jnp.clip(mine, 0, count - 1), 0, keepdims=False)
-    state = jnp.where(inside, chosen, jnp.zeros(ensemble.shape[1:], jnp.float32))
+    state, gathered = resample(ensemble[0], ancestors, altimetry)
+    all_lines = jnp.moveaxis(gathered, 0, 1).reshape(
+        (altimetry.shape[0], -1) + altimetry.shape[2:]
+    )
     level_ids = jnp.arange(levels, dtype=jnp.int32)
     masks = (level_ids[:, None, None] < depth_levels[None]).astype(jnp.float32)
     full_mask = jnp.concatenate([masks, masks, masks, masks[:1]], axis=0)
     state = state * full_mask
     columns = jnp.arange(width_y, dtype=jnp.int32)
     for step in range(STEPS):
-        lines = lax.all_gather(altimetry[step], "particle", axis=0, tiled=True)
+        lines = all_lines[step]
         onehot = (obs_rows[step][:, None] == columns[None, :]).astype(jnp.float32)
         target = jnp.dot(
             lines.T, onehot, precision=lax.Precision.HIGHEST, preferred_element_type=jnp.float32

time: 483 us -> 152 us (0.31)
  waiting for transfers between devices: 327 us -> 20.1 us
  blocking collectives: 117 us -> 0 us
  Pallas kernels: 0 us -> 94.7 us
  starting transfers between devices: 3.51 us -> 20.3 us
  between operations: 15.7 us -> 0.35 us
    all_gather x1 -> x0, waiting for transfers between devices: 312 us -> none  [per_device(): piece = lax.all_gather(ensemble, 'particle', axis=0, tiled=True)]
    all_gather x3 -> x0, blocking collectives: 117 us -> none  [per_device(): lines = lax.all_gather(altimetry[step], 'particle', axis=0, tiled=True)]
    pallas_call x0 -> x1, Pallas kernels: none -> 94.7 us  [resample(): pl.pallas_call(functools.partial(exchange_kernel, count, grid_cols), out_...]
    ppermute x6, starting transfers between devices: 0.5 us -> 19.4 us  [with_halo(): lax.ppermute(lax.slice_in_dim(block, 0, width, axis=dim), axis, backward)]
  transfers between devices with their start and end apart: 13 -> 12, of which waited for: 7 -> 9; matrix products, arithmetic and copies ran while one was open for 0% -> 0% of each run, Pallas kernels for 0% -> 0%
where the time goes in v1:
time: 152 us; the launch traced here: 151 us
  Pallas kernels  94.7 us (62%)
  starting transfers between devices  20.3 us (13%)
  waiting for transfers between devices  20.1 us (13%)
  other arithmetic  14.6 us (10%)
    pallas_call x1, Pallas kernels, resample(): pl.pallas_call(functools.partial(exchange_kernel, count, grid_cols), out_...  94.7 us
    ppermute x6, starting transfers between devices, with_halo(): lax.ppermute(lax.slice_in_dim(block, 0, width, axis=dim), axis, backward)  19.4 us
    ppermute x6, waiting for transfers between devices, with_halo(): lax.ppermute(lax.slice_in_dim(block, block.shape[dim] - width, None, axis...  15.1 us
    sub x3, other arithmetic, gradients(): laplace = east + west + padded[..., 2:] + padded[..., :-2] - 4.0 * center  5.93 us
    ppermute x6, waiting for transfers between devices, with_halo(): lax.ppermute(lax.slice_in_dim(block, 0, width, axis=dim), axis, backward)  5.08 us
  transfers between devices with their start and end apart: 12, of which 9 were waited for; matrix products, arithmetic and copies ran while one was open for 0% of the time, Pallas kernels for 0%

profile of v1, /device:TPU:24, one launch (start us, length us, event | category | flops | bytes accessed | tf_op | source)
XLA Modules:
  0.0 151.4 jit_solution(5484298823306661150)
XLA Ops:
  0.0 1.0 fusion.52
  1.0 94.7 %shard_map.64 = (f32[13,32,1024]{2,1,0:T(8,128)}, f32[16,3,4,32]{3,2,1,0:T(4,128)}) custom-call(s32[16]{0:T(128)} %anc_ref.1, f32[13,32,1024]{2,1,0:T(8,128)} %bitcast.66, f32[3,4,32]{2,1,0:T(4,128)} %alt_ref.1), custom_call_target="tpu_custom_call" | custom-call | tf_op jit(solution)/shard_map/pallas_call | solution.py:192
  95.7 1.7 %maximum_multiply_fusion = f32[13,32,1024]{2,1,0:T(8,128)S(1)} fusion(f32[13,32,1024]{2,1,0:T(8,128)} %get-tuple-element.7, f32[1,32,1024]{2,1,0:T(8,128)S(1)} %slice.314, f32[4,32,1024]{2,1,0:T(8,128)S(1)} %fusion.52), kind=kLoop, calls=%fused_computation.24 | loop fusion | flops 1703936 | bytes 4063232 | tf_op jit(solution)/shard_map/mul | solution.py:227
  97.4 0.1 fusion.78
  97.5 0.1 collective-permute-start
  97.6 0.5 collective-permute-start.1
  98.1 0.1 convert_reduce_fusion.2
  98.3 1.4 collective-permute-done
  99.6 3.7 %collective-permute-done.1 = f32[13,1,1024]{2,1,0:T(1,128)S(1)} collective-permute-done((f32[13,1,1024]{2,1,0:T(1,128)S(1)}, f32[13,1,1024]{2,1,0:T(1,128)S(1)}, u32[]{:S(2)}, u32[]{:S(2)}) %collective-permute-start.1) | collective-permute-done | bytes 53280 | tf_op jit(solution)/shard_map/ppermute | solution.py:27
  103.3 1.8 %multiply_subtract_fusion.2 = (f32[13,32,1024]{2,1,0:T(8,128)S(1)}, f32[13,32,1024]{2,1,0:T(8,128)S(1)}, f32[13,32,1024]{2,1,0:T(8,128)S(1)}) fusion(f32[13,32,1024]{2,1,0:T(8,128)S(1)} %maximum_multiply_fusion, f32[13,1,1024]{2,1,0:T(1,128)S(1)} %collective-permute-done, f32[13,1,1024]{2,1,0:T(1,128)S(1)} %collective-permute-done.1), kind=kLoop, calls=%fused_computation.34 | loop fusion | flops 4685824 | bytes 6922240 | tf_op jit(solution)/shard_map/sub | solution.py:46
  105.1 0.2 fusion.10
  105.3 0.3 fusion.9
  105.6 0.1 collective-permute-start.3
  105.7 3.8 %collective-permute-start.2 = (f32[1,1,1024]{2,1,0:T(1,128)S(1)}, f32[1,1,1024]{2,1,0:T(1,128)S(1)}, u32[]{:S(2)}, u32[]{:S(2)}) collective-permute-start(f32[1,1,1024]{2,1,0:T(1,128)S(1)} %get-tuple-element.43), channel_id=1, source_target_pairs={{1,0},{2,1},{3,2},{4,3},{5,4},{6,5},{7,6},{8,7},{9,8},{10,9},{11,1... | collective-permute-start | bytes 12296 | tf_op jit(solution)/shard_map/ppermute | solution.py:30
  109.6 0.1 convert_reduce_fusion.1
  109.7 1.2 collective-permute-done.3
  110.9 0.1 fusion.70
  111.0 0.6 fusion.51
  111.7 0.2 pad_maximum_fusion.18
  111.9 0.1 fusion.77
  111.9 3.9 %collective-permute-start.4 = (f32[13,1,1024]{2,1,0:T(1,128)S(1)}, f32[13,1,1024]{2,1,0:T(1,128)S(1)}, u32[]{:S(2)}, u32[]{:S(2)}) collective-permute-start(f32[13,1,1024]{2,1,0:T(1,128)S(1)} %get-tuple-element.29), channel_id=1, source_target_pairs={{1,0},{2,1},{3,2},{4,3},{5,4},{6,5},{7,6},{8,7},{9,8},{10,9},{11,1... | collective-permute-start | bytes 159752 | tf_op jit(solution)/shard_map/ppermute | solution.py:30
  115.8 1.8 %collective-permute-done.4 = f32[13,1,1024]{2,1,0:T(1,128)S(1)} collective-permute-done((f32[13,1,1024]{2,1,0:T(1,128)S(1)}, f32[13,1,1024]{2,1,0:T(1,128)S(1)}, u32[]{:S(2)}, u32[]{:S(2)}) %collective-permute-start.4) | collective-permute-done | bytes 53280 | tf_op jit(solution)/shard_map/ppermute | solution.py:30
  117.6 3.9 %collective-permute-done.5 = f32[13,1,1024]{2,1,0:T(1,128)S(1)} collective-permute-done((f32[13,1,1024]{2,1,0:T(1,128)S(1)}, f32[13,1,1024]{2,1,0:T(1,128)S(1)}, u32[]{:S(2)}, u32[]{:S(2)}) %collective-permute-start.5) | collective-permute-done | bytes 53280 | tf_op jit(solution)/shard_map/ppermute | solution.py:27
  121.5 2.1 %multiply_subtract_fusion.1 = (f32[13,32,1024]{2,1,0:T(8,128)S(1)}, f32[13,32,1024]{2,1,0:T(8,128)S(1)}) fusion(f32[13,32,1024]{2,1,0:T(8,128)S(1)} %pad_maximum_fusion.18, f32[13,1,1024]{2,1,0:T(1,128)S(1)} %collective-permute-done.4, f32[1,32,1024]{2,1,0:T(8,128)S(1)} %bitcast.64, f32[4,32,1024]{2,1,0:T(8,128)S(1)} %get-tuple-element.15, ...), kind=kLoop, calls=%fused_computation.31 | loop fusion | flops 6389760 | bytes 6922240 | tf_op jit(solution)/shard_map/sub | solution.py:46
  123.6 0.5 subtract_multiply_fusion.3
  124.0 0.5 fusion.29
  124.6 0.3 fusion.6
  124.9 0.3 collective-permute-start.7
  125.2 3.8 %collective-permute-start.6 = (f32[1,1,1024]{2,1,0:T(1,128)S(1)}, f32[1,1,1024]{2,1,0:T(1,128)S(1)}, u32[]{:S(2)}, u32[]{:S(2)}) collective-permute-start(f32[1,1,1024]{2,1,0:T(1,128)S(1)} %get-tuple-element.39), channel_id=1, source_target_pairs={{1,0},{2,1},{3,2},{4,3},{5,4},{6,5},{7,6},{8,7},{9,8},{10,9},{11,1... | collective-permute-start | bytes 12296 | tf_op jit(solution)/shard_map/ppermute | solution.py:30
  129.0 0.1 convert_reduce_fusion
  129.1 1.2 collective-permute-done.7
  130.3 0.1 fusion.67
  130.5 0.4 fusion.38
  130.9 0.2 pad_maximum_fusion.19
  131.1 0.1 fusion.76
  131.2 3.9 %collective-permute-start.8 = (f32[13,1,1024]{2,1,0:T(1,128)S(1)}, f32[13,1,1024]{2,1,0:T(1,128)S(1)}, u32[]{:S(2)}, u32[]{:S(2)}) collective-permute-start(f32[13,1,1024]{2,1,0:T(1,128)S(1)} %get-tuple-element.25), channel_id=1, source_target_pairs={{1,0},{2,1},{3,2},{4,3},{5,4},{6,5},{7,6},{8,7},{9,8},{10,9},{11,1... | collective-permute-start | bytes 159752 | tf_op jit(solution)/shard_map/ppermute | solution.py:30
  135.1 1.8 %collective-permute-done.8 = f32[13,1,1024]{2,1,0:T(1,128)S(1)} collective-permute-done((f32[13,1,1024]{2,1,0:T(1,128)S(1)}, f32[13,1,1024]{2,1,0:T(1,128)S(1)}, u32[]{:S(2)}, u32[]{:S(2)}) %collective-permute-start.8) | collective-permute-done | bytes 53280 | tf_op jit(solution)/shard_map/ppermute | solution.py:30
  136.9 3.9 %collective-permute-done.9 = f32[13,1,1024]{2,1,0:T(1,128)S(1)} collective-permute-done((f32[13,1,1024]{2,1,0:T(1,128)S(1)}, f32[13,1,1024]{2,1,0:T(1,128)S(1)}, u32[]{:S(2)}, u32[]{:S(2)}) %collective-permute-start.9) | collective-permute-done | bytes 53280 | tf_op jit(solution)/shard_map/ppermute | solution.py:27
  140.7 2.1 %multiply_subtract_fusion = (f32[13,32,1024]{2,1,0:T(8,128)S(1)}, f32[13,32,1024]{2,1,0:T(8,128)S(1)}) fusion(f32[13,32,1024]{2,1,0:T(8,128)S(1)} %pad_maximum_fusion.19, f32[13,1,1024]{2,1,0:T(1,128)S(1)} %collective-permute-done.8, f32[1,32,1024]{2,1,0:T(8,128)S(1)} %bitcast.59, f32[4,32,1024]{2,1,0:T(8,128)S(1)} %get-tuple-element.13, ...), kind=kLoop, calls=%fused_computation.28 | loop fusion | flops 6389760 | bytes 6922240 | tf_op jit(solution)/shard_map/sub | solution.py:46
  142.8 0.5 subtract_multiply_fusion.1
  143.3 0.5 fusion.16
  143.8 0.3 fusion.3
  144.1 0.1 collective-permute-start.11
  144.2 3.8 %collective-permute-start.10 = (f32[1,1,1024]{2,1,0:T(1,128)S(1)}, f32[1,1,1024]{2,1,0:T(1,128)S(1)}, u32[]{:S(2)}, u32[]{:S(2)}) collective-permute-start(f32[1,1,1024]{2,1,0:T(1,128)S(1)} %get-tuple-element.35), channel_id=1, source_target_pairs={{1,0},{2,1},{3,2},{4,3},{5,4},{6,5},{7,6},{8,7},{9,8},{10,9},{11,1... | collective-permute-start | bytes 12296 | tf_op jit(solution)/shard_map/ppermute | solution.py:30
  148.1 1.3 collective-permute-done.11
  149.4 0.1 fusion.64
  149.5 0.4 fusion.25
  150.0 1.4 maximum_bitcast_fusion
  (23 shorter events, 0.2 us)
Async XLA Ops:
  95.7 2.4 %copy-start.1 = (f32[16,3,4,32]{3,2,1,0:T(4,128)S(1)}, f32[16,3,4,32]{3,2,1,0:T(4,128)}, u32[]{:S(2)}) copy-start(f32[16,3,4,32]{3,2,1,0:T(4,128)} %get-tuple-element.8) | copy-start | bytes 73732
  95.7 2.4 %copy-start.2 = (s32[3,64]{1,0:T(4,128)S(1)}, s32[3,64]{1,0:T(4,128)}, u32[]{:S(2)}) copy-start(s32[3,64]{1,0:T(4,128)} %param.11) | copy-start | bytes 2308
  95.7 2.5 %copy-start.3 = (f32[3,4]{1,0:T(4,128)S(1)}, f32[3,4]{1,0:T(4,128)}, u32[]{:S(2)}) copy-start(f32[3,4]{1,0:T(4,128)} %param.9) | copy-start | bytes 148
  97.5 2.2 %collective-permute-start = (f32[13,1,1024]{2,1,0:T(1,128)S(1)}, f32[13,1,1024]{2,1,0:T(1,128)S(1)}, u32[]{:S(2)}, u32[]{:S(2)}) collective-permute-start(f32[13,1,1024]{2,1,0:T(1,128)S(1)} %get-tuple-element.32), channel_id=1, source_target_pairs={{1,0},{2,1},{3,2},{4,3},{5,4},{6,5},{7,6},{8,7},{9,8},{10,9},{11,1... | collective-permute-start | bytes 159752 | tf_op jit(solution)/shard_map/ppermute | solution.py:30
  97.6 5.7 %collective-permute-start.1 = (f32[13,1,1024]{2,1,0:T(1,128)S(1)}, f32[13,1,1024]{2,1,0:T(1,128)S(1)}, u32[]{:S(2)}, u32[]{:S(2)}) collective-permute-start(f32[13,1,1024]{2,1,0:T(1,128)S(1)} %get-tuple-element.31), channel_id=1, source_target_pairs={{0,1},{1,2},{2,3},{3,4},{4,5},{5,6},{6,7},{7,8},{8,9},{9,10},{10,1... | collective-permute-start | bytes 159752 | tf_op jit(solution)/shard_map/ppermute | solution.py:27
  98.2 6.9 %copy-start = (s32[32,1024]{1,0:T(8,128)S(1)}, s32[32,1024]{1,0:T(8,128)}, u32[]{:S(2)}) copy-start(s32[32,1024]{1,0:T(8,128)} %param.8) | copy-start | bytes 393220
  105.6 5.2 %collective-permute-start.3 = (f32[1,1,1024]{2,1,0:T(1,128)S(1)}, f32[1,1,1024]{2,1,0:T(1,128)S(1)}, u32[]{:S(2)}, u32[]{:S(2)}) collective-permute-start(f32[1,1,1024]{2,1,0:T(1,128)S(1)} %get-tuple-element.44), channel_id=1, source_target_pairs={{0,1},{1,2},{2,3},{3,4},{4,5},{5,6},{6,7},{7,8},{8,9},{9,10},{10,1... | collective-permute-start | bytes 12296 | tf_op jit(solution)/shard_map/ppermute | solution.py:27
  105.7 5.2 %collective-permute-start.2 = (f32[1,1,1024]{2,1,0:T(1,128)S(1)}, f32[1,1,1024]{2,1,0:T(1,128)S(1)}, u32[]{:S(2)}, u32[]{:S(2)}) collective-permute-start(f32[1,1,1024]{2,1,0:T(1,128)S(1)} %get-tuple-element.43), channel_id=1, source_target_pairs={{1,0},{2,1},{3,2},{4,3},{5,4},{6,5},{7,6},{8,7},{9,8},{10,9},{11,1... | collective-permute-start | bytes 12296 | tf_op jit(solution)/shard_map/ppermute | solution.py:30
  111.9 5.7 %collective-permute-start.4 = (f32[13,1,1024]{2,1,0:T(1,128)S(1)}, f32[13,1,1024]{2,1,0:T(1,128)S(1)}, u32[]{:S(2)}, u32[]{:S(2)}) collective-permute-start(f32[13,1,1024]{2,1,0:T(1,128)S(1)} %get-tuple-element.29), channel_id=1, source_target_pairs={{1,0},{2,1},{3,2},{4,3},{5,4},{6,5},{7,6},{8,7},{9,8},{10,9},{11,1... | collective-permute-start | bytes 159752 | tf_op jit(solution)/shard_map/ppermute | solution.py:30
  115.8 5.7 %collective-permute-start.5 = (f32[13,1,1024]{2,1,0:T(1,128)S(1)}, f32[13,1,1024]{2,1,0:T(1,128)S(1)}, u32[]{:S(2)}, u32[]{:S(2)}) collective-permute-start(f32[13,1,1024]{2,1,0:T(1,128)S(1)} %get-tuple-element.28), channel_id=1, source_target_pairs={{0,1},{1,2},{2,3},{3,4},{4,5},{5,6},{6,7},{7,8},{8,9},{9,10},{10,1... | collective-permute-start | bytes 159752 | tf_op jit(solution)/shard_map/ppermute | solution.py:27
  124.9 5.4 %collective-permute-start.7 = (f32[1,1,1024]{2,1,0:T(1,128)S(1)}, f32[1,1,1024]{2,1,0:T(1,128)S(1)}, u32[]{:S(2)}, u32[]{:S(2)}) collective-permute-start(f32[1,1,1024]{2,1,0:T(1,128)S(1)} %get-tuple-element.40), channel_id=1, source_target_pairs={{0,1},{1,2},{2,3},{3,4},{4,5},{5,6},{6,7},{7,8},{8,9},{9,10},{10,1... | collective-permute-start | bytes 12296 | tf_op jit(solution)/shard_map/ppermute | solution.py:27
  125.2 5.2 %collective-permute-start.6 = (f32[1,1,1024]{2,1,0:T(1,128)S(1)}, f32[1,1,1024]{2,1,0:T(1,128)S(1)}, u32[]{:S(2)}, u32[]{:S(2)}) collective-permute-start(f32[1,1,1024]{2,1,0:T(1,128)S(1)} %get-tuple-element.39), channel_id=1, source_target_pairs={{1,0},{2,1},{3,2},{4,3},{5,4},{6,5},{7,6},{8,7},{9,8},{10,9},{11,1... | collective-permute-start | bytes 12296 | tf_op jit(solution)/shard_map/ppermute | solution.py:30
  131.2 5.7 %collective-permute-start.8 = (f32[13,1,1024]{2,1,0:T(1,128)S(1)}, f32[13,1,1024]{2,1,0:T(1,128)S(1)}, u32[]{:S(2)}, u32[]{:S(2)}) collective-permute-start(f32[13,1,1024]{2,1,0:T(1,128)S(1)} %get-tuple-element.25), channel_id=1, source_target_pairs={{1,0},{2,1},{3,2},{4,3},{5,4},{6,5},{7,6},{8,7},{9,8},{10,9},{11,1... | collective-permute-start | bytes 159752 | tf_op jit(solution)/shard_map/ppermute | solution.py:30
  135.1 5.7 %collective-permute-start.9 = (f32[13,1,1024]{2,1,0:T(1,128)S(1)}, f32[13,1,1024]{2,1,0:T(1,128)S(1)}, u32[]{:S(2)}, u32[]{:S(2)}) collective-permute-start(f32[13,1,1024]{2,1,0:T(1,128)S(1)} %get-tuple-element.24), channel_id=1, source_target_pairs={{0,1},{1,2},{2,3},{3,4},{4,5},{5,6},{6,7},{7,8},{8,9},{9,10},{10,1... | collective-permute-start | bytes 159752 | tf_op jit(solution)/shard_map/ppermute | solution.py:27
  144.1 5.2 %collective-permute-start.11 = (f32[1,1,1024]{2,1,0:T(1,128)S(1)}, f32[1,1,1024]{2,1,0:T(1,128)S(1)}, u32[]{:S(2)}, u32[]{:S(2)}) collective-permute-start(f32[1,1,1024]{2,1,0:T(1,128)S(1)} %get-tuple-element.36), channel_id=1, source_target_pairs={{0,1},{1,2},{2,3},{3,4},{4,5},{5,6},{6,7},{7,8},{8,9},{9,10},{10,1... | collective-permute-start | bytes 12296 | tf_op jit(solution)/shard_map/ppermute | solution.py:27
  144.2 5.2 %collective-permute-start.10 = (f32[1,1,1024]{2,1,0:T(1,128)S(1)}, f32[1,1,1024]{2,1,0:T(1,128)S(1)}, u32[]{:S(2)}, u32[]{:S(2)}) collective-permute-start(f32[1,1,1024]{2,1,0:T(1,128)S(1)} %get-tuple-element.35), channel_id=1, source_target_pairs={{1,0},{2,1},{3,2},{4,3},{5,4},{6,5},{7,6},{8,7},{9,8},{10,9},{11,1... | collective-permute-start | bytes 12296 | tf_op jit(solution)/shard_map/ppermute | solution.py:30

commit v2 on v1

--- a/solution.py
+++ b/solution.py
@@ -214,26 +214,49 @@
     )(ancestors, tile, altimetry)
 
 
+def wide_step(state, masks, coefs, target, hit):
+    levels = masks.shape[0]
+    center, ddx, ddy, laplace = gradients(state)
+    height = center[3 * levels]
+    thick, visc, kappa = level_terms(coefs)
+    spread = ddx[:levels] + ddy[levels : 2 * levels]
+    surface = masks[0]
+    height_one = surface * (height - DT * jnp.sum(thick * masks * spread, axis=0))
+    height_two = surface * (height_one + NUDGE * hit * (target - height_one))
+    unused, grad_x, grad_y, unused_lap = gradients(height_two[None])
+    inner = lambda field: field[:, 1:-1]
+    return finish(
+        inner(center), inner(ddx), inner(ddy), inner(laplace), inner(masks),
+        visc, kappa, grad_x, grad_y, height_two[1:-1],
+    )
+
+
 def per_device(ensemble, ancestors, depth_levels, level_coefs, altimetry, obs_rows):
     levels = level_coefs.shape[1]
     width_y = ensemble.shape[3]
+    reach = 2 * STEPS
     state, gathered = resample(ensemble[0], ancestors, altimetry)
     all_lines = jnp.moveaxis(gathered, 0, 1).reshape(
         (altimetry.shape[0], -1) + altimetry.shape[2:]
     )
+    state = with_halo(state, (("space", 1),), reach)
+    depth = with_halo(depth_levels, (("space", 0),), reach)
+    all_lines = with_halo(all_lines, (("space", 2),), reach)
+    span = depth.shape[0]
     level_ids = jnp.arange(levels, dtype=jnp.int32)
-    masks = (level_ids[:, None, None] < depth_levels[None]).astype(jnp.float32)
+    masks = (level_ids[:, None, None] < depth[None]).astype(jnp.float32)
     full_mask = jnp.concatenate([masks, masks, masks, masks[:1]], axis=0)
     state = state * full_mask
     columns = jnp.arange(width_y, dtype=jnp.int32)
     for step in range(STEPS):
-        lines = all_lines[step]
+        low, high = 2 * step + 1, span - 2 * step - 1
+        lines = all_lines[step][:, low:high]
         onehot = (obs_rows[step][:, None] == columns[None, :]).astype(jnp.float32)
         target = jnp.dot(
             lines.T, onehot, precision=lax.Precision.HIGHEST, preferred_element_type=jnp.float32
         )
         hit = jnp.sum(onehot, axis=0)[None, :]
-        state = one_step(state, masks, level_coefs, target, hit)
+        state = wide_step(state, masks[:, low:high], level_coefs, target, hit)
     return state[None]
 
 

time: 152 us -> 157 us (1.033)
  the two profiles are of different devices: /device:TPU:24 before, /device:TPU:19 now
where the time goes in v2:
time: 157 us
  Pallas kernels  75.9 us (48%)
  starting transfers between devices  38.8 us (25%)
  other arithmetic  18.5 us (12%)
  waiting for transfers between devices  15.1 us (10%)
  local copies, waits for them, and re-layouts  6.93 us (4%)
    pallas_call x1, Pallas kernels, resample(): pl.pallas_call(functools.partial(exchange_kernel, count, grid_cols), out_...  75.9 us
    ppermute x3, starting transfers between devices, with_halo(): lax.ppermute(lax.slice_in_dim(block, block.shape[dim] - width, None, axis...  38.3 us
    sub x3, other arithmetic, gradients(): laplace = east + west + padded[..., 2:] + padded[..., :-2] - 4.0 * center  9.07 us
    ppermute x3, waiting for transfers between devices, with_halo(): lax.ppermute(lax.slice_in_dim(block, block.shape[dim] - width, None, axis...  7.74 us
    ppermute x3, waiting for transfers between devices, with_halo(): lax.ppermute(lax.slice_in_dim(block, 0, width, axis=dim), axis, backward)  7.37 us
    mul x3, other arithmetic, finish(): masks * (east_vel + DT * (CORIOLIS * north_vel - GRAVITY * grad_x + visc...  4.08 us
  transfers between devices with their start and end apart: 6, of which 2 were waited for; matrix products, arithmetic and copies ran while one was open for 2% of the time, Pallas kernels for 48%

profile of v2, /device:TPU:19, one launch (start us, length us, event | category | flops | bytes accessed | tf_op | source)
XLA Modules:
  0.0 156.7 jit_solution(12066895738121757243)
XLA Ops:
  0.0 0.8 fusion.83
  0.8 2.2 %collective-permute-start = (s32[6,1024]{1,0:T(8,128)S(1)}, s32[6,1024]{1,0:T(8,128)S(1)}, u32[]{:S(2)}, u32[]{:S(2)}) collective-permute-start(s32[6,1024]{1,0:T(8,128)S(1)} %get-tuple-element.35), channel_id=1, source_target_pairs={{0,1},{1,2},{2,3},{3,4},{4,5},{5,6},{6,7},{7,8},{8,9},{9,10},{10,1... | collective-permute-start | bytes 73736 | tf_op jit(solution)/shard_map/ppermute | solution.py:27
  3.0 75.9 %shard_map.64 = (f32[13,32,1024]{2,1,0:T(8,128)}, f32[16,3,4,32]{3,2,1,0:T(4,128)}) custom-call(s32[16]{0:T(128)} %anc_ref.1, f32[13,32,1024]{2,1,0:T(8,128)} %bitcast.83, f32[3,4,32]{2,1,0:T(4,128)} %alt_ref.1), custom_call_target="tpu_custom_call" | custom-call | tf_op jit(solution)/shard_map/pallas_call | solution.py:192
  78.9 1.3 fusion.82
  80.3 36.0 %collective-permute-start.2 = (f32[13,6,1024]{2,1,0:T(8,128)S(1)}, f32[13,6,1024]{2,1,0:T(8,128)S(1)}, u32[]{:S(2)}, u32[]{:S(2)}) collective-permute-start(f32[13,6,1024]{2,1,0:T(8,128)S(1)} %get-tuple-element.27), channel_id=1, source_target_pairs={{0,1},{1,2},{2,3},{3,4},{4,5},{5,6},{6,7},{7,8},{8,9},{9,10},{10,1... | collective-permute-start | bytes 958472 | tf_op jit(solution)/shard_map/ppermute | solution.py:27
  116.2 0.9 copy.8
  117.1 0.1 fusion.84
  117.2 0.1 collective-permute-start.4
  117.3 0.5 collective-permute-start.5
  117.8 0.1 convert_reduce_fusion.1
  118.0 0.1 convert_reduce_fusion
  118.1 7.7 %collective-permute-done.4 = f32[3,64,6]{2,1,0:T(8,128)S(1)} collective-permute-done((f32[3,64,6]{2,1,0:T(8,128)S(1)}, f32[3,64,6]{2,1,0:T(8,128)S(1)}, u32[]{:S(2)}, u32[]{:S(2)}) %collective-permute-start.4) | collective-permute-done | bytes 4640 | tf_op jit(solution)/shard_map/ppermute | solution.py:27
  125.9 0.0 collective-permute-start.3
  125.9 0.0 collective-permute-done.5
  125.9 0.1 pad_maximum_fusion.2
  126.0 0.6 slice_bitcast_fusion.8
  126.6 0.0 collective-permute-done
  126.7 0.1 fusion.11
  126.8 7.4 %collective-permute-done.3 = f32[13,6,1024]{2,1,0:T(8,128)S(1)} collective-permute-done((f32[13,6,1024]{2,1,0:T(8,128)S(1)}, f32[13,6,1024]{2,1,0:T(8,128)S(1)}, u32[]{:S(2)}, u32[]{:S(2)}) %collective-permute-start.3) | collective-permute-done | bytes 319520 | tf_op jit(solution)/shard_map/ppermute | solution.py:30
  134.2 0.6 maximum_multiply_fusion
  134.8 0.5 slice.455
  135.3 3.2 %multiply_subtract_fusion = (f32[13,42,1024]{2,1,0:T(8,128)S(1)}, f32[13,42,1024]{2,1,0:T(8,128)S(1)}, f32[13,42,1024]{2,1,0:T(8,128)S(1)}) fusion(f32[13,42,1024]{2,1,0:T(8,128)S(1)} %slice.455, f32[13,44,1024]{2,1,0:T(8,128)S(1)} %maximum_multiply_fusion), kind=kLoop, calls=%fused_computation.3 | loop fusion | flops 5031936 | bytes 13418496 | tf_op jit(solution)/shard_map/sub | solution.py:46
  138.5 0.3 fusion.10
  138.8 0.4 fusion.2
  139.3 0.1 fusion.59
  139.4 1.0 fusion.41
  140.5 0.2 pad_maximum_fusion
  140.7 0.4 slice.479
  141.2 3.6 %multiply_subtract_fusion.2 = (f32[13,38,1024]{2,1,0:T(8,128)S(1)}, f32[13,38,1024]{2,1,0:T(8,128)S(1)}, f32[13,38,1024]{2,1,0:T(8,128)}) fusion(f32[13,38,1024]{2,1,0:T(8,128)S(1)} %slice.479, f32[13,40,1024]{2,1,0:T(8,128)S(1)} %pad_maximum_fusion), kind=kLoop, calls=%fused_computation.15 | loop fusion | flops 4552704 | bytes 12140544 | tf_op jit(solution)/shard_map/sub | solution.py:46
  144.8 1.4 fusion.28
  146.2 0.4 fusion.8
  146.6 0.1 fusion.62
  146.8 2.1 %fusion.26 = (f32[4,36,1024]{2,1,0:T(8,128)S(1)}, f32[4,36,1024]{2,1,0:T(8,128)S(1)}, f32[4,36,1024]{2,1,0:T(8,128)S(1)}) fusion(f32[13,38,1024]{2,1,0:T(8,128)S(1)} %get-tuple-element.24, f32[4,40,1024]{2,1,0:T(8,128)S(1)} %get-tuple-element.10, f32[4,40,1024]{2,1,0:T(8,128)S(1)} %get-tuple-element.9, f32[4,44,1024]{2,1,0:T(8,128)S(1)} %fusion.11, ...), kind=kLoop, calls=%fused_computation.58 | loop fusion | flops 3244032 | bytes 7372832 | tf_op jit(solution)/shard_map/mul | solution.py:70
  148.9 0.0 copy-start.3
  148.9 0.2 pad_maximum_fusion.1
  149.2 0.6 copy-done.1
  149.8 0.2 copy-done.3
  149.9 0.2 copy-done.5
  150.2 0.4 slice.501
  150.6 2.3 %multiply_subtract_fusion.1 = (f32[13,34,1024]{2,1,0:T(8,128)S(1)}, f32[13,34,1024]{2,1,0:T(8,128)S(1)}, f32[13,34,1024]{2,1,0:T(8,128)S(1)}) fusion(f32[13,34,1024]{2,1,0:T(8,128)S(1)} %slice.501, f32[13,36,1024]{2,1,0:T(8,128)S(1)} %pad_maximum_fusion.1), kind=kLoop, calls=%fused_computation.12 | loop fusion | flops 4073472 | bytes 10862592 | tf_op jit(solution)/shard_map/sub | solution.py:46
  152.9 0.0 copy-start.4
  152.9 0.2 fusion.13
  153.2 0.6 copy-done.8
  153.8 0.4 fusion.5
  154.2 0.1 fusion.73
  154.4 0.1 copy-done.6
  154.5 1.0 fusion.54
  155.4 1.3 maximum_bitcast_fusion
  (43 shorter events, 0.3 us)
Async XLA Ops:
  0.0 117.8 %copy-start.15 = (s32[3,64]{1,0:T(4,128)S(1)}, s32[3,64]{1,0:T(4,128)}, u32[]{:S(2)}) copy-start(s32[3,64]{1,0:T(4,128)} %param.11) | copy-start | bytes 2308
  0.0 118.1 %copy-start.16 = (f32[3,4]{1,0:T(4,128)S(1)}, f32[3,4]{1,0:T(4,128)}, u32[]{:S(2)}) copy-start(f32[3,4]{1,0:T(4,128)} %param.9) | copy-start | bytes 148
  0.8 125.8 %collective-permute-start = (s32[6,1024]{1,0:T(8,128)S(1)}, s32[6,1024]{1,0:T(8,128)S(1)}, u32[]{:S(2)}, u32[]{:S(2)}) collective-permute-start(s32[6,1024]{1,0:T(8,128)S(1)} %get-tuple-element.35), channel_id=1, source_target_pairs={{0,1},{1,2},{2,3},{3,4},{4,5},{5,6},{6,7},{7,8},{8,9},{9,10},{10,1... | collective-permute-start | bytes 73736 | tf_op jit(solution)/shard_map/ppermute | solution.py:27
  3.0 123.6 %collective-permute-start.1 = (s32[6,1024]{1,0:T(8,128)S(1)}, s32[6,1024]{1,0:T(8,128)S(1)}, u32[]{:S(2)}, u32[]{:S(2)}) collective-permute-start(s32[6,1024]{1,0:T(8,128)S(1)} %get-tuple-element.36), channel_id=1, source_target_pairs={{1,0},{2,1},{3,2},{4,3},{5,4},{6,5},{7,6},{8,7},{9,8},{10,9},{11,1... | collective-permute-start | bytes 73736 | tf_op jit(solution)/shard_map/ppermute | solution.py:30
  3.0 123.6 %copy-start.9 = (s32[32,1024]{1,0:T(8,128)S(1)}, s32[32,1024]{1,0:T(8,128)}, u32[]{:S(2)}) copy-start(s32[32,1024]{1,0:T(8,128)} %param.8) | copy-start | bytes 393220
  78.9 55.3 %copy-start = (f32[13,32,1024]{2,1,0:T(8,128)S(1)}, f32[13,32,1024]{2,1,0:T(8,128)}, u32[]{:S(2)}) copy-start(f32[13,32,1024]{2,1,0:T(8,128)} %get-tuple-element.7) | copy-start | bytes 5111812
  80.3 46.5 %collective-permute-start.2 = (f32[13,6,1024]{2,1,0:T(8,128)S(1)}, f32[13,6,1024]{2,1,0:T(8,128)S(1)}, u32[]{:S(2)}, u32[]{:S(2)}) collective-permute-start(f32[13,6,1024]{2,1,0:T(8,128)S(1)} %get-tuple-element.27), channel_id=1, source_target_pairs={{0,1},{1,2},{2,3},{3,4},{4,5},{5,6},{6,7},{7,8},{8,9},{9,10},{10,1... | collective-permute-start | bytes 958472 | tf_op jit(solution)/shard_map/ppermute | solution.py:27
  117.2 8.6 %collective-permute-start.4 = (f32[3,64,6]{2,1,0:T(8,128)S(1)}, f32[3,64,6]{2,1,0:T(8,128)S(1)}, u32[]{:S(2)}, u32[]{:S(2)}) collective-permute-start(f32[3,64,6]{2,1,0:T(8,128)S(1)} %get-tuple-element.40), channel_id=1, source_target_pairs={{0,1},{1,2},{2,3},{3,4},{4,5},{5,6},{6,7},{7,8},{8,9},{9,10},{10,1... | collective-permute-start | bytes 13832 | tf_op jit(solution)/shard_map/ppermute | solution.py:27
  117.3 8.6 %collective-permute-start.5 = (f32[3,64,6]{2,1,0:T(8,128)S(1)}, f32[3,64,6]{2,1,0:T(8,128)S(1)}, u32[]{:S(2)}, u32[]{:S(2)}) collective-permute-start(f32[3,64,6]{2,1,0:T(8,128)S(1)} %get-tuple-element.41), channel_id=1, source_target_pairs={{1,0},{2,1},{3,2},{4,3},{5,4},{6,5},{7,6},{8,7},{9,8},{10,9},{11,1... | collective-permute-start | bytes 13832 | tf_op jit(solution)/shard_map/ppermute | solution.py:30
  117.8 8.1 %copy-start.11 = (s32[64]{0:T(128)}, s32[64]{0:T(128)S(1)}, u32[]{:S(2)}) copy-start(s32[64]{0:T(128)S(1)} %get-tuple-element.42) | copy-start | bytes 772
  117.8 8.1 %copy-start.13 = (s32[64]{0:T(128)}, s32[64]{0:T(128)S(1)}, u32[]{:S(2)}) copy-start(s32[64]{0:T(128)S(1)} %get-tuple-element.44) | copy-start | bytes 772
  125.9 8.3 %collective-permute-start.3 = (f32[13,6,1024]{2,1,0:T(8,128)S(1)}, f32[13,6,1024]{2,1,0:T(8,128)S(1)}, u32[]{:S(2)}, u32[]{:S(2)}) collective-permute-start(f32[13,6,1024]{2,1,0:T(8,128)S(1)} %get-tuple-element.28), channel_id=1, source_target_pairs={{1,0},{2,1},{3,2},{4,3},{5,4},{6,5},{7,6},{8,7},{9,8},{10,9},{11,1... | collective-permute-start | bytes 958472 | tf_op jit(solution)/shard_map/ppermute | solution.py:30
  144.8 1.4 copy-start.10
  144.8 1.4 copy-start.14
  146.6 2.3 %copy-start.7 = (f32[1,36,1024]{2,1,0:T(8,128)}, f32[1,36,1024]{2,1,0:T(8,128)S(1)}, u32[]{:S(2)}) copy-start(f32[1,36,1024]{2,1,0:T(8,128)S(1)} %slice_bitcast_fusion.2) | copy-start | bytes 442372
  148.9 0.9 copy-start.1
  148.9 1.0 copy-start.3
  148.9 1.3 copy-start.5
  152.9 0.9 copy-start.8
  152.9 0.9 copy-start.12
  152.9 1.5 copy-start.2
  152.9 1.5 copy-start.4
  152.9 1.5 copy-start.6

commit v3 on v2

--- a/solution.py
+++ b/solution.py
@@ -104,17 +104,28 @@
 
 
 def exchange_kernel(
-    count, grid_cols, anc_ref, ens_ref, alt_ref, out_ref, lines_ref,
-    held, outgoing, send1, recv1, send2, recv2, send3, recv3, local,
+    count, grid_rows, grid_cols, anc_ref, ens_ref, alt_ref, out_ref, top_ref, bottom_ref, lines_ref,
+    held, outgoing, send1, recv1, send2, recv2, send3, recv3, send4, top_sem, bottom_sem, local,
 ):
     me = lax.axis_index("particle")
+    space = lax.axis_index("space")
+    spaces = lax.axis_size("space")
+    above = lax.rem(space + spaces - 1, spaces)
+    below = lax.rem(space + 1, spaces)
     rows, cols = held.shape[2], held.shape[3]
+    block_row = me // grid_cols
+    block_col = me % grid_cols
 
     barrier = pltpu.get_barrier_semaphore()
     for offset in range(1, count):
         peer = lax.rem(me + offset, count)
         pl.semaphore_signal(barrier, inc=1, device_id={"particle": peer}, device_id_type=MESH)
-    pl.semaphore_wait(barrier, count - 1)
+    for peer in range(count):
+        for side in (above, below):
+            pl.semaphore_signal(
+                barrier, inc=1, device_id={"particle": peer, "space": side}, device_id_type=MESH
+            )
+    pl.semaphore_wait(barrier, 3 * count - 1)
 
     def chunk_of(dest):
         r, c = window(dest, grid_cols, rows, cols)
@@ -158,6 +169,31 @@
         outgoing[member] = held[source]
 
     r_me, c_me = window(me, grid_cols, rows, cols)
+    edge = lambda ref, col: ref.at[:, :, pl.ds(col * cols, cols)]
+
+    def halo_copy(peer, side, target, sem):
+        return pltpu.make_async_remote_copy(
+            src_ref=outgoing.at[peer], dst_ref=edge(target, block_col),
+            send_sem=send4.at[peer], recv_sem=sem.at[block_col],
+            device_id={"particle": peer, "space": side}, device_id_type=MESH,
+        )
+
+    def send_halo(side, target, sem):
+        copies = [halo_copy(peer, side, target, sem) for peer in range(count)]
+        for copy in copies:
+            copy.start()
+        return copies
+
+    @pl.when(block_row == 0)
+    def _():
+        for copy in send_halo(above, bottom_ref, bottom_sem):
+            copy.wait_send()
+
+    @pl.when(block_row == grid_rows - 1)
+    def _():
+        for copy in send_halo(below, top_ref, top_sem):
+            copy.wait_send()
+
     mine = pltpu.make_async_copy(outgoing.at[me], out_ref.at[:, r_me, c_me], local.at[2])
     mine.start()
     second = []
@@ -180,6 +216,13 @@
             send_sem=send2.at[offset], recv_sem=recv2.at[sender],
             device_id={"particle": sender}, device_id_type=MESH,
         ).wait_recv()
+    for col in range(grid_cols):
+        for target, sem in ((top_ref, top_sem), (bottom_ref, bottom_sem)):
+            pltpu.make_async_remote_copy(
+                src_ref=outgoing.at[me], dst_ref=edge(target, col), send_sem=send4.at[me],
+                recv_sem=sem.at[col], device_id={"particle": me, "space": above},
+                device_id_type=MESH,
+            ).wait_recv()
 
 
 def resample(tile, ancestors, altimetry):
@@ -189,10 +232,13 @@
     grid_cols = count // grid_rows
     rows, cols = height // grid_rows, width // grid_cols
     sems = pltpu.SemaphoreType.DMA((count,))
+    edges = pltpu.SemaphoreType.DMA((grid_cols,))
     return pl.pallas_call(
-        functools.partial(exchange_kernel, count, grid_cols),
+        functools.partial(exchange_kernel, count, grid_rows, grid_cols),
         out_shape=(
             jax.ShapeDtypeStruct(tile.shape, tile.dtype),
+            jax.ShapeDtypeStruct((fields, rows, width), tile.dtype),
+            jax.ShapeDtypeStruct((fields, rows, width), tile.dtype),
             jax.ShapeDtypeStruct((count,) + altimetry.shape, altimetry.dtype),
         ),
         in_specs=[
@@ -202,12 +248,14 @@
         ],
         out_specs=(
             pl.BlockSpec(memory_space=pl.ANY),
+            pl.BlockSpec(memory_space=pl.ANY),
+            pl.BlockSpec(memory_space=pl.ANY),
             pl.BlockSpec(memory_space=pltpu.VMEM),
         ),
         scratch_shapes=[
             pltpu.VMEM((count, fields, rows, cols), tile.dtype),
             pltpu.VMEM((count, fields, rows, cols), tile.dtype),
-            sems, sems, sems, sems, sems, sems,
+            sems, sems, sems, sems, sems, sems, sems, edges, edges,
             pltpu.SemaphoreType.DMA((3,)),
         ],
         compiler_params=pltpu.CompilerParams(collective_id=0, has_side_effects=True),
@@ -235,13 +283,15 @@
     levels = level_coefs.shape[1]
     width_y = ensemble.shape[3]
     reach = 2 * STEPS
-    state, gathered = resample(ensemble[0], ancestors, altimetry)
+    depth = with_halo(depth_levels, (("space", 0),), reach)
+    wide_lines = with_halo(altimetry, (("space", 2),), reach)
+    tile, top, bottom, gathered = resample(ensemble[0], ancestors, wide_lines)
     all_lines = jnp.moveaxis(gathered, 0, 1).reshape(
-        (altimetry.shape[0], -1) + altimetry.shape[2:]
-    )
-    state = with_halo(state, (("space", 1),), reach)
-    depth = with_halo(depth_levels, (("space", 0),), reach)
-    all_lines = with_halo(all_lines, (("space", 2),), reach)
+        (altimetry.shape[0], -1) + wide_lines.shape[2:]
+    )
+    state = jnp.concatenate(
+        [top[:, top.shape[1] - reach :], tile, bottom[:, :reach]], axis=1
+    )
     span = depth.shape[0]
     level_ids = jnp.arange(levels, dtype=jnp.int32)
     masks = (level_ids[:, None, None] < depth[None]).astype(jnp.float32)

time: 157 us -> 174 us (1.11)
  the two profiles are of different devices: /device:TPU:19 before, /device:TPU:60 now
where the time goes in v3:
time: 174 us; the launch traced here: 173 us
  Pallas kernels  140 us (80%)
  other arithmetic  20.5 us (12%)
  local copies, waits for them, and re-layouts  8.24 us (5%)
  starting transfers between devices  3.49 us (2%)
    pallas_call x1, Pallas kernels, resample(): pl.pallas_call(functools.partial(exchange_kernel, count, grid_rows, grid_...  140 us
    sub x3, other arithmetic, gradients(): laplace = east + west + padded[..., 2:] + padded[..., :-2] - 4.0 * center  9.07 us
    mul x3, other arithmetic, finish(): masks * (east_vel + DT * (CORIOLIS * north_vel - GRAVITY * grad_x + visc...  4.03 us
    ppermute x2, starting transfers between devices, with_halo(): lax.ppermute(lax.slice_in_dim(block, 0, width, axis=dim), axis, backward)  3.48 us
  transfers between devices with their start and end apart: 4, of which 0 were waited for; matrix products, arithmetic and copies ran while one was open for 4% of the time, Pallas kernels for 81%

profile of v3, /device:TPU:60, one launch (start us, length us, event | category | flops | bytes accessed | tf_op | source)
XLA Modules:
  0.0 173.5 jit_solution(16331393760568306728)
XLA Ops:
  0.0 0.8 fusion.82
  0.8 0.0 collective-permute-start
  0.8 1.7 %collective-permute-start.1 = (s32[6,1024]{1,0:T(8,128)S(1)}, s32[6,1024]{1,0:T(8,128)S(1)}, u32[]{:S(2)}, u32[]{:S(2)}) collective-permute-start(s32[6,1024]{1,0:T(8,128)S(1)} %get-tuple-element.38), channel_id=1, source_target_pairs={{1,0},{2,1},{3,2},{4,3},{5,4},{6,5},{7,6},{8,7},{9,8},{10,9},{11,1... | collective-permute-start | bytes 73736 | tf_op jit(solution)/shard_map/ppermute | solution.py:30
  2.6 0.8 fusion.84
  3.4 0.0 collective-permute-start.2
  3.4 1.7 %collective-permute-start.3 = (f32[3,4,6]{2,1,0:T(4,128)S(1)}, f32[3,4,6]{2,1,0:T(4,128)S(1)}, u32[]{:S(2)}, u32[]{:S(2)}) collective-permute-start(f32[3,4,6]{2,1,0:T(4,128)S(1)} %get-tuple-element.43), channel_id=1, source_target_pairs={{1,0},{2,1},{3,2},{4,3},{5,4},{6,5},{7,6},{8,7},{9,8},{10,9},{11,1... | collective-permute-start | bytes 872 | tf_op jit(solution)/shard_map/ppermute | solution.py:30
  5.2 0.8 slice_bitcast_fusion.8
  6.0 0.1 convert_reduce_fusion.2
  6.1 0.1 convert_reduce_fusion
  6.2 0.8 multiply_bitcast_fusion.2
  7.0 0.0 collective-permute-done.2
  7.1 0.0 collective-permute-done.3
  7.1 1.4 pad_maximum_fusion.2.alt_ref
  8.4 139.7 %shard_map.64 = (f32[13,32,1024]{2,1,0:T(8,128)}, f32[13,8,1024]{2,1,0:T(8,128)}, f32[13,8,1024]{2,1,0:T(8,128)}, f32[16,3,4,44]{3,2,1,0:T(4,128)}) custom-call(s32[16]{0:T(128)} %anc_ref.1, f32[13,32,1024]{2,1,0:T(8,128)} %bitcast.82, f32[3,4,44]{2,1,0:T(4,128)} %pad_maximum_fusion.2.alt_ref), custom_call_target="tpu_custom_call" | custom-call | tf_op jit(solution)/shard_map/pallas_call | solution.py:236
  148.1 1.6 fusion.83
  149.7 1.0 slice.360
  150.7 0.0 collective-permute-done
  150.8 0.0 collective-permute-done.1
  150.8 0.1 fusion.11
  151.0 0.6 maximum_multiply_fusion
  151.6 0.5 slice.458
  152.1 3.2 %multiply_subtract_fusion = (f32[13,42,1024]{2,1,0:T(8,128)S(1)}, f32[13,42,1024]{2,1,0:T(8,128)S(1)}, f32[13,42,1024]{2,1,0:T(8,128)S(1)}) fusion(f32[13,42,1024]{2,1,0:T(8,128)S(1)} %slice.458, f32[13,44,1024]{2,1,0:T(8,128)S(1)} %maximum_multiply_fusion), kind=kLoop, calls=%fused_computation.3 | loop fusion | flops 5031936 | bytes 13418496 | tf_op jit(solution)/shard_map/sub | solution.py:46
  155.3 0.3 fusion.10
  155.6 0.4 fusion.2
  156.1 0.1 fusion.59
  156.2 1.0 fusion.41
  157.3 0.2 pad_maximum_fusion
  157.5 0.4 slice.480
  158.0 3.6 %multiply_subtract_fusion.2 = (f32[13,38,1024]{2,1,0:T(8,128)S(1)}, f32[13,38,1024]{2,1,0:T(8,128)S(1)}, f32[13,38,1024]{2,1,0:T(8,128)}) fusion(f32[13,38,1024]{2,1,0:T(8,128)S(1)} %slice.480, f32[13,40,1024]{2,1,0:T(8,128)S(1)} %pad_maximum_fusion), kind=kLoop, calls=%fused_computation.15 | loop fusion | flops 4552704 | bytes 12140544 | tf_op jit(solution)/shard_map/sub | solution.py:46
  161.6 1.4 fusion.28
  163.0 0.4 fusion.8
  163.4 0.1 fusion.62
  163.6 2.1 %fusion.26 = (f32[4,36,1024]{2,1,0:T(8,128)S(1)}, f32[4,36,1024]{2,1,0:T(8,128)S(1)}, f32[4,36,1024]{2,1,0:T(8,128)S(1)}) fusion(f32[13,38,1024]{2,1,0:T(8,128)S(1)} %get-tuple-element.28, f32[4,40,1024]{2,1,0:T(8,128)S(1)} %get-tuple-element.14, f32[4,40,1024]{2,1,0:T(8,128)S(1)} %get-tuple-element.13, f32[4,44,1024]{2,1,0:T(8,128)S(1)} %fusion.11, ...), kind=kLoop, calls=%fused_computation.58 | loop fusion | flops 3244032 | bytes 7372832 | tf_op jit(solution)/shard_map/mul | solution.py:70
  165.7 0.0 copy-start.3
  165.7 0.2 pad_maximum_fusion.1
  166.0 0.6 copy-done.1
  166.5 0.2 copy-done.3
  166.7 0.2 copy-done.5
  167.0 0.4 slice.502
  167.4 2.3 %multiply_subtract_fusion.1 = (f32[13,34,1024]{2,1,0:T(8,128)S(1)}, f32[13,34,1024]{2,1,0:T(8,128)S(1)}, f32[13,34,1024]{2,1,0:T(8,128)S(1)}) fusion(f32[13,34,1024]{2,1,0:T(8,128)S(1)} %slice.502, f32[13,36,1024]{2,1,0:T(8,128)S(1)} %pad_maximum_fusion.1), kind=kLoop, calls=%fused_computation.12 | loop fusion | flops 4073472 | bytes 10862592 | tf_op jit(solution)/shard_map/sub | solution.py:46
  169.7 0.0 copy-start.4
  169.7 0.3 fusion.13
  170.0 0.6 copy-done.9
  170.6 0.4 fusion.5
  171.0 0.1 fusion.73
  171.2 0.1 copy-done.6
  171.3 0.9 fusion.54
  172.2 1.3 maximum_bitcast_fusion
  (36 shorter events, 0.3 us)
Async XLA Ops:
  0.0 150.8 %copy-start.10 = (s32[32,1024]{1,0:T(8,128)S(1)}, s32[32,1024]{1,0:T(8,128)}, u32[]{:S(2)}) copy-start(s32[32,1024]{1,0:T(8,128)} %param.8) | copy-start | bytes 393220
  0.8 149.9 %collective-permute-start = (s32[6,1024]{1,0:T(8,128)S(1)}, s32[6,1024]{1,0:T(8,128)S(1)}, u32[]{:S(2)}, u32[]{:S(2)}) collective-permute-start(s32[6,1024]{1,0:T(8,128)S(1)} %get-tuple-element.37), channel_id=1, source_target_pairs={{0,1},{1,2},{2,3},{3,4},{4,5},{5,6},{6,7},{7,8},{8,9},{9,10},{10,1... | collective-permute-start | bytes 73736 | tf_op jit(solution)/shard_map/ppermute | solution.py:27
  0.8 149.9 %collective-permute-start.1 = (s32[6,1024]{1,0:T(8,128)S(1)}, s32[6,1024]{1,0:T(8,128)S(1)}, u32[]{:S(2)}, u32[]{:S(2)}) collective-permute-start(s32[6,1024]{1,0:T(8,128)S(1)} %get-tuple-element.38), channel_id=1, source_target_pairs={{1,0},{2,1},{3,2},{4,3},{5,4},{6,5},{7,6},{8,7},{9,8},{10,9},{11,1... | collective-permute-start | bytes 73736 | tf_op jit(solution)/shard_map/ppermute | solution.py:30
  3.4 3.6 %collective-permute-start.2 = (f32[3,4,6]{2,1,0:T(4,128)S(1)}, f32[3,4,6]{2,1,0:T(4,128)S(1)}, u32[]{:S(2)}, u32[]{:S(2)}) collective-permute-start(f32[3,4,6]{2,1,0:T(4,128)S(1)} %get-tuple-element.42), channel_id=1, source_target_pairs={{0,1},{1,2},{2,3},{3,4},{4,5},{5,6},{6,7},{7,8},{8,9},{9,10},{10,1... | collective-permute-start | bytes 872 | tf_op jit(solution)/shard_map/ppermute | solution.py:27
  3.4 3.6 %collective-permute-start.3 = (f32[3,4,6]{2,1,0:T(4,128)S(1)}, f32[3,4,6]{2,1,0:T(4,128)S(1)}, u32[]{:S(2)}, u32[]{:S(2)}) collective-permute-start(f32[3,4,6]{2,1,0:T(4,128)S(1)} %get-tuple-element.43), channel_id=1, source_target_pairs={{1,0},{2,1},{3,2},{4,3},{5,4},{6,5},{7,6},{8,7},{9,8},{10,9},{11,1... | collective-permute-start | bytes 872 | tf_op jit(solution)/shard_map/ppermute | solution.py:30
  6.0 144.8 %copy-start.12 = (s32[64]{0:T(128)}, s32[64]{0:T(128)S(1)}, u32[]{:S(2)}) copy-start(s32[64]{0:T(128)S(1)} %get-tuple-element.44) | copy-start | bytes 772
  6.0 144.8 %copy-start.14 = (s32[64]{0:T(128)}, s32[64]{0:T(128)S(1)}, u32[]{:S(2)}) copy-start(s32[64]{0:T(128)S(1)} %get-tuple-element.46) | copy-start | bytes 772
  148.1 2.8 %copy-start = (f32[13,32,1024]{2,1,0:T(8,128)S(1)}, f32[13,32,1024]{2,1,0:T(8,128)}, u32[]{:S(2)}) copy-start(f32[13,32,1024]{2,1,0:T(8,128)} %get-tuple-element.10) | copy-start | bytes 5111812
  148.1 2.8 %copy-start.7 = (f32[13,8,1024]{2,1,0:T(8,128)S(1)}, f32[13,8,1024]{2,1,0:T(8,128)}, u32[]{:S(2)}) copy-start(f32[13,8,1024]{2,1,0:T(8,128)} %get-tuple-element.11) | copy-start | bytes 1277956
  161.6 1.4 copy-start.11
  161.6 1.4 copy-start.15
  163.4 2.3 %copy-start.8 = (f32[1,36,1024]{2,1,0:T(8,128)}, f32[1,36,1024]{2,1,0:T(8,128)S(1)}, u32[]{:S(2)}) copy-start(f32[1,36,1024]{2,1,0:T(8,128)S(1)} %slice_bitcast_fusion.2) | copy-start | bytes 442372
  165.7 0.8 copy-start.1
  165.7 1.0 copy-start.3
  165.7 1.3 copy-start.5
  169.7 0.9 copy-start.9
  169.7 0.9 copy-start.13
  169.7 1.5 copy-start.2
  169.7 1.5 copy-start.4
  169.7 1.5 copy-start.6

commit v4 on v1

--- a/solution.py
+++ b/solution.py
@@ -214,26 +214,122 @@
     )(ancestors, tile, altimetry)
 
 
+def stencil_kernel(coef_ref, tile_ref, aux_ref, top_ref, bottom_ref, hit_ref, out_ref, state, aux):
+    fields, rows, width = tile_ref.shape
+    extra = aux_ref.shape[0]
+    reach = top_ref.shape[1]
+    levels = coef_ref.shape[1]
+    span = state.shape[1]
+    state[:, :reach] = top_ref[:fields]
+    state[:, reach : reach + rows] = tile_ref[...]
+    state[:, reach + rows :] = bottom_ref[:fields]
+    aux[:, :reach] = top_ref[fields:]
+    aux[:, reach : reach + rows] = aux_ref[...]
+    aux[:, reach + rows :] = bottom_ref[fields:]
+
+    lane = lax.broadcasted_iota(jnp.int32, (span, width), 1)
+    first_lane = lane == 0
+    last_lane = lane == width - 1
+
+    def east(f):
+        return pltpu.roll(f, span - 1, 0)
+
+    def west(f):
+        return pltpu.roll(f, 1, 0)
+
+    def north(f):
+        return jnp.where(last_lane, 0.0, pltpu.roll(f, width - 1, 1))
+
+    def south(f):
+        return jnp.where(first_lane, 0.0, pltpu.roll(f, 1, 1))
+
+    def parts(f):
+        e, w, n, s = east(f), west(f), north(f), south(f)
+        return (e - w) * 0.5, (n - s) * 0.5, e + w + n + s - 4.0 * f
+
+    depth = aux[extra - 1]
+    masks = [(k < depth).astype(jnp.float32) for k in range(levels)]
+    surface = masks[0]
+    for field in range(fields):
+        state[field] = state[field] * masks[field % levels]
+    for step in range(STEPS):
+        spread = None
+        for k in range(levels):
+            ddx_u = parts(state[k])[0]
+            ddy_v = parts(state[levels + k])[1]
+            term = (coef_ref[0, k] * masks[k]) * (ddx_u + ddy_v)
+            spread = term if spread is None else spread + term
+        height = state[3 * levels]
+        height_one = surface * (height - DT * spread)
+        hit = hit_ref[step]
+        height_two = surface * (height_one + NUDGE * hit * (aux[step] - height_one))
+        grad_x, grad_y, unused = parts(height_two)
+        for k in range(levels):
+            visc = 0.2 * coef_ref[1, k]
+            kappa = 0.2 * coef_ref[2, k]
+            east_vel = state[k]
+            north_vel = state[levels + k]
+            temper = state[2 * levels + k]
+            unused_x, unused_y, lap_u = parts(east_vel)
+            unused_x, unused_y, lap_v = parts(north_vel)
+            ddx_t, ddy_t, lap_t = parts(temper)
+            state[k] = masks[k] * (
+                east_vel + DT * (CORIOLIS * north_vel - grad_x + visc * lap_u)
+            )
+            state[levels + k] = masks[k] * (
+                north_vel + DT * (-CORIOLIS * east_vel - grad_y + visc * lap_v)
+            )
+            state[2 * levels + k] = masks[k] * (
+                temper + DT * (kappa * lap_t - east_vel * ddx_t - north_vel * ddy_t)
+            )
+        state[3 * levels] = height_two
+    out_ref[...] = state[:, reach : reach + rows]
+
+
+def run_steps(coefs, tile, aux, top, bottom, hits):
+    fields, rows, width = tile.shape
+    span = rows + 2 * top.shape[1]
+    vmem = pl.BlockSpec(memory_space=pltpu.VMEM)
+    return pl.pallas_call(
+        stencil_kernel,
+        out_shape=jax.ShapeDtypeStruct(tile.shape, tile.dtype),
+        in_specs=[pl.BlockSpec(memory_space=pltpu.SMEM)] + [vmem] * 5,
+        out_specs=vmem,
+        scratch_shapes=[
+            pltpu.VMEM((fields, span, width), tile.dtype),
+            pltpu.VMEM((aux.shape[0], span, width), tile.dtype),
+        ],
+    )(coefs, tile, aux, top, bottom, hits)
+
+
 def per_device(ensemble, ancestors, depth_levels, level_coefs, altimetry, obs_rows):
-    levels = level_coefs.shape[1]
     width_y = ensemble.shape[3]
-    state, gathered = resample(ensemble[0], ancestors, altimetry)
+    reach = 8
+    tile, gathered = resample(ensemble[0], ancestors, altimetry)
     all_lines = jnp.moveaxis(gathered, 0, 1).reshape(
         (altimetry.shape[0], -1) + altimetry.shape[2:]
     )
-    level_ids = jnp.arange(levels, dtype=jnp.int32)
-    masks = (level_ids[:, None, None] < depth_levels[None]).astype(jnp.float32)
-    full_mask = jnp.concatenate([masks, masks, masks, masks[:1]], axis=0)
-    state = state * full_mask
     columns = jnp.arange(width_y, dtype=jnp.int32)
+    targets = []
+    hits = []
     for step in range(STEPS):
-        lines = all_lines[step]
         onehot = (obs_rows[step][:, None] == columns[None, :]).astype(jnp.float32)
-        target = jnp.dot(
-            lines.T, onehot, precision=lax.Precision.HIGHEST, preferred_element_type=jnp.float32
-        )
-        hit = jnp.sum(onehot, axis=0)[None, :]
-        state = one_step(state, masks, level_coefs, target, hit)
+        targets.append(
+            jnp.dot(
+                all_lines[step].T, onehot, precision=lax.Precision.HIGHEST,
+                preferred_element_type=jnp.float32,
+            )
+        )
+        hits.append(jnp.sum(onehot, axis=0)[None, :])
+    aux = jnp.stack(targets + [depth_levels.astype(jnp.float32)], axis=0)
+    count = lax.axis_size("space")
+    forward = [(i, (i + 1) % count) for i in range(count)]
+    backward = [(target, source) for source, target in forward]
+    low = jnp.concatenate([tile[:, :reach], aux[:, :reach]], axis=0)
+    high = jnp.concatenate([tile[:, -reach:], aux[:, -reach:]], axis=0)
+    top = lax.ppermute(high, "space", forward)
+    bottom = lax.ppermute(low, "space", backward)
+    state = run_steps(level_coefs, tile, aux, top, bottom, jnp.stack(hits, axis=0))
     return state[None]
 
 

time: 152 us -> 125 us (0.82)
  starting transfers between devices: 20.3 us -> 3.49 us
  other arithmetic: 14.6 us -> 1.87 us
  Pallas kernels: 94.7 us -> 104 us
  waiting for transfers between devices: 20.1 us -> 11 us
  local copies, waits for them, and re-layouts: 0.32 us -> 3.95 us
    ppermute x12 -> x2, starting transfers between devices: 20.3 us -> 3.49 us  [the longest x1 3.4 us: per_device(): bottom = lax.ppermute(low, 'space', backward)]
    pallas_call x0 -> x1, Pallas kernels: none -> 9.16 us  [run_steps(): pl.pallas_call(stencil_kernel, out_shape=jax.ShapeDtypeStruct(tile.shape,...]
    ppermute x12 -> x2, waiting for transfers between devices: 20.1 us -> 11 us  [the longest x1 11 us: per_device(): top = lax.ppermute(high, 'space', forward)]
    sub x6 -> x0, other arithmetic: 6.34 us -> none  [the longest x3 5.93 us: gradients(): laplace = east + west + padded[..., 2:] + padded[..., :-2] - 4.0 * center]
    mul x12 -> x0, other arithmetic: 5.13 us -> none  [the longest x1 1.68 us: per_device(): state = state * full_mask]
    unnamed x8, local copies, waits for them, and re-layouts: 0.02 us -> 2.15 us
    another operation x0 -> x3, other arithmetic: none -> 1.56 us  [the longest x2 0.96 us: per_device(): aux = jnp.stack(targets + [depth_levels.astype(jnp.float32)], axis=0)]
  transfers between devices with their start and end apart: 12 -> 2, of which waited for: 9 -> 1; matrix products, arithmetic and copies ran while one was open for 0% -> 1% of each run, Pallas kernels for 0% -> 0%
where the time goes in v4:
time: 125 us
  Pallas kernels  104 us (83%)
  waiting for transfers between devices  11 us (9%)
  local copies, waits for them, and re-layouts  3.95 us (3%)
  starting transfers between devices  3.49 us (3%)
  other arithmetic  1.87 us (1%)
    pallas_call x1, Pallas kernels, resample(): pl.pallas_call(functools.partial(exchange_kernel, count, grid_cols), out_...  94.7 us
    ppermute x1, waiting for transfers between devices, per_device(): top = lax.ppermute(high, 'space', forward)  11 us
    pallas_call x1, Pallas kernels, run_steps(): pl.pallas_call(stencil_kernel, out_shape=jax.ShapeDtypeStruct(tile.shape,...  9.16 us
    ppermute x1, starting transfers between devices, per_device(): bottom = lax.ppermute(low, 'space', backward)  3.4 us
  transfers between devices with their start and end apart: 2, of which 1 were waited for; matrix products, arithmetic and copies ran while one was open for 1% of the time, Pallas kernels for 0%

profile of v4, /device:TPU:24, one launch (start us, length us, event | category | flops | bytes accessed | tf_op | source)
XLA Modules:
  0.0 125.2 jit_solution(9957941480759108021)
XLA Ops:
  0.0 0.8 slice_bitcast_fusion.2
  0.8 0.9 convert_bitcast_fusion
  1.7 94.7 %shard_map.64 = (f32[13,32,1024]{2,1,0:T(8,128)}, f32[16,3,4,32]{3,2,1,0:T(4,128)}) custom-call(s32[16]{0:T(128)} %anc_ref.1, f32[13,32,1024]{2,1,0:T(8,128)} %bitcast.26, f32[3,4,32]{2,1,0:T(4,128)} %alt_ref.1), custom_call_target="tpu_custom_call" | custom-call | tf_op jit(solution)/shard_map/pallas_call | solution.py:192
  96.4 0.0 copy-start
  96.4 0.9 fusion.5
  97.3 0.3 convolution_bitcast_fusion
  97.6 0.3 convolution_bitcast_fusion.2
  97.9 0.3 convolution_bitcast_fusion.1
  98.3 0.0 copy-start.1
  98.3 0.0 copy-done
  98.3 0.1 fusion.3
  98.4 0.1 collective-permute-start
  98.6 0.5 copy-done.1
  99.1 3.4 %collective-permute-start.1 = (f32[17,8,1024]{2,1,0:T(8,128)S(1)}, f32[17,8,1024]{2,1,0:T(8,128)S(1)}, u32[]{:S(2)}, u32[]{:S(2)}) collective-permute-start(f32[17,8,1024]{2,1,0:T(8,128)S(1)} %pad_maximum_fusion.1), channel_id=1, source_target_pairs={{1,0},{2,1},{3,2},{4,3},{5,4},{6,5},{7,6},{8,7},{9,8},{10,9},{11,1... | collective-permute-start | bytes 1671176 | tf_op jit(solution)/shard_map/ppermute | solution.py:331
  102.5 0.1 convert_reduce_fusion.2
  102.6 0.1 convert_reduce_fusion
  102.7 0.6 pad_maximum_fusion.3.hit_ref
  103.3 11.0 %collective-permute-done.top_ref = f32[17,8,1024]{2,1,0:T(8,128)S(1)} collective-permute-done((f32[17,8,1024]{2,1,0:T(8,128)S(1)}, f32[17,8,1024]{2,1,0:T(8,128)S(1)}, u32[]{:S(2)}, u32[]{:S(2)}) %collective-permute-start) | collective-permute-done | bytes 557088 | tf_op jit(solution)/shard_map/ppermute | solution.py:330
  114.4 0.0 copy-start.2
  114.4 0.0 collective-permute-done.1.bottom_ref
  114.4 0.8 copy-done.2
  115.2 0.0 copy-start.3
  115.2 0.8 copy-done.3
  116.0 9.2 %shard_map.65 = f32[13,32,1024]{2,1,0:T(8,128)} custom-call(f32[3,4]{1,0:T(4,128)} %coef_ref.1, f32[13,32,1024]{2,1,0:T(8,128)} %get-tuple-element.7.tile_ref, f32[4,32,1024]{2,1,0:T(8,128)} %copy-done.1, f32[17,8,1024]{2,1,0:T(8,128)} %copy-done.2, f32[17,8,1024]{2,1,0:T(8,128)} %copy-done.3, f32[3,1,1024]{2,1,0:T(1,128)} %pad_maximum_fusion.3.hit_ref), custom_call_target="tpu_custom_call" | custom-call | tf_op jit(solution)/shard_map/pallas_call | solution.py:293
  (4 shorter events, 0.1 us)
Async XLA Ops:
  96.4 1.9 %copy-start = (f32[13,32,1024]{2,1,0:T(8,128)S(1)}, f32[13,32,1024]{2,1,0:T(8,128)}, u32[]{:S(2)}) copy-start(f32[13,32,1024]{2,1,0:T(8,128)} %get-tuple-element.7.tile_ref) | copy-start | bytes 5111812
  98.3 0.8 copy-start.1
  98.4 16.0 %collective-permute-start = (f32[17,8,1024]{2,1,0:T(8,128)S(1)}, f32[17,8,1024]{2,1,0:T(8,128)S(1)}, u32[]{:S(2)}, u32[]{:S(2)}) collective-permute-start(f32[17,8,1024]{2,1,0:T(8,128)S(1)} %pad_maximum_fusion), channel_id=1, source_target_pairs={{0,1},{1,2},{2,3},{3,4},{4,5},{5,6},{6,7},{7,8},{8,9},{9,10},{10,1... | collective-permute-start | bytes 1671176 | tf_op jit(solution)/shard_map/ppermute | solution.py:330
  99.1 15.3 %collective-permute-start.1 = (f32[17,8,1024]{2,1,0:T(8,128)S(1)}, f32[17,8,1024]{2,1,0:T(8,128)S(1)}, u32[]{:S(2)}, u32[]{:S(2)}) collective-permute-start(f32[17,8,1024]{2,1,0:T(8,128)S(1)} %pad_maximum_fusion.1), channel_id=1, source_target_pairs={{1,0},{2,1},{3,2},{4,3},{5,4},{6,5},{7,6},{8,7},{9,8},{10,9},{11,1... | collective-permute-start | bytes 1671176 | tf_op jit(solution)/shard_map/ppermute | solution.py:331
  114.4 0.8 copy-start.2
  115.2 0.8 copy-start.3

commit v5 on v4

--- a/solution.py
+++ b/solution.py
@@ -104,11 +104,13 @@
 
 
 def exchange_kernel(
-    count, grid_cols, anc_ref, ens_ref, alt_ref, out_ref, lines_ref,
-    held, outgoing, send1, recv1, send2, recv2, send3, recv3, local,
+    count, grid_cols, groups, anc_ref, ens_ref, alt_ref, out_ref, lines_ref,
+    held_a, held_b, outgoing_a, outgoing_b, send1, recv1, send2, recv2, send3, recv3, local,
 ):
     me = lax.axis_index("particle")
-    rows, cols = held.shape[2], held.shape[3]
+    held = (held_a, held_b)
+    outgoing = (outgoing_a, outgoing_b)
+    rows, cols = held_a.shape[2], held_a.shape[3]
 
     barrier = pltpu.get_barrier_semaphore()
     for offset in range(1, count):
@@ -116,70 +118,95 @@
         pl.semaphore_signal(barrier, inc=1, device_id={"particle": peer}, device_id_type=MESH)
     pl.semaphore_wait(barrier, count - 1)
 
-    def chunk_of(dest):
+    def chunk_of(dest, fields):
         r, c = window(dest, grid_cols, rows, cols)
-        return ens_ref.at[:, r, c]
-
-    own = pltpu.make_async_copy(chunk_of(me), held.at[me], local.at[0])
-    own.start()
-    own_lines = pltpu.make_async_copy(alt_ref, lines_ref.at[me], local.at[1])
+        return ens_ref.at[fields, r, c]
+
+    def first_copy(group, fields, offset, peer):
+        return pltpu.make_async_remote_copy(
+            src_ref=chunk_of(peer, fields), dst_ref=held[group].at[me],
+            send_sem=send1.at[group, offset], recv_sem=recv1.at[group, me],
+            device_id={"particle": peer}, device_id_type=MESH,
+        )
+
+    def second_copy(group, fields, offset, peer):
+        r_me, c_me = window(me, grid_cols, rows, cols)
+        return pltpu.make_async_remote_copy(
+            src_ref=outgoing[group].at[peer], dst_ref=out_ref.at[fields, r_me, c_me],
+            send_sem=send2.at[group, offset], recv_sem=recv2.at[group, me],
+            device_id={"particle": peer}, device_id_type=MESH,
+        )
+
+    own_lines = pltpu.make_async_copy(alt_ref, lines_ref.at[me], local.at[0])
     own_lines.start()
-    first = []
+    line_copies = []
     for offset in range(1, count):
         peer = lax.rem(me + offset, count)
-        copy = pltpu.make_async_remote_copy(
-            src_ref=chunk_of(peer), dst_ref=held.at[me], send_sem=send1.at[offset],
-            recv_sem=recv1.at[me], device_id={"particle": peer}, device_id_type=MESH,
-        )
-        copy.start()
         lines = pltpu.make_async_remote_copy(
             src_ref=alt_ref, dst_ref=lines_ref.at[me], send_sem=send3.at[offset],
             recv_sem=recv3.at[me], device_id={"particle": peer}, device_id_type=MESH,
         )
         lines.start()
-        first.append((copy, lines))
-    own.wait()
+        line_copies.append(lines)
+
+    own_parts = []
+    firsts = []
+    for group, fields in enumerate(groups):
+        own = pltpu.make_async_copy(chunk_of(me, fields), held[group].at[me], local.at[1 + group])
+        own.start()
+        own_parts.append(own)
+        copies = []
+        for offset in range(1, count):
+            copy = first_copy(group, fields, offset, lax.rem(me + offset, count))
+            copy.start()
+            copies.append(copy)
+        firsts.append(copies)
+
+    seconds = []
+    for group, fields in enumerate(groups):
+        own_parts[group].wait()
+        for offset, copy in zip(range(1, count), firsts[group]):
+            sender = lax.rem(me + count - offset, count)
+            copy.wait_send()
+            pltpu.make_async_remote_copy(
+                src_ref=chunk_of(me, fields), dst_ref=held[group].at[sender],
+                send_sem=send1.at[group, offset], recv_sem=recv1.at[group, sender],
+                device_id={"particle": sender}, device_id_type=MESH,
+            ).wait_recv()
+        for member in range(count):
+            source = jnp.clip(anc_ref[member], 0, count - 1)
+            outgoing[group][member] = held[group][source]
+        r_me, c_me = window(me, grid_cols, rows, cols)
+        mine = pltpu.make_async_copy(
+            outgoing[group].at[me], out_ref.at[fields, r_me, c_me], local.at[3 + group]
+        )
+        mine.start()
+        copies = [mine]
+        for offset in range(1, count):
+            copy = second_copy(group, fields, offset, lax.rem(me + offset, count))
+            copy.start()
+            copies.append(copy)
+        seconds.append(copies)
+
     own_lines.wait()
-    for offset, (copy, lines) in zip(range(1, count), first):
+    for offset, lines in zip(range(1, count), line_copies):
         sender = lax.rem(me + count - offset, count)
-        copy.wait_send()
         lines.wait_send()
-        pltpu.make_async_remote_copy(
-            src_ref=chunk_of(me), dst_ref=held.at[sender], send_sem=send1.at[offset],
-            recv_sem=recv1.at[sender], device_id={"particle": sender}, device_id_type=MESH,
-        ).wait_recv()
         pltpu.make_async_remote_copy(
             src_ref=alt_ref, dst_ref=lines_ref.at[sender], send_sem=send3.at[offset],
             recv_sem=recv3.at[sender], device_id={"particle": sender}, device_id_type=MESH,
         ).wait_recv()
-
-    for member in range(count):
-        source = jnp.clip(anc_ref[member], 0, count - 1)
-        outgoing[member] = held[source]
-
-    r_me, c_me = window(me, grid_cols, rows, cols)
-    mine = pltpu.make_async_copy(outgoing.at[me], out_ref.at[:, r_me, c_me], local.at[2])
-    mine.start()
-    second = []
-    for offset in range(1, count):
-        peer = lax.rem(me + offset, count)
-        copy = pltpu.make_async_remote_copy(
-            src_ref=outgoing.at[peer], dst_ref=out_ref.at[:, r_me, c_me],
-            send_sem=send2.at[offset], recv_sem=recv2.at[me],
-            device_id={"particle": peer}, device_id_type=MESH,
-        )
-        copy.start()
-        second.append(copy)
-    mine.wait()
-    for offset, copy in zip(range(1, count), second):
-        sender = lax.rem(me + count - offset, count)
-        r_s, c_s = window(sender, grid_cols, rows, cols)
-        copy.wait_send()
-        pltpu.make_async_remote_copy(
-            src_ref=outgoing.at[me], dst_ref=out_ref.at[:, r_s, c_s],
-            send_sem=send2.at[offset], recv_sem=recv2.at[sender],
-            device_id={"particle": sender}, device_id_type=MESH,
-        ).wait_recv()
+    for group, fields in enumerate(groups):
+        seconds[group][0].wait()
+        for offset, copy in zip(range(1, count), seconds[group][1:]):
+            sender = lax.rem(me + count - offset, count)
+            r_s, c_s = window(sender, grid_cols, rows, cols)
+            copy.wait_send()
+            pltpu.make_async_remote_copy(
+                src_ref=outgoing[group].at[me], dst_ref=out_ref.at[fields, r_s, c_s],
+                send_sem=send2.at[group, offset], recv_sem=recv2.at[group, sender],
+                device_id={"particle": sender}, device_id_type=MESH,
+            ).wait_recv()
 
 
 def resample(tile, ancestors, altimetry):
@@ -188,9 +215,12 @@
     grid_rows = 4
     grid_cols = count // grid_rows
     rows, cols = height // grid_rows, width // grid_cols
+    split = (fields + 1) // 2
+    groups = (pl.ds(0, split), pl.ds(split, fields - split))
     sems = pltpu.SemaphoreType.DMA((count,))
+    grouped = pltpu.SemaphoreType.DMA((len(groups), count))
     return pl.pallas_call(
-        functools.partial(exchange_kernel, count, grid_cols),
+        functools.partial(exchange_kernel, count, grid_cols, groups),
         out_shape=(
             jax.ShapeDtypeStruct(tile.shape, tile.dtype),
             jax.ShapeDtypeStruct((count,) + altimetry.shape, altimetry.dtype),
@@ -205,10 +235,12 @@
             pl.BlockSpec(memory_space=pltpu.VMEM),
         ),
         scratch_shapes=[
-            pltpu.VMEM((count, fields, rows, cols), tile.dtype),
-            pltpu.VMEM((count, fields, rows, cols), tile.dtype),
-            sems, sems, sems, sems, sems, sems,
-            pltpu.SemaphoreType.DMA((3,)),
+            pltpu.VMEM((count, split, rows, cols), tile.dtype),
+            pltpu.VMEM((count, fields - split, rows, cols), tile.dtype),
+            pltpu.VMEM((count, split, rows, cols), tile.dtype),
+            pltpu.VMEM((count, fields - split, rows, cols), tile.dtype),
+            grouped, grouped, grouped, grouped, sems, sems,
+            pltpu.SemaphoreType.DMA((1 + 2 * len(groups),)),
         ],
         compiler_params=pltpu.CompilerParams(collective_id=0, has_side_effects=True),
     )(ancestors, tile, altimetry)

time: 125 us -> 119 us (0.952); the launches traced: 125 us -> 117 us
  Pallas kernels: 104 us -> 96.5 us
  starting transfers between devices: 3.49 us -> 4.91 us
    pallas_call x1, Pallas kernels: 94.7 us -> 87.4 us  [resample(): pl.pallas_call(functools.partial(exchange_kernel, count, grid_cols, group...]
    ppermute x1, waiting for transfers between devices: 11 us -> 8.42 us  [per_device(): top = lax.ppermute(high, 'space', forward)]
    ppermute x1, waiting for transfers between devices: 0.01 us -> 1.49 us  [per_device(): bottom = lax.ppermute(low, 'space', backward)]
    ppermute x1, starting transfers between devices: 3.4 us -> 4.83 us  [per_device(): bottom = lax.ppermute(low, 'space', backward)]
  transfers between devices with their start and end apart: 2 -> 2, of which waited for: 1 -> 2; matrix products, arithmetic and copies ran while one was open for 1% -> 1% of each run, Pallas kernels for 0% -> 0%
where the time goes in v5:
time: 119 us; the launch traced here: 117 us
  Pallas kernels  96.5 us (81%)
  waiting for transfers between devices  9.91 us (8%)
  starting transfers between devices  4.91 us (4%)
  local copies, waits for them, and re-layouts  3.14 us (3%)
  other arithmetic  1.87 us (2%)
    pallas_call x1, Pallas kernels, resample(): pl.pallas_call(functools.partial(exchange_kernel, count, grid_cols, group...  87.4 us
    pallas_call x1, Pallas kernels, run_steps(): pl.pallas_call(stencil_kernel, out_shape=jax.ShapeDtypeStruct(tile.shape,...  9.16 us
    ppermute x1, waiting for transfers between devices, per_device(): top = lax.ppermute(high, 'space', forward)  8.42 us
    ppermute x1, starting transfers between devices, per_device(): bottom = lax.ppermute(low, 'space', backward)  4.83 us
  transfers between devices with their start and end apart: 2, of which 2 were waited for; matrix products, arithmetic and copies ran while one was open for 1% of the time, Pallas kernels for 0%

profile of v5, /device:TPU:24, one launch (start us, length us, event | category | flops | bytes accessed | tf_op | source)
XLA Modules:
  0.0 117.4 jit_solution(14761329906226091402)
XLA Ops:
  0.0 0.8 slice_bitcast_fusion.2
  0.8 0.9 convert_bitcast_fusion
  1.7 87.4 %shard_map.64 = (f32[13,32,1024]{2,1,0:T(8,128)}, f32[16,3,4,32]{3,2,1,0:T(4,128)}) custom-call(s32[16]{0:T(128)} %anc_ref.1, f32[13,32,1024]{2,1,0:T(8,128)} %bitcast.26, f32[3,4,32]{2,1,0:T(4,128)} %alt_ref.1), custom_call_target="tpu_custom_call" | custom-call | tf_op jit(solution)/shard_map/pallas_call | solution.py:222
  89.1 0.0 copy-start
  89.1 0.9 fusion.5
  90.0 0.3 convolution_bitcast_fusion
  90.3 0.3 convolution_bitcast_fusion.2
  90.6 0.3 convolution_bitcast_fusion.1
  91.0 0.0 copy-start.1
  91.0 0.0 copy-done
  91.0 0.1 fusion.3
  91.1 0.1 collective-permute-start
  91.3 0.5 copy-done.1
  91.8 4.8 %collective-permute-start.1 = (f32[17,8,1024]{2,1,0:T(8,128)S(1)}, f32[17,8,1024]{2,1,0:T(8,128)S(1)}, u32[]{:S(2)}, u32[]{:S(2)}) collective-permute-start(f32[17,8,1024]{2,1,0:T(8,128)S(1)} %pad_maximum_fusion.1), channel_id=1, source_target_pairs={{1,0},{2,1},{3,2},{4,3},{5,4},{6,5},{7,6},{8,7},{9,8},{10,9},{11,1... | collective-permute-start | bytes 1671176 | tf_op jit(solution)/shard_map/ppermute | solution.py:363
  96.6 0.1 convert_reduce_fusion.2
  96.7 0.1 convert_reduce_fusion
  96.9 0.6 pad_maximum_fusion.3.hit_ref
  97.5 8.4 %collective-permute-done.top_ref = f32[17,8,1024]{2,1,0:T(8,128)S(1)} collective-permute-done((f32[17,8,1024]{2,1,0:T(8,128)S(1)}, f32[17,8,1024]{2,1,0:T(8,128)S(1)}, u32[]{:S(2)}, u32[]{:S(2)}) %collective-permute-start) | collective-permute-done | bytes 557088 | tf_op jit(solution)/shard_map/ppermute | solution.py:362
  105.9 0.0 copy-start.2
  105.9 1.5 %collective-permute-done.1.bottom_ref = f32[17,8,1024]{2,1,0:T(8,128)S(1)} collective-permute-done((f32[17,8,1024]{2,1,0:T(8,128)S(1)}, f32[17,8,1024]{2,1,0:T(8,128)S(1)}, u32[]{:S(2)}, u32[]{:S(2)}) %collective-permute-start.1) | collective-permute-done | bytes 557088 | tf_op jit(solution)/shard_map/ppermute | solution.py:363
  107.4 0.0 copy-done.2
  107.4 0.0 copy-start.3
  107.4 0.8 copy-done.3
  108.2 9.2 %shard_map.65 = f32[13,32,1024]{2,1,0:T(8,128)} custom-call(f32[3,4]{1,0:T(4,128)} %coef_ref.1, f32[13,32,1024]{2,1,0:T(8,128)} %get-tuple-element.7.tile_ref, f32[4,32,1024]{2,1,0:T(8,128)} %copy-done.1, f32[17,8,1024]{2,1,0:T(8,128)} %copy-done.2, f32[17,8,1024]{2,1,0:T(8,128)} %copy-done.3, f32[3,1,1024]{2,1,0:T(1,128)} %pad_maximum_fusion.3.hit_ref), custom_call_target="tpu_custom_call" | custom-call | tf_op jit(solution)/shard_map/pallas_call | solution.py:325
  (4 shorter events, 0.1 us)
Async XLA Ops:
  89.1 1.9 %copy-start = (f32[13,32,1024]{2,1,0:T(8,128)S(1)}, f32[13,32,1024]{2,1,0:T(8,128)}, u32[]{:S(2)}) copy-start(f32[13,32,1024]{2,1,0:T(8,128)} %get-tuple-element.7.tile_ref) | copy-start | bytes 5111812
  91.0 0.8 copy-start.1
  91.1 14.8 %collective-permute-start = (f32[17,8,1024]{2,1,0:T(8,128)S(1)}, f32[17,8,1024]{2,1,0:T(8,128)S(1)}, u32[]{:S(2)}, u32[]{:S(2)}) collective-permute-start(f32[17,8,1024]{2,1,0:T(8,128)S(1)} %pad_maximum_fusion), channel_id=1, source_target_pairs={{0,1},{1,2},{2,3},{3,4},{4,5},{5,6},{6,7},{7,8},{8,9},{9,10},{10,1... | collective-permute-start | bytes 1671176 | tf_op jit(solution)/shard_map/ppermute | solution.py:362
  91.8 15.6 %collective-permute-start.1 = (f32[17,8,1024]{2,1,0:T(8,128)S(1)}, f32[17,8,1024]{2,1,0:T(8,128)S(1)}, u32[]{:S(2)}, u32[]{:S(2)}) collective-permute-start(f32[17,8,1024]{2,1,0:T(8,128)S(1)} %pad_maximum_fusion.1), channel_id=1, source_target_pairs={{1,0},{2,1},{3,2},{4,3},{5,4},{6,5},{7,6},{8,7},{9,8},{10,9},{11,1... | collective-permute-start | bytes 1671176 | tf_op jit(solution)/shard_map/ppermute | solution.py:363
  105.9 1.5 %copy-start.2 = (f32[17,8,1024]{2,1,0:T(8,128)}, f32[17,8,1024]{2,1,0:T(8,128)S(1)}, u32[]{:S(2)}) copy-start(f32[17,8,1024]{2,1,0:T(8,128)S(1)} %collective-permute-done.top_ref) | copy-start | bytes 1671172
  107.4 0.8 copy-start.3

commit v6 on v5

--- a/solution.py
+++ b/solution.py
@@ -104,8 +104,8 @@
 
 
 def exchange_kernel(
-    count, grid_cols, groups, anc_ref, ens_ref, alt_ref, out_ref, lines_ref,
-    held_a, held_b, outgoing_a, outgoing_b, send1, recv1, send2, recv2, send3, recv3, local,
+    count, grid_cols, groups, anc_ref, ens_ref, out_ref,
+    held_a, held_b, outgoing_a, outgoing_b, send1, recv1, send2, recv2, local,
 ):
     me = lax.axis_index("particle")
     held = (held_a, held_b)
@@ -136,18 +136,6 @@
             send_sem=send2.at[group, offset], recv_sem=recv2.at[group, me],
             device_id={"particle": peer}, device_id_type=MESH,
         )
-
-    own_lines = pltpu.make_async_copy(alt_ref, lines_ref.at[me], local.at[0])
-    own_lines.start()
-    line_copies = []
-    for offset in range(1, count):
-        peer = lax.rem(me + offset, count)
-        lines = pltpu.make_async_remote_copy(
-            src_ref=alt_ref, dst_ref=lines_ref.at[me], send_sem=send3.at[offset],
-            recv_sem=recv3.at[me], device_id={"particle": peer}, device_id_type=MESH,
-        )
-        lines.start()
-        line_copies.append(lines)
 
     own_parts = []
     firsts = []
@@ -188,14 +176,6 @@
             copies.append(copy)
         seconds.append(copies)
 
-    own_lines.wait()
-    for offset, lines in zip(range(1, count), line_copies):
-        sender = lax.rem(me + count - offset, count)
-        lines.wait_send()
-        pltpu.make_async_remote_copy(
-            src_ref=alt_ref, dst_ref=lines_ref.at[sender], send_sem=send3.at[offset],
-            recv_sem=recv3.at[sender], device_id={"particle": sender}, device_id_type=MESH,
-        ).wait_recv()
     for group, fields in enumerate(groups):
         seconds[group][0].wait()
         for offset, copy in zip(range(1, count), seconds[group][1:]):
@@ -209,7 +189,48 @@
             ).wait_recv()
 
 
-def resample(tile, ancestors, altimetry):
+def gather_kernel(count, alt_ref, lines_ref, send, recv, local):
+    me = lax.axis_index("particle")
+    barrier = pltpu.get_barrier_semaphore()
+    for offset in range(1, count):
+        peer = lax.rem(me + offset, count)
+        pl.semaphore_signal(barrier, inc=1, device_id={"particle": peer}, device_id_type=MESH)
+    pl.semaphore_wait(barrier, count - 1)
+    own = pltpu.make_async_copy(alt_ref, lines_ref.at[me], local.at[0])
+    own.start()
+    copies = []
+    for offset in range(1, count):
+        peer = lax.rem(me + offset, count)
+        copy = pltpu.make_async_remote_copy(
+            src_ref=alt_ref, dst_ref=lines_ref.at[me], send_sem=send.at[offset],
+            recv_sem=recv.at[me], device_id={"particle": peer}, device_id_type=MESH,
+        )
+        copy.start()
+        copies.append(copy)
+    own.wait()
+    for offset, copy in zip(range(1, count), copies):
+        sender = lax.rem(me + count - offset, count)
+        copy.wait_send()
+        pltpu.make_async_remote_copy(
+            src_ref=alt_ref, dst_ref=lines_ref.at[sender], send_sem=send.at[offset],
+            recv_sem=recv.at[sender], device_id={"particle": sender}, device_id_type=MESH,
+        ).wait_recv()
+
+
+def gather_lines(altimetry):
+    count = lax.axis_size("particle")
+    sems = pltpu.SemaphoreType.DMA((count,))
+    return pl.pallas_call(
+        functools.partial(gather_kernel, count),
+        out_shape=jax.ShapeDtypeStruct((count,) + altimetry.shape, altimetry.dtype),
+        in_specs=[pl.BlockSpec(memory_space=pltpu.VMEM)],
+        out_specs=pl.BlockSpec(memory_space=pltpu.VMEM),
+        scratch_shapes=[sems, sems, pltpu.SemaphoreType.DMA((1,))],
+        compiler_params=pltpu.CompilerParams(collective_id=1, has_side_effects=True),
+    )(altimetry)
+
+
+def resample(tile, ancestors):
     count = lax.axis_size("particle")
     fields, height, width = tile.shape
     grid_rows = 4
@@ -217,33 +238,25 @@
     rows, cols = height // grid_rows, width // grid_cols
     split = (fields + 1) // 2
     groups = (pl.ds(0, split), pl.ds(split, fields - split))
-    sems = pltpu.SemaphoreType.DMA((count,))
     grouped = pltpu.SemaphoreType.DMA((len(groups), count))
     return pl.pallas_call(
         functools.partial(exchange_kernel, count, grid_cols, groups),
-        out_shape=(
-            jax.ShapeDtypeStruct(tile.shape, tile.dtype),
-            jax.ShapeDtypeStruct((count,) + altimetry.shape, altimetry.dtype),
-        ),
+        out_shape=jax.ShapeDtypeStruct(tile.shape, tile.dtype),
         in_specs=[
             pl.BlockSpec(memory_space=pltpu.SMEM),
             pl.BlockSpec(memory_space=pl.ANY),
-            pl.BlockSpec(memory_space=pltpu.VMEM),
         ],
-        out_specs=(
-            pl.BlockSpec(memory_space=pl.ANY),
-            pl.BlockSpec(memory_space=pltpu.VMEM),
-        ),
+        out_specs=pl.BlockSpec(memory_space=pl.ANY),
         scratch_shapes=[
             pltpu.VMEM((count, split, rows, cols), tile.dtype),
             pltpu.VMEM((count, fields - split, rows, cols), tile.dtype),
             pltpu.VMEM((count, split, rows, cols), tile.dtype),
             pltpu.VMEM((count, fields - split, rows, cols), tile.dtype),
-            grouped, grouped, grouped, grouped, sems, sems,
+            grouped, grouped, grouped, grouped,
             pltpu.SemaphoreType.DMA((1 + 2 * len(groups),)),
         ],
         compiler_params=pltpu.CompilerParams(collective_id=0, has_side_effects=True),
-    )(ancestors, tile, altimetry)
+    )(ancestors, tile)
 
 
 def stencil_kernel(coef_ref, tile_ref, aux_ref, top_ref, bottom_ref, hit_ref, out_ref, state, aux):
@@ -337,9 +350,20 @@
 def per_device(ensemble, ancestors, depth_levels, level_coefs, altimetry, obs_rows):
     width_y = ensemble.shape[3]
     reach = 8
-    tile, gathered = resample(ensemble[0], ancestors, altimetry)
+    member = ensemble[0]
+    fields, rows = member.shape[0], member.shape[1]
+    depth = depth_levels.astype(jnp.float32)[None]
+    count = lax.axis_size("space")
+    forward = [(i, (i + 1) % count) for i in range(count)]
+    backward = [(target, source) for source, target in forward]
+    low = jnp.concatenate([member[:, :reach], depth[:, :reach]], axis=0)
+    high = jnp.concatenate([member[:, -reach:], depth[:, -reach:]], axis=0)
+    top_in = lax.ppermute(high, "space", forward)
+    bottom_in = lax.ppermute(low, "space", backward)
+    wide_lines = with_halo(altimetry, (("space", 2),), reach)
+    gathered = gather_lines(wide_lines)
     all_lines = jnp.moveaxis(gathered, 0, 1).reshape(
-        (altimetry.shape[0], -1) + altimetry.shape[2:]
+        (altimetry.shape[0], -1) + wide_lines.shape[2:]
     )
     columns = jnp.arange(width_y, dtype=jnp.int32)
     targets = []
@@ -353,16 +377,14 @@
             )
         )
         hits.append(jnp.sum(onehot, axis=0)[None, :])
-    aux = jnp.stack(targets + [depth_levels.astype(jnp.float32)], axis=0)
-    count = lax.axis_size("space")
-    forward = [(i, (i + 1) % count) for i in range(count)]
-    backward = [(target, source) for source, target in forward]
-    low = jnp.concatenate([tile[:, :reach], aux[:, :reach]], axis=0)
-    high = jnp.concatenate([tile[:, -reach:], aux[:, -reach:]], axis=0)
-    top = lax.ppermute(high, "space", forward)
-    bottom = lax.ppermute(low, "space", backward)
-    state = run_steps(level_coefs, tile, aux, top, bottom, jnp.stack(hits, axis=0))
-    return state[None]
+    targets = jnp.stack(targets, axis=0)
+    aux = jnp.concatenate([targets[:, reach : reach + rows], depth], axis=0)
+    top = jnp.concatenate([top_in[:fields], targets[:, :reach], top_in[fields:]], axis=0)
+    bottom = jnp.concatenate(
+        [bottom_in[:fields], targets[:, reach + rows :], bottom_in[fields:]], axis=0
+    )
+    result = run_steps(level_coefs, member, aux, top, bottom, jnp.stack(hits, axis=0))
+    return resample(result, ancestors)[None]
 
 
 def solution(mesh):

time: 119 us -> 141 us (1.18)
  the two profiles are of different devices: /device:TPU:24 before, /device:TPU:40 now
where the time goes in v6:
time: 141 us
  Pallas kernels  126 us (89%)
  local copies, waits for them, and re-layouts  5.82 us (4%)
  other arithmetic  4.5 us (3%)
  starting transfers between devices  3.81 us (3%)
    pallas_call x1, Pallas kernels, resample(): pl.pallas_call(functools.partial(exchange_kernel, count, grid_cols, group...  97.3 us
    pallas_call x1, Pallas kernels, gather_lines(): pl.pallas_call(functools.partial(gather_kernel, count), out_shape=jax.Sha...  19.4 us
    pallas_call x1, Pallas kernels, run_steps(): pl.pallas_call(stencil_kernel, out_shape=jax.ShapeDtypeStruct(tile.shape,...  9.16 us
    unnamed x5, local copies, waits for them, and re-layouts  2.85 us
  transfers between devices with their start and end apart: 4, of which 0 were waited for; matrix products, arithmetic and copies ran while one was open for 5% of the time, Pallas kernels for 14%

profile of v6, /device:TPU:40, one launch (start us, length us, event | category | flops | bytes accessed | tf_op | source)
XLA Modules:
  0.0 141.0 jit_solution(13038146012660958926)
XLA Ops:
  0.0 0.8 fusion.10
  0.8 0.0 collective-permute-start
  0.8 1.7 %collective-permute-start.1 = (f32[3,4,8]{2,1,0:T(4,128)S(1)}, f32[3,4,8]{2,1,0:T(4,128)S(1)}, u32[]{:S(2)}, u32[]{:S(2)}) collective-permute-start(f32[3,4,8]{2,1,0:T(4,128)S(1)} %get-tuple-element.15), channel_id=1, source_target_pairs={{1,0},{2,1},{3,2},{4,3},{5,4},{6,5},{7,6},{8,7},{9,8},{10,9},{11,1... | collective-permute-start | bytes 1160 | tf_op jit(solution)/shard_map/ppermute | solution.py:30
  2.6 0.9 convert_bitcast_fusion
  3.5 0.0 copy-start.1
  3.5 0.0 copy-start
  3.5 1.2 fusion.7
  4.8 0.1 collective-permute-start.2
  4.9 2.0 %collective-permute-start.3 = (f32[14,8,1024]{2,1,0:T(8,128)S(1)}, f32[14,8,1024]{2,1,0:T(8,128)S(1)}, u32[]{:S(2)}, u32[]{:S(2)}) collective-permute-start(f32[14,8,1024]{2,1,0:T(8,128)S(1)} %pad_maximum_fusion.7), channel_id=1, source_target_pairs={{1,0},{2,1},{3,2},{4,3},{5,4},{6,5},{7,6},{8,7},{9,8},{10,9},{11,1... | collective-permute-start | bytes 1376264 | tf_op jit(solution)/shard_map/ppermute | solution.py:362
  6.9 0.0 copy-done.1
  6.9 0.1 convert_reduce_fusion.2
  7.0 0.1 convert_reduce_fusion
  7.2 0.6 pad_maximum_fusion.8.hit_ref
  7.8 0.0 collective-permute-done
  7.8 0.0 collective-permute-done.1
  7.8 0.0 copy-done
  7.8 0.7 pad_maximum_fusion.9.alt_ref
  8.5 19.4 %shard_map.64 = f32[16,3,4,48]{3,2,1,0:T(4,128)} custom-call(f32[3,4,48]{2,1,0:T(4,128)} %pad_maximum_fusion.9.alt_ref), custom_call_target="tpu_custom_call" | custom-call | tf_op jit(solution)/shard_map/pallas_call | solution.py:223
  27.9 0.8 fusion.9
  28.7 0.3 convolution_bitcast_fusion
  29.0 0.3 convolution_bitcast_fusion.2
  29.3 0.3 convolution_bitcast_fusion.1
  29.7 0.8 pad_maximum_fusion.5.aux_ref
  30.5 0.0 collective-permute-done.2
  30.6 0.0 collective-permute-done.3
  30.7 1.1 fusion.1
  31.8 9.2 %shard_map.65.ens_ref = f32[13,32,1024]{2,1,0:T(8,128)} custom-call(f32[3,4]{1,0:T(4,128)} %coef_ref.1, f32[13,32,1024]{2,1,0:T(8,128)} %bitcast.28, f32[4,32,1024]{2,1,0:T(8,128)} %pad_maximum_fusion.5.aux_ref, f32[17,8,1024]{2,1,0:T(8,128)} %get-tuple-element.8.top_ref, f32[17,8,1024]{2,1,0:T(8,128)} %get-tuple-element.7.bottom_ref, ...), custom_call_target="tpu_custom_call" | custom-call | tf_op jit(solution)/shard_map/pallas_call | solution.py:338
  40.9 97.3 %shard_map.66 = f32[13,32,1024]{2,1,0:T(8,128)} custom-call(s32[16]{0:T(128)} %anc_ref.1, f32[13,32,1024]{2,1,0:T(8,128)} %shard_map.65.ens_ref), custom_call_target="tpu_custom_call" | custom-call | tf_op jit(solution)/shard_map/pallas_call | solution.py:242
  138.2 2.8 %copy.8 = f32[1,13,32,1024]{3,2,1,0:T(8,128)} copy(f32[1,13,32,1024]{3,2,1,0:T(8,128)} %bitcast.26) | data formatting | bytes 3407872
  (10 shorter events, 0.2 us)
Async XLA Ops:
  0.8 7.0 %collective-permute-start = (f32[3,4,8]{2,1,0:T(4,128)S(1)}, f32[3,4,8]{2,1,0:T(4,128)S(1)}, u32[]{:S(2)}, u32[]{:S(2)}) collective-permute-start(f32[3,4,8]{2,1,0:T(4,128)S(1)} %get-tuple-element.14), channel_id=1, source_target_pairs={{0,1},{1,2},{2,3},{3,4},{4,5},{5,6},{6,7},{7,8},{8,9},{9,10},{10,1... | collective-permute-start | bytes 1160 | tf_op jit(solution)/shard_map/ppermute | solution.py:27
  0.8 7.0 %collective-permute-start.1 = (f32[3,4,8]{2,1,0:T(4,128)S(1)}, f32[3,4,8]{2,1,0:T(4,128)S(1)}, u32[]{:S(2)}, u32[]{:S(2)}) collective-permute-start(f32[3,4,8]{2,1,0:T(4,128)S(1)} %get-tuple-element.15), channel_id=1, source_target_pairs={{1,0},{2,1},{3,2},{4,3},{5,4},{6,5},{7,6},{8,7},{9,8},{10,9},{11,1... | collective-permute-start | bytes 1160 | tf_op jit(solution)/shard_map/ppermute | solution.py:30
  3.5 3.4 %copy-start.1 = (s32[3,64]{1,0:T(4,128)S(1)}, s32[3,64]{1,0:T(4,128)}, u32[]{:S(2)}) copy-start(s32[3,64]{1,0:T(4,128)} %param.11) | copy-start | bytes 2308
  3.5 4.3 %copy-start = (f32[3,4,32]{2,1,0:T(4,128)S(1)}, f32[3,4,32]{2,1,0:T(4,128)}, u32[]{:S(2)}) copy-start(f32[3,4,32]{2,1,0:T(4,128)} %param.10) | copy-start | bytes 4612
  4.8 25.7 %collective-permute-start.2 = (f32[14,8,1024]{2,1,0:T(8,128)S(1)}, f32[14,8,1024]{2,1,0:T(8,128)S(1)}, u32[]{:S(2)}, u32[]{:S(2)}) collective-permute-start(f32[14,8,1024]{2,1,0:T(8,128)S(1)} %pad_maximum_fusion.6), channel_id=1, source_target_pairs={{0,1},{1,2},{2,3},{3,4},{4,5},{5,6},{6,7},{7,8},{8,9},{9,10},{10,1... | collective-permute-start | bytes 1376264 | tf_op jit(solution)/shard_map/ppermute | solution.py:361
  4.9 25.7 %collective-permute-start.3 = (f32[14,8,1024]{2,1,0:T(8,128)S(1)}, f32[14,8,1024]{2,1,0:T(8,128)S(1)}, u32[]{:S(2)}, u32[]{:S(2)}) collective-permute-start(f32[14,8,1024]{2,1,0:T(8,128)S(1)} %pad_maximum_fusion.7), channel_id=1, source_target_pairs={{1,0},{2,1},{3,2},{4,3},{5,4},{6,5},{7,6},{8,7},{9,8},{10,9},{11,1... | collective-permute-start | bytes 1376264 | tf_op jit(solution)/shard_map/ppermute | solution.py:362

commit v7 on v5

--- a/solution.py
+++ b/solution.py
@@ -104,19 +104,43 @@
 
 
 def exchange_kernel(
-    count, grid_cols, groups, anc_ref, ens_ref, alt_ref, out_ref, lines_ref,
-    held_a, held_b, outgoing_a, outgoing_b, send1, recv1, send2, recv2, send3, recv3, local,
+    count, grid_cols, groups, reach, anc_ref, ens_ref, alt_ref, depth_ref,
+    out_ref, top_ref, bottom_ref, lines_ref, depth_top_ref, depth_bottom_ref,
+    held_a, held_b, outgoing_a, outgoing_b, alt_near,
+    send1, recv1, send2, recv2, send3, recv3, edge_send, edge_recv, local,
 ):
     me = lax.axis_index("particle")
+    space = lax.axis_index("space")
+    spaces = lax.axis_size("space")
+    above = lax.rem(space + spaces - 1, spaces)
+    below = lax.rem(space + 1, spaces)
     held = (held_a, held_b)
     outgoing = (outgoing_a, outgoing_b)
     rows, cols = held_a.shape[2], held_a.shape[3]
+    height = out_ref.shape[1]
 
     barrier = pltpu.get_barrier_semaphore()
     for offset in range(1, count):
         peer = lax.rem(me + offset, count)
         pl.semaphore_signal(barrier, inc=1, device_id={"particle": peer}, device_id_type=MESH)
-    pl.semaphore_wait(barrier, count - 1)
+    for side in (above, below):
+        pl.semaphore_signal(barrier, inc=1, device_id={"space": side}, device_id_type=MESH)
+    pl.semaphore_wait(barrier, count + 1)
+
+    def neighbour_copy(src, dst, slot, side):
+        return pltpu.make_async_remote_copy(
+            src_ref=src, dst_ref=dst, send_sem=edge_send.at[slot], recv_sem=edge_recv.at[slot],
+            device_id={"space": side}, device_id_type=MESH,
+        )
+
+    early = [
+        neighbour_copy(depth_ref.at[pl.ds(0, reach)], depth_bottom_ref, 0, above),
+        neighbour_copy(depth_ref.at[pl.ds(height - reach, reach)], depth_top_ref, 1, below),
+        neighbour_copy(alt_ref, alt_near.at[1], 2, above),
+        neighbour_copy(alt_ref, alt_near.at[0], 3, below),
+    ]
+    for copy in early:
+        copy.start()
 
     def chunk_of(dest, fields):
         r, c = window(dest, grid_cols, rows, cols)
@@ -136,18 +160,6 @@
             send_sem=send2.at[group, offset], recv_sem=recv2.at[group, me],
             device_id={"particle": peer}, device_id_type=MESH,
         )
-
-    own_lines = pltpu.make_async_copy(alt_ref, lines_ref.at[me], local.at[0])
-    own_lines.start()
-    line_copies = []
-    for offset in range(1, count):
-        peer = lax.rem(me + offset, count)
-        lines = pltpu.make_async_remote_copy(
-            src_ref=alt_ref, dst_ref=lines_ref.at[me], send_sem=send3.at[offset],
-            recv_sem=recv3.at[me], device_id={"particle": peer}, device_id_type=MESH,
-        )
-        lines.start()
-        line_copies.append(lines)
 
     own_parts = []
     firsts = []
@@ -161,6 +173,24 @@
             copy.start()
             copies.append(copy)
         firsts.append(copies)
+
+    for copy in early:
+        copy.wait()
+    pieces = (alt_ref, alt_near.at[0], alt_near.at[1])
+    own_lines = []
+    line_copies = []
+    for kind, piece in enumerate(pieces):
+        own = pltpu.make_async_copy(piece, lines_ref.at[kind, me], local.at[5 + kind])
+        own.start()
+        own_lines.append(own)
+        for offset in range(1, count):
+            peer = lax.rem(me + offset, count)
+            lines = pltpu.make_async_remote_copy(
+                src_ref=piece, dst_ref=lines_ref.at[kind, me], send_sem=send3.at[kind, offset],
+                recv_sem=recv3.at[kind, me], device_id={"particle": peer}, device_id_type=MESH,
+            )
+            lines.start()
+            line_copies.append((kind, offset, piece, lines))
 
     seconds = []
     for group, fields in enumerate(groups):
@@ -188,13 +218,14 @@
             copies.append(copy)
         seconds.append(copies)
 
-    own_lines.wait()
-    for offset, lines in zip(range(1, count), line_copies):
+    for own in own_lines:
+        own.wait()
+    for kind, offset, piece, lines in line_copies:
         sender = lax.rem(me + count - offset, count)
         lines.wait_send()
         pltpu.make_async_remote_copy(
-            src_ref=alt_ref, dst_ref=lines_ref.at[sender], send_sem=send3.at[offset],
-            recv_sem=recv3.at[sender], device_id={"particle": sender}, device_id_type=MESH,
+            src_ref=piece, dst_ref=lines_ref.at[kind, sender], send_sem=send3.at[kind, offset],
+            recv_sem=recv3.at[kind, sender], device_id={"particle": sender}, device_id_type=MESH,
         ).wait_recv()
     for group, fields in enumerate(groups):
         seconds[group][0].wait()
@@ -208,8 +239,17 @@
                 device_id={"particle": sender}, device_id_type=MESH,
             ).wait_recv()
 
-
-def resample(tile, ancestors, altimetry):
+    late = [
+        neighbour_copy(out_ref.at[:, pl.ds(0, reach)], bottom_ref, 4, above),
+        neighbour_copy(out_ref.at[:, pl.ds(height - reach, reach)], top_ref, 5, below),
+    ]
+    for copy in late:
+        copy.start()
+    for copy in late:
+        copy.wait()
+
+
+def resample(tile, ancestors, altimetry, depth, reach):
     count = lax.axis_size("particle")
     fields, height, width = tile.shape
     grid_rows = 4
@@ -217,33 +257,36 @@
     rows, cols = height // grid_rows, width // grid_cols
     split = (fields + 1) // 2
     groups = (pl.ds(0, split), pl.ds(split, fields - split))
-    sems = pltpu.SemaphoreType.DMA((count,))
     grouped = pltpu.SemaphoreType.DMA((len(groups), count))
+    any_space = pl.BlockSpec(memory_space=pl.ANY)
+    vmem = pl.BlockSpec(memory_space=pltpu.VMEM)
     return pl.pallas_call(
-        functools.partial(exchange_kernel, count, grid_cols, groups),
+        functools.partial(exchange_kernel, count, grid_cols, groups, reach),
         out_shape=(
             jax.ShapeDtypeStruct(tile.shape, tile.dtype),
-            jax.ShapeDtypeStruct((count,) + altimetry.shape, altimetry.dtype),
+            jax.ShapeDtypeStruct((fields, reach, width), tile.dtype),
+            jax.ShapeDtypeStruct((fields, reach, width), tile.dtype),
+            jax.ShapeDtypeStruct((3, count) + altimetry.shape, altimetry.dtype),
+            jax.ShapeDtypeStruct((reach, width), depth.dtype),
+            jax.ShapeDtypeStruct((reach, width), depth.dtype),
         ),
-        in_specs=[
-            pl.BlockSpec(memory_space=pltpu.SMEM),
-            pl.BlockSpec(memory_space=pl.ANY),
-            pl.BlockSpec(memory_space=pltpu.VMEM),
-        ],
-        out_specs=(
-            pl.BlockSpec(memory_space=pl.ANY),
-            pl.BlockSpec(memory_space=pltpu.VMEM),
-        ),
+        in_specs=[pl.BlockSpec(memory_space=pltpu.SMEM), any_space, vmem, any_space],
+        out_specs=(any_space, any_space, any_space, vmem, any_space, any_space),
         scratch_shapes=[
             pltpu.VMEM((count, split, rows, cols), tile.dtype),
             pltpu.VMEM((count, fields - split, rows, cols), tile.dtype),
             pltpu.VMEM((count, split, rows, cols), tile.dtype),
             pltpu.VMEM((count, fields - split, rows, cols), tile.dtype),
-            grouped, grouped, grouped, grouped, sems, sems,
-            pltpu.SemaphoreType.DMA((1 + 2 * len(groups),)),
+            pltpu.VMEM((2,) + altimetry.shape, altimetry.dtype),
+            grouped, grouped, grouped, grouped,
+            pltpu.SemaphoreType.DMA((3, count)),
+            pltpu.SemaphoreType.DMA((3, count)),
+            pltpu.SemaphoreType.DMA((6,)),
+            pltpu.SemaphoreType.DMA((6,)),
+            pltpu.SemaphoreType.DMA((8,)),
         ],
         compiler_params=pltpu.CompilerParams(collective_id=0, has_side_effects=True),
-    )(ancestors, tile, altimetry)
+    )(ancestors, tile, altimetry, depth)
 
 
 def stencil_kernel(coef_ref, tile_ref, aux_ref, top_ref, bottom_ref, hit_ref, out_ref, state, aux):
@@ -337,9 +380,17 @@
 def per_device(ensemble, ancestors, depth_levels, level_coefs, altimetry, obs_rows):
     width_y = ensemble.shape[3]
     reach = 8
-    tile, gathered = resample(ensemble[0], ancestors, altimetry)
-    all_lines = jnp.moveaxis(gathered, 0, 1).reshape(
-        (altimetry.shape[0], -1) + altimetry.shape[2:]
+    depth = depth_levels.astype(jnp.float32)
+    tile, top, bottom, gathered, depth_top, depth_bottom = resample(
+        ensemble[0], ancestors, altimetry, depth, reach
+    )
+    fields, rows = tile.shape[0], tile.shape[1]
+    own_lines, from_above, from_below = (
+        jnp.moveaxis(piece, 0, 1).reshape((altimetry.shape[0], -1) + altimetry.shape[2:])
+        for piece in gathered
+    )
+    all_lines = jnp.concatenate(
+        [from_above[..., -reach:], own_lines, from_below[..., :reach]], axis=-1
     )
     columns = jnp.arange(width_y, dtype=jnp.int32)
     targets = []
@@ -353,14 +404,10 @@
             )
         )
         hits.append(jnp.sum(onehot, axis=0)[None, :])
-    aux = jnp.stack(targets + [depth_levels.astype(jnp.float32)], axis=0)
-    count = lax.axis_size("space")
-    forward = [(i, (i + 1) % count) for i in range(count)]
-    backward = [(target, source) for source, target in forward]
-    low = jnp.concatenate([tile[:, :reach], aux[:, :reach]], axis=0)
-    high = jnp.concatenate([tile[:, -reach:], aux[:, -reach:]], axis=0)
-    top = lax.ppermute(high, "space", forward)
-    bottom = lax.ppermute(low, "space", backward)
+    targets = jnp.stack(targets, axis=0)
+    aux = jnp.concatenate([targets[:, reach : reach + rows], depth[None]], axis=0)
+    top = jnp.concatenate([top, targets[:, :reach], depth_top[None]], axis=0)
+    bottom = jnp.concatenate([bottom, targets[:, reach + rows :], depth_bottom[None]], axis=0)
     state = run_steps(level_coefs, tile, aux, top, bottom, jnp.stack(hits, axis=0))
     return state[None]
 

time: 119 us -> 125 us (1.050)
  Pallas kernels: 96.5 us -> 117 us
  waiting for transfers between devices: 9.91 us -> 0 us
  starting transfers between devices: 4.91 us -> 0 us
  other arithmetic: 1.87 us -> 4.55 us
    pallas_call x1, Pallas kernels: 87.4 us -> 108 us  [resample(): pl.pallas_call(functools.partial(exchange_kernel, count, grid_cols, group...]
    ppermute x2 -> x0, waiting for transfers between devices: 9.91 us -> none  [the longest x1 8.42 us: per_device(): top = lax.ppermute(high, 'space', forward)]
    ppermute x2 -> x0, starting transfers between devices: 4.91 us -> none  [the longest x1 4.83 us: per_device(): bottom = lax.ppermute(low, 'space', backward)]
    concatenate x2 -> x3, other arithmetic: 0.08 us -> 2.09 us  [the longest x1 1.13 us: per_device(): jnp.concatenate([bottom, targets[:, reach + rows:], depth_bottom[None]],...]
    broadcast_in_dim x0 -> x1, other arithmetic: none -> 1.58 us  [per_device(): aux = jnp.concatenate([targets[:, reach:reach + rows], depth[None]], axis=0)]
    unnamed x8, local copies, waits for them, and re-layouts: 1.35 us -> 0.02 us
  transfers between devices with their start and end apart: 2 -> 0, of which waited for: 2 -> 0; matrix products, arithmetic and copies ran while one was open for 1% -> 0% of each run, Pallas kernels for 0% -> 0%
where the time goes in v7:
time: 125 us
  Pallas kernels  117 us (94%)
  other arithmetic  4.55 us (4%)
  local copies, waits for them, and re-layouts  2.07 us (2%)
    pallas_call x1, Pallas kernels, resample(): pl.pallas_call(functools.partial(exchange_kernel, count, grid_cols, group...  108 us
    pallas_call x1, Pallas kernels, run_steps(): pl.pallas_call(stencil_kernel, out_shape=jax.ShapeDtypeStruct(tile.shape,...  9.16 us

profile of v7, /device:TPU:24, one launch (start us, length us, event | category | flops | bytes accessed | tf_op | source)
XLA Modules:
  0.0 124.6 jit_solution(15236707441295454650)
XLA Ops:
  0.0 0.8 slice_bitcast_fusion.11
  0.8 0.1 convert_reduce_fusion.2
  0.9 0.1 convert_reduce_fusion
  1.0 0.6 pad_maximum_fusion.7.hit_ref
  1.7 1.6 %convert_bitcast_fusion = (f32[1,32,1024]{2,1,0:T(8,128)S(1)}, f32[32,1024]{1,0:T(8,128)}) fusion(s32[32,1024]{1,0:T(8,128)} %param.8), kind=kLoop, calls=%fused_computation.33 | loop fusion | flops 32768 | bytes 393216 | tf_op jit(solution)/shard_map/broadcast_in_dim | solution.py:408
  3.2 107.7 %shard_map.64 = (f32[13,32,1024]{2,1,0:T(8,128)}, f32[13,8,1024]{2,1,0:T(8,128)}, f32[13,8,1024]{2,1,0:T(8,128)}, f32[3,16,3,4,32]{4,3,2,1,0:T(4,128)}, f32[8,1024]{1,0:T(8,128)}, /*index=5*/f32[8,1024]{1,0:T(8,128)}) custom-call(s32[16]{0:T(128)} %anc_ref.1, f32[13,32,1024]{2,1,0:T(8,128)} %bitcast.46, f32[3,4,32]{2,1,0:T(4,128)} %alt_ref.1, ...), custom_call_target="tpu_custom_call" | custom-call | tf_op jit(solution)/shard_map/pallas_call | solution.py:263
  110.9 0.0 copy-start
  110.9 0.0 copy-start.1
  111.0 0.0 copy-start.2
  111.0 0.0 copy-start.3
  111.0 1.1 slice_bitcast_fusion.2
  112.1 0.1 slice.44
  112.2 0.1 pad_maximum_fusion.6
  112.4 0.3 convolution_bitcast_fusion
  112.7 0.3 convolution_bitcast_fusion.1
  113.0 0.3 convolution_bitcast_fusion.2
  113.3 0.0 copy-done
  113.3 0.0 copy-done.1
  113.3 0.0 copy-done.2
  113.4 0.0 copy-done.3
  113.4 1.1 fusion.1
  114.6 0.8 pad_maximum_fusion.5.aux_ref
  115.4 9.2 %shard_map.65 = f32[13,32,1024]{2,1,0:T(8,128)} custom-call(f32[3,4]{1,0:T(4,128)} %coef_ref.1, f32[13,32,1024]{2,1,0:T(8,128)} %get-tuple-element.11.tile_ref, f32[4,32,1024]{2,1,0:T(8,128)} %pad_maximum_fusion.5.aux_ref, f32[17,8,1024]{2,1,0:T(8,128)} %get-tuple-element.18.top_ref, f32[17,8,1024]{2,1,0:T(8,128)} %get-tuple-element.17.bottom_ref, ...), custom_call_target="tpu_custom_call" | custom-call | tf_op jit(solution)/shard_map/pallas_call | solution.py:368
  (5 shorter events, 0.1 us)
Async XLA Ops:
  110.9 2.4 %copy-start = (f32[13,8,1024]{2,1,0:T(8,128)S(1)}, f32[13,8,1024]{2,1,0:T(8,128)}, u32[]{:S(2)}) copy-start(f32[13,8,1024]{2,1,0:T(8,128)} %get-tuple-element.13) | copy-start | bytes 1277956
  110.9 2.4 %copy-start.1 = (f32[13,8,1024]{2,1,0:T(8,128)S(1)}, f32[13,8,1024]{2,1,0:T(8,128)}, u32[]{:S(2)}) copy-start(f32[13,8,1024]{2,1,0:T(8,128)} %get-tuple-element.15) | copy-start | bytes 1277956
  111.0 2.4 %copy-start.2 = (f32[8,1024]{1,0:T(8,128)S(1)}, f32[8,1024]{1,0:T(8,128)}, u32[]{:S(2)}) copy-start(f32[8,1024]{1,0:T(8,128)} %get-tuple-element.14) | copy-start | bytes 98308
  111.0 2.4 %copy-start.3 = (f32[8,1024]{1,0:T(8,128)S(1)}, f32[8,1024]{1,0:T(8,128)}, u32[]{:S(2)}) copy-start(f32[8,1024]{1,0:T(8,128)} %get-tuple-element.16) | copy-start | bytes 98308

commit v8 on v7

--- a/solution.py
+++ b/solution.py
@@ -227,6 +227,7 @@
             src_ref=piece, dst_ref=lines_ref.at[kind, sender], send_sem=send3.at[kind, offset],
             recv_sem=recv3.at[kind, sender], device_id={"particle": sender}, device_id_type=MESH,
         ).wait_recv()
+    late = []
     for group, fields in enumerate(groups):
         seconds[group][0].wait()
         for offset, copy in zip(range(1, count), seconds[group][1:]):
@@ -238,13 +239,18 @@
                 send_sem=send2.at[group, offset], recv_sem=recv2.at[group, sender],
                 device_id={"particle": sender}, device_id_type=MESH,
             ).wait_recv()
-
-    late = [
-        neighbour_copy(out_ref.at[:, pl.ds(0, reach)], bottom_ref, 4, above),
-        neighbour_copy(out_ref.at[:, pl.ds(height - reach, reach)], top_ref, 5, below),
-    ]
-    for copy in late:
-        copy.start()
+        edges = [
+            neighbour_copy(
+                out_ref.at[fields, pl.ds(0, reach)], bottom_ref.at[fields], 4 + 2 * group, above
+            ),
+            neighbour_copy(
+                out_ref.at[fields, pl.ds(height - reach, reach)], top_ref.at[fields],
+                5 + 2 * group, below,
+            ),
+        ]
+        for copy in edges:
+            copy.start()
+        late.extend(edges)
     for copy in late:
         copy.wait()
 
@@ -281,8 +287,8 @@
             grouped, grouped, grouped, grouped,
             pltpu.SemaphoreType.DMA((3, count)),
             pltpu.SemaphoreType.DMA((3, count)),
-            pltpu.SemaphoreType.DMA((6,)),
-            pltpu.SemaphoreType.DMA((6,)),
+            pltpu.SemaphoreType.DMA((4 + 2 * len(groups),)),
+            pltpu.SemaphoreType.DMA((4 + 2 * len(groups),)),
             pltpu.SemaphoreType.DMA((8,)),
         ],
         compiler_params=pltpu.CompilerParams(collective_id=0, has_side_effects=True),

time: 125 us -> 123 us (0.984); the launches traced: 125 us -> 121 us
  Pallas kernels: 117 us -> 114 us
    pallas_call x1, Pallas kernels: 108 us -> 104 us  [resample(): pl.pallas_call(functools.partial(exchange_kernel, count, grid_cols, group...]
where the time goes in v8:
time: 123 us; the launch traced here: 121 us
  Pallas kernels  114 us (93%)
  other arithmetic  4.55 us (4%)
  local copies, waits for them, and re-layouts  2.07 us (2%)
    pallas_call x1, Pallas kernels, resample(): pl.pallas_call(functools.partial(exchange_kernel, count, grid_cols, group...  104 us
    pallas_call x1, Pallas kernels, run_steps(): pl.pallas_call(stencil_kernel, out_shape=jax.ShapeDtypeStruct(tile.shape,...  9.16 us

profile of v8, /device:TPU:24, one launch (start us, length us, event | category | flops | bytes accessed | tf_op | source)
XLA Modules:
  0.0 121.2 jit_solution(2508115226781769978)
XLA Ops:
  0.0 0.8 slice_bitcast_fusion.11
  0.8 0.1 convert_reduce_fusion.2
  0.9 0.1 convert_reduce_fusion
  1.0 0.6 pad_maximum_fusion.7.hit_ref
  1.7 1.6 %convert_bitcast_fusion = (f32[1,32,1024]{2,1,0:T(8,128)S(1)}, f32[32,1024]{1,0:T(8,128)}) fusion(s32[32,1024]{1,0:T(8,128)} %param.8), kind=kLoop, calls=%fused_computation.33 | loop fusion | flops 32768 | bytes 393216 | tf_op jit(solution)/shard_map/broadcast_in_dim | solution.py:414
  3.2 104.4 %shard_map.64 = (f32[13,32,1024]{2,1,0:T(8,128)}, f32[13,8,1024]{2,1,0:T(8,128)}, f32[13,8,1024]{2,1,0:T(8,128)}, f32[3,16,3,4,32]{4,3,2,1,0:T(4,128)}, f32[8,1024]{1,0:T(8,128)}, /*index=5*/f32[8,1024]{1,0:T(8,128)}) custom-call(s32[16]{0:T(128)} %anc_ref.1, f32[13,32,1024]{2,1,0:T(8,128)} %bitcast.46, f32[3,4,32]{2,1,0:T(4,128)} %alt_ref.1, ...), custom_call_target="tpu_custom_call" | custom-call | tf_op jit(solution)/shard_map/pallas_call | solution.py:269
  107.6 0.0 copy-start
  107.6 0.0 copy-start.1
  107.6 0.0 copy-start.2
  107.6 0.0 copy-start.3
  107.6 1.1 slice_bitcast_fusion.2
  108.7 0.1 slice.44
  108.9 0.1 pad_maximum_fusion.6
  109.0 0.3 convolution_bitcast_fusion
  109.3 0.3 convolution_bitcast_fusion.1
  109.7 0.3 convolution_bitcast_fusion.2
  110.0 0.0 copy-done
  110.0 0.0 copy-done.1
  110.0 0.0 copy-done.2
  110.0 0.0 copy-done.3
  110.0 1.1 fusion.1
  111.2 0.8 pad_maximum_fusion.5.aux_ref
  112.1 9.2 %shard_map.65 = f32[13,32,1024]{2,1,0:T(8,128)} custom-call(f32[3,4]{1,0:T(4,128)} %coef_ref.1, f32[13,32,1024]{2,1,0:T(8,128)} %get-tuple-element.11.tile_ref, f32[4,32,1024]{2,1,0:T(8,128)} %pad_maximum_fusion.5.aux_ref, f32[17,8,1024]{2,1,0:T(8,128)} %get-tuple-element.18.top_ref, f32[17,8,1024]{2,1,0:T(8,128)} %get-tuple-element.17.bottom_ref, ...), custom_call_target="tpu_custom_call" | custom-call | tf_op jit(solution)/shard_map/pallas_call | solution.py:374
  (5 shorter events, 0.1 us)
Async XLA Ops:
  107.6 2.4 %copy-start = (f32[13,8,1024]{2,1,0:T(8,128)S(1)}, f32[13,8,1024]{2,1,0:T(8,128)}, u32[]{:S(2)}) copy-start(f32[13,8,1024]{2,1,0:T(8,128)} %get-tuple-element.13) | copy-start | bytes 1277956
  107.6 2.4 %copy-start.1 = (f32[13,8,1024]{2,1,0:T(8,128)S(1)}, f32[13,8,1024]{2,1,0:T(8,128)}, u32[]{:S(2)}) copy-start(f32[13,8,1024]{2,1,0:T(8,128)} %get-tuple-element.15) | copy-start | bytes 1277956
  107.6 2.4 %copy-start.2 = (f32[8,1024]{1,0:T(8,128)S(1)}, f32[8,1024]{1,0:T(8,128)}, u32[]{:S(2)}) copy-start(f32[8,1024]{1,0:T(8,128)} %get-tuple-element.14) | copy-start | bytes 98308
  107.6 2.4 %copy-start.3 = (f32[8,1024]{1,0:T(8,128)S(1)}, f32[8,1024]{1,0:T(8,128)}, u32[]{:S(2)}) copy-start(f32[8,1024]{1,0:T(8,128)} %get-tuple-element.16) | copy-start | bytes 98308

commit v9 on v5

--- a/solution.py
+++ b/solution.py
@@ -104,13 +104,13 @@
 
 
 def exchange_kernel(
-    count, grid_cols, groups, anc_ref, ens_ref, alt_ref, out_ref, lines_ref,
-    held_a, held_b, outgoing_a, outgoing_b, send1, recv1, send2, recv2, send3, recv3, local,
+    count, grid_cols, groups, anc_ref, ens_ref, alt_ref, out_ref, lines_ref, *scratch,
 ):
     me = lax.axis_index("particle")
-    held = (held_a, held_b)
-    outgoing = (outgoing_a, outgoing_b)
-    rows, cols = held_a.shape[2], held_a.shape[3]
+    held = scratch[: len(groups)]
+    outgoing = scratch[len(groups) : 2 * len(groups)]
+    send1, recv1, send2, recv2, send3, recv3, local = scratch[2 * len(groups) :]
+    rows, cols = held[0].shape[2], held[0].shape[3]
 
     barrier = pltpu.get_barrier_semaphore()
     for offset in range(1, count):
@@ -178,7 +178,7 @@
             outgoing[group][member] = held[group][source]
         r_me, c_me = window(me, grid_cols, rows, cols)
         mine = pltpu.make_async_copy(
-            outgoing[group].at[me], out_ref.at[fields, r_me, c_me], local.at[3 + group]
+            outgoing[group].at[me], out_ref.at[fields, r_me, c_me], local.at[1 + len(groups) + group]
         )
         mine.start()
         copies = [mine]
@@ -215,8 +215,11 @@
     grid_rows = 4
     grid_cols = count // grid_rows
     rows, cols = height // grid_rows, width // grid_cols
-    split = (fields + 1) // 2
-    groups = (pl.ds(0, split), pl.ds(split, fields - split))
+    parts = 4
+    sizes = [fields // parts + (1 if g < fields % parts else 0) for g in range(parts)]
+    starts = [sum(sizes[:g]) for g in range(parts)]
+    groups = tuple(pl.ds(start, size) for start, size in zip(starts, sizes))
+    buffers = [pltpu.VMEM((count, size, rows, cols), tile.dtype) for size in sizes]
     sems = pltpu.SemaphoreType.DMA((count,))
     grouped = pltpu.SemaphoreType.DMA((len(groups), count))
     return pl.pallas_call(
@@ -235,10 +238,8 @@
             pl.BlockSpec(memory_space=pltpu.VMEM),
         ),
         scratch_shapes=[
-            pltpu.VMEM((count, split, rows, cols), tile.dtype),
-            pltpu.VMEM((count, fields - split, rows, cols), tile.dtype),
-            pltpu.VMEM((count, split, rows, cols), tile.dtype),
-            pltpu.VMEM((count, fields - split, rows, cols), tile.dtype),
+            *buffers,
+            *buffers,
             grouped, grouped, grouped, grouped, sems, sems,
             pltpu.SemaphoreType.DMA((1 + 2 * len(groups),)),
         ],

time: 119 us -> 121 us (1.017)
  the two profiles are of different devices: /device:TPU:24 before, /device:TPU:64 now
where the time goes in v9:
time: 121 us; the launch traced here: 120 us
  Pallas kernels  98.3 us (81%)
  waiting for transfers between devices  11.8 us (10%)
  local copies, waits for them, and re-layouts  3.95 us (3%)
  starting transfers between devices  3.49 us (3%)
  other arithmetic  1.87 us (2%)
    pallas_call x1, Pallas kernels, resample(): pl.pallas_call(functools.partial(exchange_kernel, count, grid_cols, group...  89.1 us
    ppermute x1, waiting for transfers between devices, per_device(): top = lax.ppermute(high, 'space', forward)  11.8 us
    pallas_call x1, Pallas kernels, run_steps(): pl.pallas_call(stencil_kernel, out_shape=jax.ShapeDtypeStruct(tile.shape,...  9.16 us
    ppermute x1, starting transfers between devices, per_device(): bottom = lax.ppermute(low, 'space', backward)  3.4 us
  transfers between devices with their start and end apart: 2, of which 1 were waited for; matrix products, arithmetic and copies ran while one was open for 1% of the time, Pallas kernels for 0%

profile of v9, /device:TPU:64, one launch (start us, length us, event | category | flops | bytes accessed | tf_op | source)
XLA Modules:
  0.0 120.3 jit_solution(15582626997830588856)
XLA Ops:
  0.0 0.8 slice_bitcast_fusion.2
  0.8 0.9 convert_bitcast_fusion
  1.7 89.1 %shard_map.64 = (f32[13,32,1024]{2,1,0:T(8,128)}, f32[16,3,4,32]{3,2,1,0:T(4,128)}) custom-call(s32[16]{0:T(128)} %anc_ref.1, f32[13,32,1024]{2,1,0:T(8,128)} %bitcast.26, f32[3,4,32]{2,1,0:T(4,128)} %alt_ref.1), custom_call_target="tpu_custom_call" | custom-call | tf_op jit(solution)/shard_map/pallas_call | solution.py:225
  90.9 0.0 copy-start
  90.9 0.9 fusion.5
  91.8 0.3 convolution_bitcast_fusion
  92.1 0.3 convolution_bitcast_fusion.2
  92.4 0.3 convolution_bitcast_fusion.1
  92.7 0.0 copy-start.1
  92.7 0.0 copy-done
  92.8 0.1 fusion.3
  92.9 0.1 collective-permute-start
  93.0 0.5 copy-done.1
  93.5 3.4 %collective-permute-start.1 = (f32[17,8,1024]{2,1,0:T(8,128)S(1)}, f32[17,8,1024]{2,1,0:T(8,128)S(1)}, u32[]{:S(2)}, u32[]{:S(2)}) collective-permute-start(f32[17,8,1024]{2,1,0:T(8,128)S(1)} %pad_maximum_fusion.1), channel_id=1, source_target_pairs={{1,0},{2,1},{3,2},{4,3},{5,4},{6,5},{7,6},{8,7},{9,8},{10,9},{11,1... | collective-permute-start | bytes 1671176 | tf_op jit(solution)/shard_map/ppermute | solution.py:364
  96.9 0.1 convert_reduce_fusion.2
  97.0 0.1 convert_reduce_fusion
  97.2 0.6 pad_maximum_fusion.3.hit_ref
  97.8 11.8 %collective-permute-done.top_ref = f32[17,8,1024]{2,1,0:T(8,128)S(1)} collective-permute-done((f32[17,8,1024]{2,1,0:T(8,128)S(1)}, f32[17,8,1024]{2,1,0:T(8,128)S(1)}, u32[]{:S(2)}, u32[]{:S(2)}) %collective-permute-start) | collective-permute-done | bytes 557088 | tf_op jit(solution)/shard_map/ppermute | solution.py:363
  109.5 0.0 copy-start.2
  109.5 0.0 collective-permute-done.1.bottom_ref
  109.5 0.8 copy-done.2
  110.4 0.0 copy-start.3
  110.4 0.8 copy-done.3
  111.2 9.2 %shard_map.65 = f32[13,32,1024]{2,1,0:T(8,128)} custom-call(f32[3,4]{1,0:T(4,128)} %coef_ref.1, f32[13,32,1024]{2,1,0:T(8,128)} %get-tuple-element.7.tile_ref, f32[4,32,1024]{2,1,0:T(8,128)} %copy-done.1, f32[17,8,1024]{2,1,0:T(8,128)} %copy-done.2, f32[17,8,1024]{2,1,0:T(8,128)} %copy-done.3, f32[3,1,1024]{2,1,0:T(1,128)} %pad_maximum_fusion.3.hit_ref), custom_call_target="tpu_custom_call" | custom-call | tf_op jit(solution)/shard_map/pallas_call | solution.py:326
  (4 shorter events, 0.1 us)
Async XLA Ops:
  90.9 1.9 %copy-start = (f32[13,32,1024]{2,1,0:T(8,128)S(1)}, f32[13,32,1024]{2,1,0:T(8,128)}, u32[]{:S(2)}) copy-start(f32[13,32,1024]{2,1,0:T(8,128)} %get-tuple-element.7.tile_ref) | copy-start | bytes 5111812
  92.7 0.8 copy-start.1
  92.9 16.7 %collective-permute-start = (f32[17,8,1024]{2,1,0:T(8,128)S(1)}, f32[17,8,1024]{2,1,0:T(8,128)S(1)}, u32[]{:S(2)}, u32[]{:S(2)}) collective-permute-start(f32[17,8,1024]{2,1,0:T(8,128)S(1)} %pad_maximum_fusion), channel_id=1, source_target_pairs={{0,1},{1,2},{2,3},{3,4},{4,5},{5,6},{6,7},{7,8},{8,9},{9,10},{10,1... | collective-permute-start | bytes 1671176 | tf_op jit(solution)/shard_map/ppermute | solution.py:363
  93.5 16.0 %collective-permute-start.1 = (f32[17,8,1024]{2,1,0:T(8,128)S(1)}, f32[17,8,1024]{2,1,0:T(8,128)S(1)}, u32[]{:S(2)}, u32[]{:S(2)}) collective-permute-start(f32[17,8,1024]{2,1,0:T(8,128)S(1)} %pad_maximum_fusion.1), channel_id=1, source_target_pairs={{1,0},{2,1},{3,2},{4,3},{5,4},{6,5},{7,6},{8,7},{9,8},{10,9},{11,1... | collective-permute-start | bytes 1671176 | tf_op jit(solution)/shard_map/ppermute | solution.py:364
  109.5 0.8 copy-start.2
  110.4 0.8 copy-start.3

commit v10 on v5

--- a/solution.py
+++ b/solution.py
@@ -246,18 +246,39 @@
     )(ancestors, tile, altimetry)
 
 
-def stencil_kernel(coef_ref, tile_ref, aux_ref, top_ref, bottom_ref, hit_ref, out_ref, state, aux):
+def stencil_kernel(coef_ref, tile_ref, aux_ref, hit_ref, out_ref, state, aux, send, recv):
     fields, rows, width = tile_ref.shape
     extra = aux_ref.shape[0]
-    reach = top_ref.shape[1]
     levels = coef_ref.shape[1]
     span = state.shape[1]
-    state[:, :reach] = top_ref[:fields]
+    reach = (span - rows) // 2
+    space = lax.axis_index("space")
+    spaces = lax.axis_size("space")
+    above = lax.rem(space + spaces - 1, spaces)
+    below = lax.rem(space + 1, spaces)
+
+    barrier = pltpu.get_barrier_semaphore()
+    for side in (above, below):
+        pl.semaphore_signal(barrier, inc=1, device_id={"space": side}, device_id_type=MESH)
+    pl.semaphore_wait(barrier, 2)
+
+    edges = []
+    for slot, (source, target) in enumerate(((tile_ref, state), (aux_ref, aux))):
+        for turn, (side, start, land) in enumerate(
+            ((above, 0, reach + rows), (below, rows - reach, 0))
+        ):
+            copy = pltpu.make_async_remote_copy(
+                src_ref=source.at[:, pl.ds(start, reach)],
+                dst_ref=target.at[:, pl.ds(land, reach)],
+                send_sem=send.at[2 * slot + turn], recv_sem=recv.at[2 * slot + turn],
+                device_id={"space": side}, device_id_type=MESH,
+            )
+            copy.start()
+            edges.append(copy)
     state[:, reach : reach + rows] = tile_ref[...]
-    state[:, reach + rows :] = bottom_ref[:fields]
-    aux[:, :reach] = top_ref[fields:]
     aux[:, reach : reach + rows] = aux_ref[...]
-    aux[:, reach + rows :] = bottom_ref[fields:]
+    for copy in edges:
+        copy.wait()
 
     lane = lax.broadcasted_iota(jnp.int32, (span, width), 1)
     first_lane = lane == 0
@@ -318,20 +339,24 @@
     out_ref[...] = state[:, reach : reach + rows]
 
 
-def run_steps(coefs, tile, aux, top, bottom, hits):
+def run_steps(coefs, tile, aux, hits, reach):
     fields, rows, width = tile.shape
-    span = rows + 2 * top.shape[1]
+    span = rows + 2 * reach
     vmem = pl.BlockSpec(memory_space=pltpu.VMEM)
+    edge_sems = pltpu.SemaphoreType.DMA((4,))
     return pl.pallas_call(
         stencil_kernel,
         out_shape=jax.ShapeDtypeStruct(tile.shape, tile.dtype),
-        in_specs=[pl.BlockSpec(memory_space=pltpu.SMEM)] + [vmem] * 5,
+        in_specs=[pl.BlockSpec(memory_space=pltpu.SMEM)] + [vmem] * 3,
         out_specs=vmem,
         scratch_shapes=[
             pltpu.VMEM((fields, span, width), tile.dtype),
             pltpu.VMEM((aux.shape[0], span, width), tile.dtype),
+            edge_sems,
+            edge_sems,
         ],
-    )(coefs, tile, aux, top, bottom, hits)
+        compiler_params=pltpu.CompilerParams(collective_id=1, has_side_effects=True),
+    )(coefs, tile, aux, hits)
 
 
 def per_device(ensemble, ancestors, depth_levels, level_coefs, altimetry, obs_rows):
@@ -354,14 +379,7 @@
         )
         hits.append(jnp.sum(onehot, axis=0)[None, :])
     aux = jnp.stack(targets + [depth_levels.astype(jnp.float32)], axis=0)
-    count = lax.axis_size("space")
-    forward = [(i, (i + 1) % count) for i in range(count)]
-    backward = [(target, source) for source, target in forward]
-    low = jnp.concatenate([tile[:, :reach], aux[:, :reach]], axis=0)
-    high = jnp.concatenate([tile[:, -reach:], aux[:, -reach:]], axis=0)
-    top = lax.ppermute(high, "space", forward)
-    bottom = lax.ppermute(low, "space", backward)
-    state = run_steps(level_coefs, tile, aux, top, bottom, jnp.stack(hits, axis=0))
+    state = run_steps(level_coefs, tile, aux, jnp.stack(hits, axis=0), reach)
     return state[None]
 
 

time: 119 us -> 124 us (1.042); the launches traced: 117 us -> 124 us
  Pallas kernels: 96.5 us -> 116 us
  waiting for transfers between devices: 9.91 us -> 0 us
  starting transfers between devices: 4.91 us -> 0 us
  local copies, waits for them, and re-layouts: 3.14 us -> 4.44 us
    pallas_call x1, Pallas kernels: 9.16 us -> 28.5 us  [run_steps(): pl.pallas_call(stencil_kernel, out_shape=jax.ShapeDtypeStruct(tile.shape,...]
    ppermute x2 -> x0, waiting for transfers between devices: 9.91 us -> none  [the longest x1 8.42 us: per_device(): top = lax.ppermute(high, 'space', forward)]
    ppermute x2 -> x0, starting transfers between devices: 4.91 us -> none  [the longest x1 4.83 us: per_device(): bottom = lax.ppermute(low, 'space', backward)]
    unnamed x8 -> x1, local copies, waits for them, and re-layouts: 1.35 us -> 2.84 us
  transfers between devices with their start and end apart: 2 -> 0, of which waited for: 2 -> 0; matrix products, arithmetic and copies ran while one was open for 1% -> 0% of each run, Pallas kernels for 0% -> 0%
where the time goes in v10:
time: 124 us
  Pallas kernels  116 us (94%)
  local copies, waits for them, and re-layouts  4.44 us (4%)
  other arithmetic  2.59 us (2%)
    pallas_call x1, Pallas kernels, resample(): pl.pallas_call(functools.partial(exchange_kernel, count, grid_cols, group...  87.4 us
    pallas_call x1, Pallas kernels, run_steps(): pl.pallas_call(stencil_kernel, out_shape=jax.ShapeDtypeStruct(tile.shape,...  28.5 us
    unnamed x1, local copies, waits for them, and re-layouts  2.84 us

profile of v10, /device:TPU:24, one launch (start us, length us, event | category | flops | bytes accessed | tf_op | source)
XLA Modules:
  0.0 123.9 jit_solution(8265590669826705245)
XLA Ops:
  0.0 0.8 slice_bitcast_fusion.2
  0.8 0.1 convert_reduce_fusion.2
  0.9 0.1 convert_reduce_fusion
  1.0 0.6 pad_maximum_fusion.1.hit_ref
  1.6 0.9 convert_bitcast_fusion
  2.6 87.4 %shard_map.64 = (f32[13,32,1024]{2,1,0:T(8,128)}, f32[16,3,4,32]{3,2,1,0:T(4,128)}) custom-call(s32[16]{0:T(128)} %anc_ref.1, f32[13,32,1024]{2,1,0:T(8,128)} %bitcast.27, f32[3,4,32]{2,1,0:T(4,128)} %alt_ref.1), custom_call_target="tpu_custom_call" | custom-call | tf_op jit(solution)/shard_map/pallas_call | solution.py:222
  89.9 0.8 fusion.3
  90.7 0.3 convolution_bitcast_fusion
  91.0 0.3 convolution_bitcast_fusion.2
  91.3 0.3 convolution_bitcast_fusion.1
  91.6 0.8 pad_maximum_fusion.aux_ref
  92.5 28.5 %shard_map.65 = f32[13,32,1024]{2,1,0:T(8,128)} custom-call(f32[3,4]{1,0:T(4,128)} %coef_ref.1, f32[13,32,1024]{2,1,0:T(8,128)} %get-tuple-element.7.tile_ref, f32[4,32,1024]{2,1,0:T(8,128)} %pad_maximum_fusion.aux_ref, f32[3,1,1024]{2,1,0:T(1,128)} %pad_maximum_fusion.1.hit_ref), custom_call_target="tpu_custom_call" | custom-call | tf_op jit(solution)/shard_map/pallas_call | solution.py:347
  121.0 2.8 %copy.8 = f32[1,13,32,1024]{3,2,1,0:T(8,128)} copy(f32[1,13,32,1024]{3,2,1,0:T(8,128)} %bitcast.26) | data formatting | bytes 3407872

commit v11 on v5

--- a/solution.py
+++ b/solution.py
@@ -286,9 +286,13 @@
         state[field] = state[field] * masks[field % levels]
     for step in range(STEPS):
         spread = None
+        shifted = []
         for k in range(levels):
-            ddx_u = parts(state[k])[0]
-            ddy_v = parts(state[levels + k])[1]
+            east_vel = state[k]
+            north_vel = state[levels + k]
+            ddx_u, unused_y, lap_u = parts(east_vel)
+            unused_x, ddy_v, lap_v = parts(north_vel)
+            shifted.append((east_vel, north_vel, lap_u, lap_v))
             term = (coef_ref[0, k] * masks[k]) * (ddx_u + ddy_v)
             spread = term if spread is None else spread + term
         height = state[3 * levels]
@@ -299,11 +303,8 @@
         for k in range(levels):
             visc = 0.2 * coef_ref[1, k]
             kappa = 0.2 * coef_ref[2, k]
-            east_vel = state[k]
-            north_vel = state[levels + k]
+            east_vel, north_vel, lap_u, lap_v = shifted[k]
             temper = state[2 * levels + k]
-            unused_x, unused_y, lap_u = parts(east_vel)
-            unused_x, unused_y, lap_v = parts(north_vel)
             ddx_t, ddy_t, lap_t = parts(temper)
             state[k] = masks[k] * (
                 east_vel + DT * (CORIOLIS * north_vel - grad_x + visc * lap_u)

time: 119 us -> 119 us (level)
  no operation moved by 1% of the time
where the time goes in v11:
time: 119 us; the launch traced here: 117 us
  Pallas kernels  96.5 us (81%)
  waiting for transfers between devices  9.91 us (8%)
  starting transfers between devices  4.91 us (4%)
  local copies, waits for them, and re-layouts  3.14 us (3%)
  other arithmetic  1.87 us (2%)
    pallas_call x1, Pallas kernels, resample(): pl.pallas_call(functools.partial(exchange_kernel, count, grid_cols, group...  87.4 us
    pallas_call x1, Pallas kernels, run_steps(): pl.pallas_call(stencil_kernel, out_shape=jax.ShapeDtypeStruct(tile.shape,...  9.13 us
    ppermute x1, waiting for transfers between devices, per_device(): top = lax.ppermute(high, 'space', forward)  8.42 us
    ppermute x1, starting transfers between devices, per_device(): bottom = lax.ppermute(low, 'space', backward)  4.83 us
  transfers between devices with their start and end apart: 2, of which 2 were waited for; matrix products, arithmetic and copies ran while one was open for 1% of the time, Pallas kernels for 0%

profile of v11, /device:TPU:24, one launch (start us, length us, event | category | flops | bytes accessed | tf_op | source)
XLA Modules:
  0.0 117.3 jit_solution(2454588272839136320)
XLA Ops:
  0.0 0.8 slice_bitcast_fusion.2
  0.8 0.9 convert_bitcast_fusion
  1.7 87.4 %shard_map.64 = (f32[13,32,1024]{2,1,0:T(8,128)}, f32[16,3,4,32]{3,2,1,0:T(4,128)}) custom-call(s32[16]{0:T(128)} %anc_ref.1, f32[13,32,1024]{2,1,0:T(8,128)} %bitcast.26, f32[3,4,32]{2,1,0:T(4,128)} %alt_ref.1), custom_call_target="tpu_custom_call" | custom-call | tf_op jit(solution)/shard_map/pallas_call | solution.py:222
  89.1 0.0 copy-start
  89.1 0.9 fusion.5
  90.0 0.3 convolution_bitcast_fusion
  90.3 0.3 convolution_bitcast_fusion.2
  90.6 0.3 convolution_bitcast_fusion.1
  91.0 0.0 copy-start.1
  91.0 0.0 copy-done
  91.0 0.1 fusion.3
  91.1 0.1 collective-permute-start
  91.3 0.5 copy-done.1
  91.8 4.8 %collective-permute-start.1 = (f32[17,8,1024]{2,1,0:T(8,128)S(1)}, f32[17,8,1024]{2,1,0:T(8,128)S(1)}, u32[]{:S(2)}, u32[]{:S(2)}) collective-permute-start(f32[17,8,1024]{2,1,0:T(8,128)S(1)} %pad_maximum_fusion.1), channel_id=1, source_target_pairs={{1,0},{2,1},{3,2},{4,3},{5,4},{6,5},{7,6},{8,7},{9,8},{10,9},{11,1... | collective-permute-start | bytes 1671176 | tf_op jit(solution)/shard_map/ppermute | solution.py:364
  96.6 0.1 convert_reduce_fusion.2
  96.7 0.1 convert_reduce_fusion
  96.9 0.6 pad_maximum_fusion.3.hit_ref
  97.5 8.4 %collective-permute-done.top_ref = f32[17,8,1024]{2,1,0:T(8,128)S(1)} collective-permute-done((f32[17,8,1024]{2,1,0:T(8,128)S(1)}, f32[17,8,1024]{2,1,0:T(8,128)S(1)}, u32[]{:S(2)}, u32[]{:S(2)}) %collective-permute-start) | collective-permute-done | bytes 557088 | tf_op jit(solution)/shard_map/ppermute | solution.py:363
  105.9 0.0 copy-start.2
  105.9 1.5 %collective-permute-done.1.bottom_ref = f32[17,8,1024]{2,1,0:T(8,128)S(1)} collective-permute-done((f32[17,8,1024]{2,1,0:T(8,128)S(1)}, f32[17,8,1024]{2,1,0:T(8,128)S(1)}, u32[]{:S(2)}, u32[]{:S(2)}) %collective-permute-start.1) | collective-permute-done | bytes 557088 | tf_op jit(solution)/shard_map/ppermute | solution.py:364
  107.4 0.0 copy-done.2
  107.4 0.0 copy-start.3
  107.4 0.8 copy-done.3
  108.2 9.1 %shard_map.65 = f32[13,32,1024]{2,1,0:T(8,128)} custom-call(f32[3,4]{1,0:T(4,128)} %coef_ref.1, f32[13,32,1024]{2,1,0:T(8,128)} %get-tuple-element.7.tile_ref, f32[4,32,1024]{2,1,0:T(8,128)} %copy-done.1, f32[17,8,1024]{2,1,0:T(8,128)} %copy-done.2, f32[17,8,1024]{2,1,0:T(8,128)} %copy-done.3, f32[3,1,1024]{2,1,0:T(1,128)} %pad_maximum_fusion.3.hit_ref), custom_call_target="tpu_custom_call" | custom-call | tf_op jit(solution)/shard_map/pallas_call | solution.py:326
  (4 shorter events, 0.1 us)
Async XLA Ops:
  89.1 1.9 %copy-start = (f32[13,32,1024]{2,1,0:T(8,128)S(1)}, f32[13,32,1024]{2,1,0:T(8,128)}, u32[]{:S(2)}) copy-start(f32[13,32,1024]{2,1,0:T(8,128)} %get-tuple-element.7.tile_ref) | copy-start | bytes 5111812
  91.0 0.8 copy-start.1
  91.1 14.8 %collective-permute-start = (f32[17,8,1024]{2,1,0:T(8,128)S(1)}, f32[17,8,1024]{2,1,0:T(8,128)S(1)}, u32[]{:S(2)}, u32[]{:S(2)}) collective-permute-start(f32[17,8,1024]{2,1,0:T(8,128)S(1)} %pad_maximum_fusion), channel_id=1, source_target_pairs={{0,1},{1,2},{2,3},{3,4},{4,5},{5,6},{6,7},{7,8},{8,9},{9,10},{10,1... | collective-permute-start | bytes 1671176 | tf_op jit(solution)/shard_map/ppermute | solution.py:363
  91.8 15.6 %collective-permute-start.1 = (f32[17,8,1024]{2,1,0:T(8,128)S(1)}, f32[17,8,1024]{2,1,0:T(8,128)S(1)}, u32[]{:S(2)}, u32[]{:S(2)}) collective-permute-start(f32[17,8,1024]{2,1,0:T(8,128)S(1)} %pad_maximum_fusion.1), channel_id=1, source_target_pairs={{1,0},{2,1},{3,2},{4,3},{5,4},{6,5},{7,6},{8,7},{9,8},{10,9},{11,1... | collective-permute-start | bytes 1671176 | tf_op jit(solution)/shard_map/ppermute | solution.py:364
  105.9 1.5 %copy-start.2 = (f32[17,8,1024]{2,1,0:T(8,128)}, f32[17,8,1024]{2,1,0:T(8,128)S(1)}, u32[]{:S(2)}) copy-start(f32[17,8,1024]{2,1,0:T(8,128)S(1)} %collective-permute-done.top_ref) | copy-start | bytes 1671172
  107.4 0.8 copy-start.3

commit v12 on v11

--- a/solution.py
+++ b/solution.py
@@ -249,15 +249,20 @@
 def stencil_kernel(coef_ref, tile_ref, aux_ref, top_ref, bottom_ref, hit_ref, out_ref, state, aux):
     fields, rows, width = tile_ref.shape
     extra = aux_ref.shape[0]
-    reach = top_ref.shape[1]
     levels = coef_ref.shape[1]
     span = state.shape[1]
-    state[:, :reach] = top_ref[:fields]
+    reach = (span - rows) // 2
+    sent = top_ref.shape[1]
+    spare = reach - sent
+    for target in (state, aux):
+        target[:, :spare] = jnp.zeros((target.shape[0], spare, width), jnp.float32)
+        target[:, span - spare :] = jnp.zeros((target.shape[0], spare, width), jnp.float32)
+    state[:, spare:reach] = top_ref[:fields]
     state[:, reach : reach + rows] = tile_ref[...]
-    state[:, reach + rows :] = bottom_ref[:fields]
-    aux[:, :reach] = top_ref[fields:]
+    state[:, reach + rows : reach + rows + sent] = bottom_ref[:fields]
+    aux[:, spare:reach] = top_ref[fields:]
     aux[:, reach : reach + rows] = aux_ref[...]
-    aux[:, reach + rows :] = bottom_ref[fields:]
+    aux[:, reach + rows : reach + rows + sent] = bottom_ref[fields:]
 
     lane = lax.broadcasted_iota(jnp.int32, (span, width), 1)
     first_lane = lane == 0
@@ -319,9 +324,9 @@
     out_ref[...] = state[:, reach : reach + rows]
 
 
-def run_steps(coefs, tile, aux, top, bottom, hits):
+def run_steps(coefs, tile, aux, top, bottom, hits, reach):
     fields, rows, width = tile.shape
-    span = rows + 2 * top.shape[1]
+    span = rows + 2 * reach
     vmem = pl.BlockSpec(memory_space=pltpu.VMEM)
     return pl.pallas_call(
         stencil_kernel,
@@ -358,11 +363,12 @@
     count = lax.axis_size("space")
     forward = [(i, (i + 1) % count) for i in range(count)]
     backward = [(target, source) for source, target in forward]
-    low = jnp.concatenate([tile[:, :reach], aux[:, :reach]], axis=0)
-    high = jnp.concatenate([tile[:, -reach:], aux[:, -reach:]], axis=0)
+    sent = 2 * STEPS
+    low = jnp.concatenate([tile[:, :sent], aux[:, :sent]], axis=0)
+    high = jnp.concatenate([tile[:, -sent:], aux[:, -sent:]], axis=0)
     top = lax.ppermute(high, "space", forward)
     bottom = lax.ppermute(low, "space", backward)
-    state = run_steps(level_coefs, tile, aux, top, bottom, jnp.stack(hits, axis=0))
+    state = run_steps(level_coefs, tile, aux, top, bottom, jnp.stack(hits, axis=0), reach)
     return state[None]
 
 

time: 119 us -> 120 us (level)
  no operation moved by 1% of the time
where the time goes in v12:
time: 120 us; the launch traced here: 118 us
  Pallas kernels  97.2 us (81%)
  waiting for transfers between devices  9.93 us (8%)
  starting transfers between devices  4.91 us (4%)
  local copies, waits for them, and re-layouts  3.11 us (3%)
  other arithmetic  1.9 us (2%)
    pallas_call x1, Pallas kernels, resample(): pl.pallas_call(functools.partial(exchange_kernel, count, grid_cols, group...  87.4 us
    pallas_call x1, Pallas kernels, run_steps(): pl.pallas_call(stencil_kernel, out_shape=jax.ShapeDtypeStruct(tile.shape,...  9.81 us
    ppermute x1, waiting for transfers between devices, per_device(): top = lax.ppermute(high, 'space', forward)  8.43 us
    ppermute x1, starting transfers between devices, per_device(): bottom = lax.ppermute(low, 'space', backward)  4.83 us
  transfers between devices with their start and end apart: 2, of which 2 were waited for; matrix products, arithmetic and copies ran while one was open for 1% of the time, Pallas kernels for 0%

profile of v12, /device:TPU:24, one launch (start us, length us, event | category | flops | bytes accessed | tf_op | source)
XLA Modules:
  0.0 118.0 jit_solution(8752589201467500610)
XLA Ops:
  0.0 0.8 slice_bitcast_fusion.2
  0.8 0.9 convert_bitcast_fusion
  1.7 87.4 %shard_map.64 = (f32[13,32,1024]{2,1,0:T(8,128)}, f32[16,3,4,32]{3,2,1,0:T(4,128)}) custom-call(s32[16]{0:T(128)} %anc_ref.1, f32[13,32,1024]{2,1,0:T(8,128)} %bitcast.26, f32[3,4,32]{2,1,0:T(4,128)} %alt_ref.1), custom_call_target="tpu_custom_call" | custom-call | tf_op jit(solution)/shard_map/pallas_call | solution.py:222
  89.1 0.0 copy-start
  89.1 0.9 fusion.5
  90.0 0.3 convolution_bitcast_fusion
  90.3 0.3 convolution_bitcast_fusion.2
  90.6 0.3 convolution_bitcast_fusion.1
  91.0 0.0 copy-start.1
  91.0 0.0 copy-done
  91.0 0.1 fusion.3
  91.1 0.1 pad_maximum_fusion
  91.1 0.1 collective-permute-start
  91.2 0.1 pad_maximum_fusion.1
  91.3 0.5 copy-done.1
  91.8 4.8 %collective-permute-start.1 = (f32[17,6,1024]{2,1,0:T(8,128)S(1)}, f32[17,6,1024]{2,1,0:T(8,128)S(1)}, u32[]{:S(2)}, u32[]{:S(2)}) collective-permute-start(f32[17,6,1024]{2,1,0:T(8,128)S(1)} %pad_maximum_fusion.1), channel_id=1, source_target_pairs={{1,0},{2,1},{3,2},{4,3},{5,4},{6,5},{7,6},{8,7},{9,8},{10,9},{11,1... | collective-permute-start | bytes 1253384 | tf_op jit(solution)/shard_map/ppermute | solution.py:370
  96.6 0.1 convert_reduce_fusion.2
  96.7 0.1 convert_reduce_fusion
  96.9 0.6 pad_maximum_fusion.3.hit_ref
  97.5 8.4 %collective-permute-done.top_ref = f32[17,6,1024]{2,1,0:T(8,128)S(1)} collective-permute-done((f32[17,6,1024]{2,1,0:T(8,128)S(1)}, f32[17,6,1024]{2,1,0:T(8,128)S(1)}, u32[]{:S(2)}, u32[]{:S(2)}) %collective-permute-start) | collective-permute-done | bytes 417824 | tf_op jit(solution)/shard_map/ppermute | solution.py:369
  105.9 0.0 copy-start.2
  105.9 1.5 %collective-permute-done.1.bottom_ref = f32[17,6,1024]{2,1,0:T(8,128)S(1)} collective-permute-done((f32[17,6,1024]{2,1,0:T(8,128)S(1)}, f32[17,6,1024]{2,1,0:T(8,128)S(1)}, u32[]{:S(2)}, u32[]{:S(2)}) %collective-permute-start.1) | collective-permute-done | bytes 417824 | tf_op jit(solution)/shard_map/ppermute | solution.py:370
  107.4 0.0 copy-done.2
  107.4 0.0 copy-start.3
  107.4 0.8 copy-done.3
  108.2 9.8 %shard_map.65 = f32[13,32,1024]{2,1,0:T(8,128)} custom-call(f32[3,4]{1,0:T(4,128)} %coef_ref.1, f32[13,32,1024]{2,1,0:T(8,128)} %get-tuple-element.7.tile_ref, f32[4,32,1024]{2,1,0:T(8,128)} %copy-done.1, f32[17,6,1024]{2,1,0:T(8,128)} %copy-done.2, f32[17,6,1024]{2,1,0:T(8,128)} %copy-done.3, f32[3,1,1024]{2,1,0:T(1,128)} %pad_maximum_fusion.3.hit_ref), custom_call_target="tpu_custom_call" | custom-call | tf_op jit(solution)/shard_map/pallas_call | solution.py:331
  (2 shorter events, 0.1 us)
Async XLA Ops:
  89.1 1.9 %copy-start = (f32[13,32,1024]{2,1,0:T(8,128)S(1)}, f32[13,32,1024]{2,1,0:T(8,128)}, u32[]{:S(2)}) copy-start(f32[13,32,1024]{2,1,0:T(8,128)} %get-tuple-element.7.tile_ref) | copy-start | bytes 5111812
  91.0 0.8 copy-start.1
  91.1 14.7 %collective-permute-start = (f32[17,6,1024]{2,1,0:T(8,128)S(1)}, f32[17,6,1024]{2,1,0:T(8,128)S(1)}, u32[]{:S(2)}, u32[]{:S(2)}) collective-permute-start(f32[17,6,1024]{2,1,0:T(8,128)S(1)} %pad_maximum_fusion), channel_id=1, source_target_pairs={{0,1},{1,2},{2,3},{3,4},{4,5},{5,6},{6,7},{7,8},{8,9},{9,10},{10,1... | collective-permute-start | bytes 1253384 | tf_op jit(solution)/shard_map/ppermute | solution.py:369
  91.8 15.6 %collective-permute-start.1 = (f32[17,6,1024]{2,1,0:T(8,128)S(1)}, f32[17,6,1024]{2,1,0:T(8,128)S(1)}, u32[]{:S(2)}, u32[]{:S(2)}) collective-permute-start(f32[17,6,1024]{2,1,0:T(8,128)S(1)} %pad_maximum_fusion.1), channel_id=1, source_target_pairs={{1,0},{2,1},{3,2},{4,3},{5,4},{6,5},{7,6},{8,7},{9,8},{10,9},{11,1... | collective-permute-start | bytes 1253384 | tf_op jit(solution)/shard_map/ppermute | solution.py:370
  105.9 1.5 %copy-start.2 = (f32[17,6,1024]{2,1,0:T(8,128)}, f32[17,6,1024]{2,1,0:T(8,128)S(1)}, u32[]{:S(2)}) copy-start(f32[17,6,1024]{2,1,0:T(8,128)S(1)} %collective-permute-done.top_ref) | copy-start | bytes 1253380
  107.4 0.8 copy-start.3

commit v13 on v5

--- a/solution.py
+++ b/solution.py
@@ -118,6 +118,19 @@
         pl.semaphore_signal(barrier, inc=1, device_id={"particle": peer}, device_id_type=MESH)
     pl.semaphore_wait(barrier, count - 1)
 
+    side = 4
+    routes = sorted(
+        ((dz, dy) for dz in range(count // side) for dy in range(side) if dz or dy),
+        key=lambda pair: -(2 * min(pair[0], count // side - pair[0]) + min(pair[1], side - pair[1])),
+    )
+
+    def peer_at(route, sign):
+        dz, dy = route
+        zs = count // side
+        z = lax.rem(me // side + zs + sign * dz, zs)
+        y = lax.rem(me % side + side + sign * dy, side)
+        return z * side + y
+
     def chunk_of(dest, fields):
         r, c = window(dest, grid_cols, rows, cols)
         return ens_ref.at[fields, r, c]
@@ -156,8 +169,8 @@
         own.start()
         own_parts.append(own)
         copies = []
-        for offset in range(1, count):
-            copy = first_copy(group, fields, offset, lax.rem(me + offset, count))
+        for offset, route in enumerate(routes, start=1):
+            copy = first_copy(group, fields, offset, peer_at(route, 1))
             copy.start()
             copies.append(copy)
         firsts.append(copies)
@@ -165,8 +178,8 @@
     seconds = []
     for group, fields in enumerate(groups):
         own_parts[group].wait()
-        for offset, copy in zip(range(1, count), firsts[group]):
-            sender = lax.rem(me + count - offset, count)
+        for offset, route, copy in zip(range(1, count), routes, firsts[group]):
+            sender = peer_at(route, -1)
             copy.wait_send()
             pltpu.make_async_remote_copy(
                 src_ref=chunk_of(me, fields), dst_ref=held[group].at[sender],
@@ -182,8 +195,8 @@
         )
         mine.start()
         copies = [mine]
-        for offset in range(1, count):
-            copy = second_copy(group, fields, offset, lax.rem(me + offset, count))
+        for offset, route in enumerate(routes, start=1):
+            copy = second_copy(group, fields, offset, peer_at(route, 1))
             copy.start()
             copies.append(copy)
         seconds.append(copies)
@@ -198,8 +211,8 @@
         ).wait_recv()
     for group, fields in enumerate(groups):
         seconds[group][0].wait()
-        for offset, copy in zip(range(1, count), seconds[group][1:]):
-            sender = lax.rem(me + count - offset, count)
+        for offset, route, copy in zip(range(1, count), routes, seconds[group][1:]):
+            sender = peer_at(route, -1)
             r_s, c_s = window(sender, grid_cols, rows, cols)
             copy.wait_send()
             pltpu.make_async_remote_copy(

time: 119 us -> 120 us (level)
  starting transfers between devices: 4.91 us -> 3.49 us
    ppermute x1, waiting for transfers between devices: 8.42 us -> 10.3 us  [per_device(): top = lax.ppermute(high, 'space', forward)]
    ppermute x1, waiting for transfers between devices: 1.49 us -> 0.01 us  [per_device(): bottom = lax.ppermute(low, 'space', backward)]
    ppermute x1, starting transfers between devices: 4.83 us -> 3.4 us  [per_device(): bottom = lax.ppermute(low, 'space', backward)]
  transfers between devices with their start and end apart: 2 -> 2, of which waited for: 2 -> 1; matrix products, arithmetic and copies ran while one was open for 1% -> 1% of each run, Pallas kernels for 0% -> 0%
where the time goes in v13:
time: 120 us; the launch traced here: 118 us
  Pallas kernels  97.3 us (81%)
  waiting for transfers between devices  10.3 us (9%)
  local copies, waits for them, and re-layouts  3.95 us (3%)
  starting transfers between devices  3.49 us (3%)
  other arithmetic  1.87 us (2%)
    pallas_call x1, Pallas kernels, resample(): pl.pallas_call(functools.partial(exchange_kernel, count, grid_cols, group...  88.2 us
    ppermute x1, waiting for transfers between devices, per_device(): top = lax.ppermute(high, 'space', forward)  10.3 us
    pallas_call x1, Pallas kernels, run_steps(): pl.pallas_call(stencil_kernel, out_shape=jax.ShapeDtypeStruct(tile.shape,...  9.16 us
    ppermute x1, starting transfers between devices, per_device(): bottom = lax.ppermute(low, 'space', backward)  3.4 us
  transfers between devices with their start and end apart: 2, of which 1 were waited for; matrix products, arithmetic and copies ran while one was open for 1% of the time, Pallas kernels for 0%

profile of v13, /device:TPU:24, one launch (start us, length us, event | category | flops | bytes accessed | tf_op | source)
XLA Modules:
  0.0 117.9 jit_solution(14439740236253924046)
XLA Ops:
  0.0 0.8 slice_bitcast_fusion.2
  0.8 0.9 convert_bitcast_fusion
  1.7 88.2 %shard_map.64 = (f32[13,32,1024]{2,1,0:T(8,128)}, f32[16,3,4,32]{3,2,1,0:T(4,128)}) custom-call(s32[16]{0:T(128)} %anc_ref.1, f32[13,32,1024]{2,1,0:T(8,128)} %bitcast.26, f32[3,4,32]{2,1,0:T(4,128)} %alt_ref.1), custom_call_target="tpu_custom_call" | custom-call | tf_op jit(solution)/shard_map/pallas_call | solution.py:235
  89.9 0.0 copy-start
  89.9 0.9 fusion.5
  90.8 0.3 convolution_bitcast_fusion
  91.1 0.3 convolution_bitcast_fusion.2
  91.4 0.3 convolution_bitcast_fusion.1
  91.8 0.0 copy-start.1
  91.8 0.0 copy-done
  91.8 0.1 fusion.3
  91.9 0.1 collective-permute-start
  92.0 0.5 copy-done.1
  92.6 3.4 %collective-permute-start.1 = (f32[17,8,1024]{2,1,0:T(8,128)S(1)}, f32[17,8,1024]{2,1,0:T(8,128)S(1)}, u32[]{:S(2)}, u32[]{:S(2)}) collective-permute-start(f32[17,8,1024]{2,1,0:T(8,128)S(1)} %pad_maximum_fusion.1), channel_id=1, source_target_pairs={{1,0},{2,1},{3,2},{4,3},{5,4},{6,5},{7,6},{8,7},{9,8},{10,9},{11,1... | collective-permute-start | bytes 1671176 | tf_op jit(solution)/shard_map/ppermute | solution.py:376
  96.0 0.1 convert_reduce_fusion.2
  96.1 0.1 convert_reduce_fusion
  96.2 0.6 pad_maximum_fusion.3.hit_ref
  96.8 10.3 %collective-permute-done.top_ref = f32[17,8,1024]{2,1,0:T(8,128)S(1)} collective-permute-done((f32[17,8,1024]{2,1,0:T(8,128)S(1)}, f32[17,8,1024]{2,1,0:T(8,128)S(1)}, u32[]{:S(2)}, u32[]{:S(2)}) %collective-permute-start) | collective-permute-done | bytes 557088 | tf_op jit(solution)/shard_map/ppermute | solution.py:375
  107.1 0.0 copy-start.2
  107.1 0.0 collective-permute-done.1.bottom_ref
  107.1 0.8 copy-done.2
  107.9 0.0 copy-start.3
  107.9 0.8 copy-done.3
  108.8 9.2 %shard_map.65 = f32[13,32,1024]{2,1,0:T(8,128)} custom-call(f32[3,4]{1,0:T(4,128)} %coef_ref.1, f32[13,32,1024]{2,1,0:T(8,128)} %get-tuple-element.7.tile_ref, f32[4,32,1024]{2,1,0:T(8,128)} %copy-done.1, f32[17,8,1024]{2,1,0:T(8,128)} %copy-done.2, f32[17,8,1024]{2,1,0:T(8,128)} %copy-done.3, f32[3,1,1024]{2,1,0:T(1,128)} %pad_maximum_fusion.3.hit_ref), custom_call_target="tpu_custom_call" | custom-call | tf_op jit(solution)/shard_map/pallas_call | solution.py:338
  (4 shorter events, 0.1 us)
Async XLA Ops:
  89.9 1.9 %copy-start = (f32[13,32,1024]{2,1,0:T(8,128)S(1)}, f32[13,32,1024]{2,1,0:T(8,128)}, u32[]{:S(2)}) copy-start(f32[13,32,1024]{2,1,0:T(8,128)} %get-tuple-element.7.tile_ref) | copy-start | bytes 5111812
  91.8 0.8 copy-start.1
  91.9 15.2 %collective-permute-start = (f32[17,8,1024]{2,1,0:T(8,128)S(1)}, f32[17,8,1024]{2,1,0:T(8,128)S(1)}, u32[]{:S(2)}, u32[]{:S(2)}) collective-permute-start(f32[17,8,1024]{2,1,0:T(8,128)S(1)} %pad_maximum_fusion), channel_id=1, source_target_pairs={{0,1},{1,2},{2,3},{3,4},{4,5},{5,6},{6,7},{7,8},{8,9},{9,10},{10,1... | collective-permute-start | bytes 1671176 | tf_op jit(solution)/shard_map/ppermute | solution.py:375
  92.6 14.6 %collective-permute-start.1 = (f32[17,8,1024]{2,1,0:T(8,128)S(1)}, f32[17,8,1024]{2,1,0:T(8,128)S(1)}, u32[]{:S(2)}, u32[]{:S(2)}) collective-permute-start(f32[17,8,1024]{2,1,0:T(8,128)S(1)} %pad_maximum_fusion.1), channel_id=1, source_target_pairs={{1,0},{2,1},{3,2},{4,3},{5,4},{6,5},{7,6},{8,7},{9,8},{10,9},{11,1... | collective-permute-start | bytes 1671176 | tf_op jit(solution)/shard_map/ppermute | solution.py:376
  107.1 0.8 copy-start.2
  107.9 0.8 copy-start.3

commit v14 on v5

--- a/solution.py
+++ b/solution.py
@@ -246,18 +246,21 @@
     )(ancestors, tile, altimetry)
 
 
-def stencil_kernel(coef_ref, tile_ref, aux_ref, top_ref, bottom_ref, hit_ref, out_ref, state, aux):
+def stencil_kernel(
+    coef_ref, tile_ref, aux_ref, top_ref, bottom_ref, top_aux_ref, bottom_aux_ref, hit_ref,
+    out_ref, state, aux,
+):
     fields, rows, width = tile_ref.shape
     extra = aux_ref.shape[0]
     reach = top_ref.shape[1]
     levels = coef_ref.shape[1]
     span = state.shape[1]
-    state[:, :reach] = top_ref[:fields]
+    state[:, :reach] = top_ref[...]
     state[:, reach : reach + rows] = tile_ref[...]
-    state[:, reach + rows :] = bottom_ref[:fields]
-    aux[:, :reach] = top_ref[fields:]
+    state[:, reach + rows :] = bottom_ref[...]
+    aux[:, :reach] = top_aux_ref[...]
     aux[:, reach : reach + rows] = aux_ref[...]
-    aux[:, reach + rows :] = bottom_ref[fields:]
+    aux[:, reach + rows :] = bottom_aux_ref[...]
 
     lane = lax.broadcasted_iota(jnp.int32, (span, width), 1)
     first_lane = lane == 0
@@ -318,26 +321,31 @@
     out_ref[...] = state[:, reach : reach + rows]
 
 
-def run_steps(coefs, tile, aux, top, bottom, hits):
+def run_steps(coefs, tile, aux, top, bottom, top_aux, bottom_aux, hits):
     fields, rows, width = tile.shape
     span = rows + 2 * top.shape[1]
     vmem = pl.BlockSpec(memory_space=pltpu.VMEM)
     return pl.pallas_call(
         stencil_kernel,
         out_shape=jax.ShapeDtypeStruct(tile.shape, tile.dtype),
-        in_specs=[pl.BlockSpec(memory_space=pltpu.SMEM)] + [vmem] * 5,
+        in_specs=[pl.BlockSpec(memory_space=pltpu.SMEM)] + [vmem] * 7,
         out_specs=vmem,
         scratch_shapes=[
             pltpu.VMEM((fields, span, width), tile.dtype),
             pltpu.VMEM((aux.shape[0], span, width), tile.dtype),
         ],
-    )(coefs, tile, aux, top, bottom, hits)
+    )(coefs, tile, aux, top, bottom, top_aux, bottom_aux, hits)
 
 
 def per_device(ensemble, ancestors, depth_levels, level_coefs, altimetry, obs_rows):
     width_y = ensemble.shape[3]
     reach = 8
     tile, gathered = resample(ensemble[0], ancestors, altimetry)
+    count = lax.axis_size("space")
+    forward = [(i, (i + 1) % count) for i in range(count)]
+    backward = [(target, source) for source, target in forward]
+    top = lax.ppermute(tile[:, -reach:], "space", forward)
+    bottom = lax.ppermute(tile[:, :reach], "space", backward)
     all_lines = jnp.moveaxis(gathered, 0, 1).reshape(
         (altimetry.shape[0], -1) + altimetry.shape[2:]
     )
@@ -354,14 +362,11 @@
         )
         hits.append(jnp.sum(onehot, axis=0)[None, :])
     aux = jnp.stack(targets + [depth_levels.astype(jnp.float32)], axis=0)
-    count = lax.axis_size("space")
-    forward = [(i, (i + 1) % count) for i in range(count)]
-    backward = [(target, source) for source, target in forward]
-    low = jnp.concatenate([tile[:, :reach], aux[:, :reach]], axis=0)
-    high = jnp.concatenate([tile[:, -reach:], aux[:, -reach:]], axis=0)
-    top = lax.ppermute(high, "space", forward)
-    bottom = lax.ppermute(low, "space", backward)
-    state = run_steps(level_coefs, tile, aux, top, bottom, jnp.stack(hits, axis=0))
+    top_aux = lax.ppermute(aux[:, -reach:], "space", forward)
+    bottom_aux = lax.ppermute(aux[:, :reach], "space", backward)
+    state = run_steps(
+        level_coefs, tile, aux, top, bottom, top_aux, bottom_aux, jnp.stack(hits, axis=0)
+    )
     return state[None]
 
 

time: 119 us -> 119 us (level); the launches traced: 117 us -> 119 us
  starting transfers between devices: 4.91 us -> 8.83 us
    ppermute x2 -> x4, starting transfers between devices: 4.91 us -> 8.83 us  [the longest x1 4.9 us: per_device(): bottom = lax.ppermute(tile[:, :reach], 'space', backward)]
    ppermute x2 -> x4, waiting for transfers between devices: 9.91 us -> 8.76 us  [the longest x1 5.62 us: per_device(): bottom_aux = lax.ppermute(aux[:, :reach], 'space', backward)]
  transfers between devices with their start and end apart: 2 -> 4, of which waited for: 2 -> 2; matrix products, arithmetic and copies ran while one was open for 1% -> 2% of each run, Pallas kernels for 0% -> 0%
where the time goes in v14:
time: 119 us
  Pallas kernels  96.5 us (81%)
  starting transfers between devices  8.83 us (7%)
  waiting for transfers between devices  8.76 us (7%)
  local copies, waits for them, and re-layouts  2.85 us (2%)
    pallas_call x1, Pallas kernels, resample(): pl.pallas_call(functools.partial(exchange_kernel, count, grid_cols, group...  87.3 us
    pallas_call x1, Pallas kernels, run_steps(): pl.pallas_call(stencil_kernel, out_shape=jax.ShapeDtypeStruct(tile.shape,...  9.14 us
    ppermute x1, waiting for transfers between devices, per_device(): bottom_aux = lax.ppermute(aux[:, :reach], 'space', backward)  5.62 us
    ppermute x1, starting transfers between devices, per_device(): bottom = lax.ppermute(tile[:, :reach], 'space', backward)  4.9 us
    ppermute x1, starting transfers between devices, per_device(): bottom_aux = lax.ppermute(aux[:, :reach], 'space', backward)  3.92 us
    ppermute x1, waiting for transfers between devices, per_device(): top_aux = lax.ppermute(aux[:, -reach:], 'space', forward)  3.14 us
  transfers between devices with their start and end apart: 4, of which 2 were waited for; matrix products, arithmetic and copies ran while one was open for 2% of the time, Pallas kernels for 0%

profile of v14, /device:TPU:24, one launch (start us, length us, event | category | flops | bytes accessed | tf_op | source)
XLA Modules:
  0.0 118.8 jit_solution(6639898146919504932)
XLA Ops:
  0.0 0.0 copy-start.7
  0.0 0.0 copy-start.5
  0.0 87.3 %shard_map.64 = (f32[13,32,1024]{2,1,0:T(8,128)}, f32[16,3,4,32]{3,2,1,0:T(4,128)}) custom-call(s32[16]{0:T(128)} %anc_ref.1, f32[13,32,1024]{2,1,0:T(8,128)} %bitcast.26, f32[3,4,32]{2,1,0:T(4,128)} %alt_ref.1), custom_call_target="tpu_custom_call" | custom-call | tf_op jit(solution)/shard_map/pallas_call | solution.py:222
  87.3 0.0 copy-start.6
  87.3 1.2 %fusion.3 = (f32[13,8,1024]{2,1,0:T(8,128)S(1)}, f32[13,8,1024]{2,1,0:T(8,128)S(1)}) fusion(f32[13,32,1024]{2,1,0:T(8,128)} %get-tuple-element.7.tile_ref), kind=kLoop, calls=%fused_computation.18 | loop fusion | bytes 1703936 | tf_op jit(solution)/shard_map/slice | solution.py:348
  88.6 4.9 %collective-permute-start.1 = (f32[13,8,1024]{2,1,0:T(8,128)S(1)}, f32[13,8,1024]{2,1,0:T(8,128)S(1)}, u32[]{:S(2)}, u32[]{:S(2)}) collective-permute-start(f32[13,8,1024]{2,1,0:T(8,128)S(1)} %get-tuple-element.9), channel_id=1, source_target_pairs={{1,0},{2,1},{3,2},{4,3},{5,4},{6,5},{7,6},{8,7},{9,8},{10,9},{11,1... | collective-permute-start | bytes 1277960 | tf_op jit(solution)/shard_map/ppermute | solution.py:348
  93.5 0.0 collective-permute-start
  93.5 0.0 copy-done.7
  93.5 0.0 copy-done.5
  93.5 0.0 copy-done.6
  93.6 0.3 convolution_bitcast_fusion
  93.9 0.3 convolution_bitcast_fusion.2
  94.2 0.3 convolution_bitcast_fusion.1
  94.5 0.0 copy-start
  94.5 3.9 %collective-permute-start.3 = (f32[4,8,1024]{2,1,0:T(8,128)S(1)}, f32[4,8,1024]{2,1,0:T(8,128)S(1)}, u32[]{:S(2)}, u32[]{:S(2)}) collective-permute-start(f32[4,8,1024]{2,1,0:T(8,128)S(1)} %get-tuple-element.11), channel_id=1, source_target_pairs={{1,0},{2,1},{3,2},{4,3},{5,4},{6,5},{7,6},{8,7},{9,8},{10,9},{11,1... | collective-permute-start | bytes 393224 | tf_op jit(solution)/shard_map/ppermute | solution.py:366
  98.5 0.0 collective-permute-start.2
  98.5 0.1 convert_reduce_fusion
  98.6 0.1 convert_reduce_fusion.2
  98.7 0.6 pad_maximum_fusion.1.hit_ref
  99.3 5.6 %collective-permute-done.3.bottom_aux_ref = f32[4,8,1024]{2,1,0:T(8,128)S(1)} collective-permute-done((f32[4,8,1024]{2,1,0:T(8,128)S(1)}, f32[4,8,1024]{2,1,0:T(8,128)S(1)}, u32[]{:S(2)}, u32[]{:S(2)}) %collective-permute-start.3) | collective-permute-done | bytes 131104 | tf_op jit(solution)/shard_map/ppermute | solution.py:366
  104.9 0.0 copy-start.3
  105.0 3.1 %collective-permute-done.2.top_aux_ref = f32[4,8,1024]{2,1,0:T(8,128)S(1)} collective-permute-done((f32[4,8,1024]{2,1,0:T(8,128)S(1)}, f32[4,8,1024]{2,1,0:T(8,128)S(1)}, u32[]{:S(2)}, u32[]{:S(2)}) %collective-permute-start.2) | collective-permute-done | bytes 131104 | tf_op jit(solution)/shard_map/ppermute | solution.py:365
  108.1 0.0 copy-start.4
  108.1 0.0 collective-permute-done.1.bottom_ref
  108.1 0.0 copy-start.1
  108.1 0.0 collective-permute-done.top_ref
  108.1 0.0 copy-done
  108.1 0.0 copy-done.3
  108.1 0.6 copy-done.4
  108.7 0.2 copy-done.1
  108.9 0.0 copy-start.2
  108.9 0.8 copy-done.2
  109.7 9.1 %shard_map.65 = f32[13,32,1024]{2,1,0:T(8,128)} custom-call(f32[3,4]{1,0:T(4,128)} %coef_ref.1, f32[13,32,1024]{2,1,0:T(8,128)} %get-tuple-element.7.tile_ref, f32[4,32,1024]{2,1,0:T(8,128)} %copy-done, f32[13,8,1024]{2,1,0:T(8,128)} %copy-done.2, f32[13,8,1024]{2,1,0:T(8,128)} %copy-done.1, f32[4,8,1024]{2,1,0:T(8,128)} %copy-done.4, ...), custom_call_target="tpu_custom_call" | custom-call | tf_op jit(solution)/shard_map/pallas_call | solution.py:328
  (5 shorter events, 0.1 us)
Async XLA Ops:
  0.0 93.5 %copy-start.7 = (s32[3,64]{1,0:T(4,128)S(1)}, s32[3,64]{1,0:T(4,128)}, u32[]{:S(2)}) copy-start(s32[3,64]{1,0:T(4,128)} %param.11) | copy-start | bytes 2308
  0.0 93.5 %copy-start.5 = (s32[32,1024]{1,0:T(8,128)S(1)}, s32[32,1024]{1,0:T(8,128)}, u32[]{:S(2)}) copy-start(s32[32,1024]{1,0:T(8,128)} %param.8) | copy-start | bytes 393220
  87.3 6.2 %copy-start.6 = (f32[16,3,4,32]{3,2,1,0:T(4,128)S(1)}, f32[16,3,4,32]{3,2,1,0:T(4,128)}, u32[]{:S(2)}) copy-start(f32[16,3,4,32]{3,2,1,0:T(4,128)} %get-tuple-element.8) | copy-start | bytes 73732
  88.6 19.5 %collective-permute-start.1 = (f32[13,8,1024]{2,1,0:T(8,128)S(1)}, f32[13,8,1024]{2,1,0:T(8,128)S(1)}, u32[]{:S(2)}, u32[]{:S(2)}) collective-permute-start(f32[13,8,1024]{2,1,0:T(8,128)S(1)} %get-tuple-element.9), channel_id=1, source_target_pairs={{1,0},{2,1},{3,2},{4,3},{5,4},{6,5},{7,6},{8,7},{9,8},{10,9},{11,1... | collective-permute-start | bytes 1277960 | tf_op jit(solution)/shard_map/ppermute | solution.py:348
  93.5 14.6 %collective-permute-start = (f32[13,8,1024]{2,1,0:T(8,128)S(1)}, f32[13,8,1024]{2,1,0:T(8,128)S(1)}, u32[]{:S(2)}, u32[]{:S(2)}) collective-permute-start(f32[13,8,1024]{2,1,0:T(8,128)S(1)} %get-tuple-element.10), channel_id=1, source_target_pairs={{0,1},{1,2},{2,3},{3,4},{4,5},{5,6},{6,7},{7,8},{8,9},{9,10},{10,1... | collective-permute-start | bytes 1277960 | tf_op jit(solution)/shard_map/ppermute | solution.py:347
  94.5 13.6 %copy-start = (f32[4,32,1024]{2,1,0:T(8,128)}, f32[4,32,1024]{2,1,0:T(8,128)S(1)}, u32[]{:S(2)}) copy-start(f32[4,32,1024]{2,1,0:T(8,128)S(1)} %pad_maximum_fusion.aux_ref) | copy-start | bytes 1572868
  94.5 10.4 %collective-permute-start.3 = (f32[4,8,1024]{2,1,0:T(8,128)S(1)}, f32[4,8,1024]{2,1,0:T(8,128)S(1)}, u32[]{:S(2)}, u32[]{:S(2)}) collective-permute-start(f32[4,8,1024]{2,1,0:T(8,128)S(1)} %get-tuple-element.11), channel_id=1, source_target_pairs={{1,0},{2,1},{3,2},{4,3},{5,4},{6,5},{7,6},{8,7},{9,8},{10,9},{11,1... | collective-permute-start | bytes 393224 | tf_op jit(solution)/shard_map/ppermute | solution.py:366
  98.5 9.6 %collective-permute-start.2 = (f32[4,8,1024]{2,1,0:T(8,128)S(1)}, f32[4,8,1024]{2,1,0:T(8,128)S(1)}, u32[]{:S(2)}, u32[]{:S(2)}) collective-permute-start(f32[4,8,1024]{2,1,0:T(8,128)S(1)} %get-tuple-element.12), channel_id=1, source_target_pairs={{0,1},{1,2},{2,3},{3,4},{4,5},{5,6},{6,7},{7,8},{8,9},{9,10},{10,1... | collective-permute-start | bytes 393224 | tf_op jit(solution)/shard_map/ppermute | solution.py:365
  104.9 3.2 %copy-start.3 = (f32[4,8,1024]{2,1,0:T(8,128)}, f32[4,8,1024]{2,1,0:T(8,128)S(1)}, u32[]{:S(2)}) copy-start(f32[4,8,1024]{2,1,0:T(8,128)S(1)} %collective-permute-done.3.bottom_aux_ref) | copy-start | bytes 393220
  108.1 0.7 copy-start.4
  108.1 0.8 copy-start.1
  108.9 0.8 copy-start.2

commit v15 on v14

--- a/solution.py
+++ b/solution.py
@@ -104,8 +104,8 @@
 
 
 def exchange_kernel(
-    count, grid_cols, groups, anc_ref, ens_ref, alt_ref, out_ref, lines_ref,
-    held_a, held_b, outgoing_a, outgoing_b, send1, recv1, send2, recv2, send3, recv3, local,
+    count, grid_cols, groups, reach, anc_ref, ens_ref, alt_ref, out_ref, lines_ref, low_ref, high_ref,
+    held_a, held_b, outgoing_a, outgoing_b, send1, recv1, send2, recv2, send3, recv3, local, edge_sems,
 ):
     me = lax.axis_index("particle")
     held = (held_a, held_b)
@@ -196,6 +196,8 @@
             src_ref=alt_ref, dst_ref=lines_ref.at[sender], send_sem=send3.at[offset],
             recv_sem=recv3.at[sender], device_id={"particle": sender}, device_id_type=MESH,
         ).wait_recv()
+    height = out_ref.shape[1]
+    edges = []
     for group, fields in enumerate(groups):
         seconds[group][0].wait()
         for offset, copy in zip(range(1, count), seconds[group][1:]):
@@ -207,9 +209,18 @@
                 send_sem=send2.at[group, offset], recv_sem=recv2.at[group, sender],
                 device_id={"particle": sender}, device_id_type=MESH,
             ).wait_recv()
-
-
-def resample(tile, ancestors, altimetry):
+        for turn, (start, target) in enumerate(((0, low_ref), (height - reach, high_ref))):
+            edge = pltpu.make_async_copy(
+                out_ref.at[fields, pl.ds(start, reach)], target.at[fields],
+                edge_sems.at[2 * group + turn],
+            )
+            edge.start()
+            edges.append(edge)
+    for edge in edges:
+        edge.wait()
+
+
+def resample(tile, ancestors, altimetry, reach):
     count = lax.axis_size("particle")
     fields, height, width = tile.shape
     grid_rows = 4
@@ -220,10 +231,12 @@
     sems = pltpu.SemaphoreType.DMA((count,))
     grouped = pltpu.SemaphoreType.DMA((len(groups), count))
     return pl.pallas_call(
-        functools.partial(exchange_kernel, count, grid_cols, groups),
+        functools.partial(exchange_kernel, count, grid_cols, groups, reach),
         out_shape=(
             jax.ShapeDtypeStruct(tile.shape, tile.dtype),
             jax.ShapeDtypeStruct((count,) + altimetry.shape, altimetry.dtype),
+            jax.ShapeDtypeStruct((fields, reach, width), tile.dtype),
+            jax.ShapeDtypeStruct((fields, reach, width), tile.dtype),
         ),
         in_specs=[
             pl.BlockSpec(memory_space=pltpu.SMEM),
@@ -233,6 +246,8 @@
         out_specs=(
             pl.BlockSpec(memory_space=pl.ANY),
             pl.BlockSpec(memory_space=pltpu.VMEM),
+            pl.BlockSpec(memory_space=pltpu.VMEM),
+            pl.BlockSpec(memory_space=pltpu.VMEM),
         ),
         scratch_shapes=[
             pltpu.VMEM((count, split, rows, cols), tile.dtype),
@@ -241,6 +256,7 @@
             pltpu.VMEM((count, fields - split, rows, cols), tile.dtype),
             grouped, grouped, grouped, grouped, sems, sems,
             pltpu.SemaphoreType.DMA((1 + 2 * len(groups),)),
+            pltpu.SemaphoreType.DMA((2 * len(groups),)),
         ],
         compiler_params=pltpu.CompilerParams(collective_id=0, has_side_effects=True),
     )(ancestors, tile, altimetry)
@@ -340,12 +356,12 @@
 def per_device(ensemble, ancestors, depth_levels, level_coefs, altimetry, obs_rows):
     width_y = ensemble.shape[3]
     reach = 8
-    tile, gathered = resample(ensemble[0], ancestors, altimetry)
+    tile, gathered, low, high = resample(ensemble[0], ancestors, altimetry, reach)
     count = lax.axis_size("space")
     forward = [(i, (i + 1) % count) for i in range(count)]
     backward = [(target, source) for source, target in forward]
-    top = lax.ppermute(tile[:, -reach:], "space", forward)
-    bottom = lax.ppermute(tile[:, :reach], "space", backward)
+    top = lax.ppermute(high, "space", forward)
+    bottom = lax.ppermute(low, "space", backward)
     all_lines = jnp.moveaxis(gathered, 0, 1).reshape(
         (altimetry.shape[0], -1) + altimetry.shape[2:]
     )

time: 119 us -> 117 us (0.983); the launches traced: 119 us -> 115 us
  starting transfers between devices: 8.83 us -> 6.27 us
  Pallas kernels: 96.5 us -> 97.8 us
  waiting for transfers between devices: 8.76 us -> 7.54 us
    ppermute x1, waiting for transfers between devices: 3.14 us -> 0.01 us  [per_device(): top_aux = lax.ppermute(aux[:, -reach:], 'space', forward)]
    ppermute x1, starting transfers between devices: 3.92 us -> 1.29 us  [per_device(): bottom_aux = lax.ppermute(aux[:, :reach], 'space', backward)]
    ppermute x1, waiting for transfers between devices: 5.62 us -> 7.53 us  [per_device(): bottom_aux = lax.ppermute(aux[:, :reach], 'space', backward)]
    pallas_call x1, Pallas kernels: 87.3 us -> 88.7 us  [resample(): pl.pallas_call(functools.partial(exchange_kernel, count, grid_cols, group...]
    slice x1 -> x0, local copies, waits for them, and re-layouts: 1.25 us -> none  [per_device(): bottom = lax.ppermute(tile[:, :reach], 'space', backward)]
  transfers between devices with their start and end apart: 4 -> 4, of which waited for: 2 -> 1; matrix products, arithmetic and copies ran while one was open for 2% -> 2% of each run, Pallas kernels for 0% -> 0%
where the time goes in v15:
time: 117 us; the launch traced here: 115 us
  Pallas kernels  97.8 us (84%)
  waiting for transfers between devices  7.54 us (6%)
  starting transfers between devices  6.27 us (5%)
  local copies, waits for them, and re-layouts  1.82 us (2%)
    pallas_call x1, Pallas kernels, resample(): pl.pallas_call(functools.partial(exchange_kernel, count, grid_cols, group...  88.7 us
    pallas_call x1, Pallas kernels, run_steps(): pl.pallas_call(stencil_kernel, out_shape=jax.ShapeDtypeStruct(tile.shape,...  9.14 us
    ppermute x1, waiting for transfers between devices, per_device(): bottom_aux = lax.ppermute(aux[:, :reach], 'space', backward)  7.53 us
    ppermute x1, starting transfers between devices, per_device(): bottom = lax.ppermute(low, 'space', backward)  4.9 us
  transfers between devices with their start and end apart: 4, of which 1 were waited for; matrix products, arithmetic and copies ran while one was open for 2% of the time, Pallas kernels for 0%

profile of v15, /device:TPU:24, one launch (start us, length us, event | category | flops | bytes accessed | tf_op | source)
XLA Modules:
  0.0 115.4 jit_solution(15049442321984769959)
XLA Ops:
  0.0 0.0 copy-start.6
  0.0 0.0 copy-start.5
  0.0 88.7 %shard_map.64 = (f32[13,32,1024]{2,1,0:T(8,128)}, f32[16,3,4,32]{3,2,1,0:T(4,128)}, f32[13,8,1024]{2,1,0:T(8,128)}, f32[13,8,1024]{2,1,0:T(8,128)}) custom-call(s32[16]{0:T(128)} %anc_ref.1, f32[13,32,1024]{2,1,0:T(8,128)} %bitcast.26, f32[3,4,32]{2,1,0:T(4,128)} %alt_ref.1), custom_call_target="tpu_custom_call" | custom-call | tf_op jit(solution)/shard_map/pallas_call | solution.py:233
  88.7 0.1 collective-permute-start
  88.8 4.9 %collective-permute-start.1 = (f32[13,8,1024]{2,1,0:T(8,128)}, f32[13,8,1024]{2,1,0:T(8,128)S(1)}, u32[]{:S(2)}, u32[]{:S(2)}) collective-permute-start(f32[13,8,1024]{2,1,0:T(8,128)} %get-tuple-element.12), channel_id=1, source_target_pairs={{1,0},{2,1},{3,2},{4,3},{5,4},{6,5},{7,6},{8,7},{9,8},{10,9},{11,1... | collective-permute-start | bytes 1277960 | tf_op jit(solution)/shard_map/ppermute | solution.py:364
  93.7 0.0 copy-done.6
  93.7 0.0 copy-done.5
  93.7 0.8 fusion.4
  94.5 0.3 convolution_bitcast_fusion
  94.8 0.3 convolution_bitcast_fusion.2
  95.1 0.3 convolution_bitcast_fusion.1
  95.5 0.0 copy-start
  95.5 1.3 %collective-permute-start.3 = (f32[4,8,1024]{2,1,0:T(8,128)S(1)}, f32[4,8,1024]{2,1,0:T(8,128)S(1)}, u32[]{:S(2)}, u32[]{:S(2)}) collective-permute-start(f32[4,8,1024]{2,1,0:T(8,128)S(1)} %get-tuple-element.13), channel_id=1, source_target_pairs={{1,0},{2,1},{3,2},{4,3},{5,4},{6,5},{7,6},{8,7},{9,8},{10,9},{11,1... | collective-permute-start | bytes 393224 | tf_op jit(solution)/shard_map/ppermute | solution.py:382
  96.8 0.0 collective-permute-start.2
  96.8 0.1 convert_reduce_fusion
  96.9 0.1 convert_reduce_fusion.2
  97.0 0.6 pad_maximum_fusion.1.hit_ref
  97.7 7.5 %collective-permute-done.3.bottom_aux_ref = f32[4,8,1024]{2,1,0:T(8,128)S(1)} collective-permute-done((f32[4,8,1024]{2,1,0:T(8,128)S(1)}, f32[4,8,1024]{2,1,0:T(8,128)S(1)}, u32[]{:S(2)}, u32[]{:S(2)}) %collective-permute-start.3) | collective-permute-done | bytes 131104 | tf_op jit(solution)/shard_map/ppermute | solution.py:382
  105.2 0.0 copy-start.3
  105.2 0.0 collective-permute-done.2.top_aux_ref
  105.2 0.0 copy-start.4
  105.2 0.0 collective-permute-done.top_ref
  105.2 0.0 copy-start.1
  105.2 0.0 collective-permute-done.1.bottom_ref
  105.2 0.0 copy-start.2
  105.2 0.0 copy-done
  105.2 0.6 copy-done.3
  105.8 0.1 copy-done.4
  105.9 0.2 copy-done.1
  106.1 0.2 copy-done.2
  106.2 9.1 %shard_map.65 = f32[13,32,1024]{2,1,0:T(8,128)} custom-call(f32[3,4]{1,0:T(4,128)} %coef_ref.1, f32[13,32,1024]{2,1,0:T(8,128)} %get-tuple-element.9.tile_ref, f32[4,32,1024]{2,1,0:T(8,128)} %copy-done, f32[13,8,1024]{2,1,0:T(8,128)} %copy-done.1, f32[13,8,1024]{2,1,0:T(8,128)} %copy-done.2, f32[4,8,1024]{2,1,0:T(8,128)} %copy-done.4, ...), custom_call_target="tpu_custom_call" | custom-call | tf_op jit(solution)/shard_map/pallas_call | solution.py:344
  (4 shorter events, 0.1 us)
Async XLA Ops:
  0.0 93.7 %copy-start.6 = (s32[3,64]{1,0:T(4,128)S(1)}, s32[3,64]{1,0:T(4,128)}, u32[]{:S(2)}) copy-start(s32[3,64]{1,0:T(4,128)} %param.11) | copy-start | bytes 2308
  0.0 93.7 %copy-start.5 = (s32[32,1024]{1,0:T(8,128)S(1)}, s32[32,1024]{1,0:T(8,128)}, u32[]{:S(2)}) copy-start(s32[32,1024]{1,0:T(8,128)} %param.8) | copy-start | bytes 393220
  88.7 16.5 %collective-permute-start = (f32[13,8,1024]{2,1,0:T(8,128)}, f32[13,8,1024]{2,1,0:T(8,128)S(1)}, u32[]{:S(2)}, u32[]{:S(2)}) collective-permute-start(f32[13,8,1024]{2,1,0:T(8,128)} %get-tuple-element.11), channel_id=1, source_target_pairs={{0,1},{1,2},{2,3},{3,4},{4,5},{5,6},{6,7},{7,8},{8,9},{9,10},{10,1... | collective-permute-start | bytes 1277960 | tf_op jit(solution)/shard_map/ppermute | solution.py:363
  88.8 16.4 %collective-permute-start.1 = (f32[13,8,1024]{2,1,0:T(8,128)}, f32[13,8,1024]{2,1,0:T(8,128)S(1)}, u32[]{:S(2)}, u32[]{:S(2)}) collective-permute-start(f32[13,8,1024]{2,1,0:T(8,128)} %get-tuple-element.12), channel_id=1, source_target_pairs={{1,0},{2,1},{3,2},{4,3},{5,4},{6,5},{7,6},{8,7},{9,8},{10,9},{11,1... | collective-permute-start | bytes 1277960 | tf_op jit(solution)/shard_map/ppermute | solution.py:364
  95.5 9.8 %copy-start = (f32[4,32,1024]{2,1,0:T(8,128)}, f32[4,32,1024]{2,1,0:T(8,128)S(1)}, u32[]{:S(2)}) copy-start(f32[4,32,1024]{2,1,0:T(8,128)S(1)} %pad_maximum_fusion.aux_ref) | copy-start | bytes 1572868
  95.5 9.7 %collective-permute-start.3 = (f32[4,8,1024]{2,1,0:T(8,128)S(1)}, f32[4,8,1024]{2,1,0:T(8,128)S(1)}, u32[]{:S(2)}, u32[]{:S(2)}) collective-permute-start(f32[4,8,1024]{2,1,0:T(8,128)S(1)} %get-tuple-element.13), channel_id=1, source_target_pairs={{1,0},{2,1},{3,2},{4,3},{5,4},{6,5},{7,6},{8,7},{9,8},{10,9},{11,1... | collective-permute-start | bytes 393224 | tf_op jit(solution)/shard_map/ppermute | solution.py:382
  96.8 8.4 %collective-permute-start.2 = (f32[4,8,1024]{2,1,0:T(8,128)S(1)}, f32[4,8,1024]{2,1,0:T(8,128)S(1)}, u32[]{:S(2)}, u32[]{:S(2)}) collective-permute-start(f32[4,8,1024]{2,1,0:T(8,128)S(1)} %get-tuple-element.14), channel_id=1, source_target_pairs={{0,1},{1,2},{2,3},{3,4},{4,5},{5,6},{6,7},{7,8},{8,9},{9,10},{10,1... | collective-permute-start | bytes 393224 | tf_op jit(solution)/shard_map/ppermute | solution.py:381
  105.2 0.6 copy-start.3
  105.2 0.7 copy-start.4
  105.2 0.9 copy-start.1
  105.2 1.0 copy-start.2

commit v16 on v15

--- a/solution.py
+++ b/solution.py
@@ -360,8 +360,6 @@
     count = lax.axis_size("space")
     forward = [(i, (i + 1) % count) for i in range(count)]
     backward = [(target, source) for source, target in forward]
-    top = lax.ppermute(high, "space", forward)
-    bottom = lax.ppermute(low, "space", backward)
     all_lines = jnp.moveaxis(gathered, 0, 1).reshape(
         (altimetry.shape[0], -1) + altimetry.shape[2:]
     )
@@ -378,10 +376,12 @@
         )
         hits.append(jnp.sum(onehot, axis=0)[None, :])
     aux = jnp.stack(targets + [depth_levels.astype(jnp.float32)], axis=0)
-    top_aux = lax.ppermute(aux[:, -reach:], "space", forward)
-    bottom_aux = lax.ppermute(aux[:, :reach], "space", backward)
+    fields = tile.shape[0]
+    top = lax.ppermute(jnp.concatenate([high, aux[:, -reach:]], axis=0), "space", forward)
+    bottom = lax.ppermute(jnp.concatenate([low, aux[:, :reach]], axis=0), "space", backward)
     state = run_steps(
-        level_coefs, tile, aux, top, bottom, top_aux, bottom_aux, jnp.stack(hits, axis=0)
+        level_coefs, tile, aux, top[:fields], bottom[:fields], top[fields:], bottom[fields:],
+        jnp.stack(hits, axis=0),
     )
     return state[None]
 

time: 117 us -> 122 us (1.043)
  the two profiles are of different devices: /device:TPU:24 before, /device:TPU:88 now
where the time goes in v16:
time: 122 us
  Pallas kernels  98.8 us (81%)
  waiting for transfers between devices  11.4 us (9%)
  local copies, waits for them, and re-layouts  4.61 us (4%)
  starting transfers between devices  3.99 us (3%)
  other arithmetic  1.88 us (2%)
    pallas_call x1, Pallas kernels, resample(): pl.pallas_call(functools.partial(exchange_kernel, count, grid_cols, group...  89.7 us
    ppermute x1, waiting for transfers between devices, per_device(): lax.ppermute(jnp.concatenate([high, aux[:, -reach:]], axis=0), 'space', f...  11.4 us
    pallas_call x1, Pallas kernels, run_steps(): pl.pallas_call(stencil_kernel, out_shape=jax.ShapeDtypeStruct(tile.shape,...  9.14 us
    ppermute x1, starting transfers between devices, per_device(): lax.ppermute(jnp.concatenate([low, aux[:, :reach]], axis=0), 'space', bac...  3.91 us
  transfers between devices with their start and end apart: 2, of which 1 were waited for; matrix products, arithmetic and copies ran while one was open for 2% of the time, Pallas kernels for 0%

profile of v16, /device:TPU:88, one launch (start us, length us, event | category | flops | bytes accessed | tf_op | source)
XLA Modules:
  0.0 121.7 jit_solution(13308058674239293291)
XLA Ops:
  0.0 0.8 slice_bitcast_fusion.2
  0.8 0.9 convert_bitcast_fusion
  1.7 89.7 %shard_map.64 = (f32[13,32,1024]{2,1,0:T(8,128)}, f32[16,3,4,32]{3,2,1,0:T(4,128)}, f32[13,8,1024]{2,1,0:T(8,128)}, f32[13,8,1024]{2,1,0:T(8,128)}) custom-call(s32[16]{0:T(128)} %anc_ref.1, f32[13,32,1024]{2,1,0:T(8,128)} %bitcast.26, f32[3,4,32]{2,1,0:T(4,128)} %alt_ref.1), custom_call_target="tpu_custom_call" | custom-call | tf_op jit(solution)/shard_map/pallas_call | solution.py:233
  91.4 0.0 copy-start.2
  91.4 0.0 copy-start.1
  91.4 0.9 fusion.4
  92.3 0.3 convolution_bitcast_fusion
  92.6 0.3 convolution_bitcast_fusion.2
  92.9 0.3 convolution_bitcast_fusion.1
  93.2 0.0 copy-start
  93.2 0.0 copy-done.2
  93.3 0.1 collective-permute-start
  93.4 0.0 copy-done.1
  93.5 3.9 %collective-permute-start.1 = (f32[17,8,1024]{2,1,0:T(8,128)S(1)}, f32[17,8,1024]{2,1,0:T(8,128)S(1)}, u32[]{:S(2)}, u32[]{:S(2)}) collective-permute-start(f32[17,8,1024]{2,1,0:T(8,128)S(1)} %pad_maximum_fusion.1), channel_id=1, source_target_pairs={{1,0},{2,1},{3,2},{4,3},{5,4},{6,5},{7,6},{8,7},{9,8},{10,9},{11,1... | collective-permute-start | bytes 1671176 | tf_op jit(solution)/shard_map/ppermute | solution.py:381
  97.4 0.1 convert_reduce_fusion.2
  97.5 0.1 convert_reduce_fusion
  97.6 0.6 pad_maximum_fusion.3.hit_ref
  98.2 11.4 %collective-permute-done = f32[17,8,1024]{2,1,0:T(8,128)S(1)} collective-permute-done((f32[17,8,1024]{2,1,0:T(8,128)S(1)}, f32[17,8,1024]{2,1,0:T(8,128)S(1)}, u32[]{:S(2)}, u32[]{:S(2)}) %collective-permute-start) | collective-permute-done | bytes 557088 | tf_op jit(solution)/shard_map/ppermute | solution.py:380
  109.6 0.7 slice.58.top_aux_ref
  110.3 0.8 slice.55.top_ref
  111.0 0.0 copy-done
  111.0 0.0 collective-permute-done.1
  111.1 0.7 slice.59.bottom_aux_ref
  111.7 0.8 slice.57.bottom_ref
  112.5 9.1 %shard_map.65 = f32[13,32,1024]{2,1,0:T(8,128)} custom-call(f32[3,4]{1,0:T(4,128)} %coef_ref.1, f32[13,32,1024]{2,1,0:T(8,128)} %get-tuple-element.9.tile_ref, f32[4,32,1024]{2,1,0:T(8,128)} %copy-done, f32[13,8,1024]{2,1,0:T(8,128)} %slice.55.top_ref, f32[13,8,1024]{2,1,0:T(8,128)} %slice.57.bottom_ref, f32[4,8,1024]{2,1,0:T(8,128)} %slice.58.top_aux_ref, ...), custom_call_target="tpu_custom_call" | custom-call | tf_op jit(solution)/shard_map/pallas_call | solution.py:344
  (4 shorter events, 0.1 us)
Async XLA Ops:
  91.4 1.9 %copy-start.2 = (f32[13,8,1024]{2,1,0:T(8,128)S(1)}, f32[13,8,1024]{2,1,0:T(8,128)}, u32[]{:S(2)}) copy-start(f32[13,8,1024]{2,1,0:T(8,128)} %get-tuple-element.11) | copy-start | bytes 1277956
  91.4 2.0 %copy-start.1 = (f32[13,8,1024]{2,1,0:T(8,128)S(1)}, f32[13,8,1024]{2,1,0:T(8,128)}, u32[]{:S(2)}) copy-start(f32[13,8,1024]{2,1,0:T(8,128)} %get-tuple-element.12) | copy-start | bytes 1277956
  93.2 17.8 %copy-start = (f32[4,32,1024]{2,1,0:T(8,128)}, f32[4,32,1024]{2,1,0:T(8,128)S(1)}, u32[]{:S(2)}) copy-start(f32[4,32,1024]{2,1,0:T(8,128)S(1)} %pad_maximum_fusion.2.aux_ref) | copy-start | bytes 1572868
  93.3 16.3 %collective-permute-start = (f32[17,8,1024]{2,1,0:T(8,128)S(1)}, f32[17,8,1024]{2,1,0:T(8,128)S(1)}, u32[]{:S(2)}, u32[]{:S(2)}) collective-permute-start(f32[17,8,1024]{2,1,0:T(8,128)S(1)} %pad_maximum_fusion), channel_id=1, source_target_pairs={{0,1},{1,2},{2,3},{3,4},{4,5},{5,6},{6,7},{7,8},{8,9},{9,10},{10,1... | collective-permute-start | bytes 1671176 | tf_op jit(solution)/shard_map/ppermute | solution.py:380
  93.5 17.6 %collective-permute-start.1 = (f32[17,8,1024]{2,1,0:T(8,128)S(1)}, f32[17,8,1024]{2,1,0:T(8,128)S(1)}, u32[]{:S(2)}, u32[]{:S(2)}) collective-permute-start(f32[17,8,1024]{2,1,0:T(8,128)S(1)} %pad_maximum_fusion.1), channel_id=1, source_target_pairs={{1,0},{2,1},{3,2},{4,3},{5,4},{6,5},{7,6},{8,7},{9,8},{10,9},{11,1... | collective-permute-start | bytes 1671176 | tf_op jit(solution)/shard_map/ppermute | solution.py:381

commit v17 on v15

--- a/solution.py
+++ b/solution.py
@@ -362,9 +362,15 @@
     backward = [(target, source) for source, target in forward]
     top = lax.ppermute(high, "space", forward)
     bottom = lax.ppermute(low, "space", backward)
-    all_lines = jnp.moveaxis(gathered, 0, 1).reshape(
+    own_lines = jnp.moveaxis(gathered, 0, 1).reshape(
         (altimetry.shape[0], -1) + altimetry.shape[2:]
     )
+    lines_above = lax.ppermute(own_lines[..., -reach:], "space", forward)
+    lines_below = lax.ppermute(own_lines[..., :reach], "space", backward)
+    depth = depth_levels.astype(jnp.float32)
+    depth_above = lax.ppermute(depth[-reach:], "space", forward)
+    depth_below = lax.ppermute(depth[:reach], "space", backward)
+    all_lines = jnp.concatenate([lines_above, own_lines, lines_below], axis=-1)
     columns = jnp.arange(width_y, dtype=jnp.int32)
     targets = []
     hits = []
@@ -377,9 +383,11 @@
             )
         )
         hits.append(jnp.sum(onehot, axis=0)[None, :])
-    aux = jnp.stack(targets + [depth_levels.astype(jnp.float32)], axis=0)
-    top_aux = lax.ppermute(aux[:, -reach:], "space", forward)
-    bottom_aux = lax.ppermute(aux[:, :reach], "space", backward)
+    targets = jnp.stack(targets, axis=0)
+    rows = tile.shape[1]
+    aux = jnp.concatenate([targets[:, reach : reach + rows], depth[None]], axis=0)
+    top_aux = jnp.concatenate([targets[:, :reach], depth_above[None]], axis=0)
+    bottom_aux = jnp.concatenate([targets[:, reach + rows :], depth_below[None]], axis=0)
     state = run_steps(
         level_coefs, tile, aux, top, bottom, top_aux, bottom_aux, jnp.stack(hits, axis=0)
     )

time: 117 us -> 123 us (1.051); the launches traced: 115 us -> 123 us
  starting transfers between devices: 6.27 us -> 9.14 us
  other arithmetic: 0.89 us -> 3.5 us
    ppermute x2 -> x4, starting transfers between devices: 1.29 us -> 7.56 us  [the longest x1 3.84 us: per_device(): lines_below = lax.ppermute(own_lines[..., :reach], 'space', backward)]
    ppermute x1, waiting for transfers between devices: 0.01 us -> 5.93 us  [per_device(): top = lax.ppermute(high, 'space', forward)]
    ppermute x2 -> x4, waiting for transfers between devices: 7.53 us -> 2.28 us  [the longest x1 2.27 us: per_device(): lines_above = lax.ppermute(own_lines[..., -reach:], 'space', forward)]
    ppermute x1, starting transfers between devices: 4.9 us -> 1.58 us  [per_device(): bottom = lax.ppermute(low, 'space', backward)]
    concatenate x0 -> x3, other arithmetic: none -> 1.68 us  [the longest x1 0.85 us: per_device(): aux = jnp.concatenate([targets[:, reach:reach + rows], depth[None]], axis=0)]
  transfers between devices with their start and end apart: 4 -> 6, of which waited for: 1 -> 2; matrix products, arithmetic and copies ran while one was open for 2% -> 4% of each run, Pallas kernels for 0% -> 73%
where the time goes in v17:
time: 123 us
  Pallas kernels  98.8 us (80%)
  starting transfers between devices  9.14 us (7%)
  waiting for transfers between devices  8.21 us (7%)
  other arithmetic  3.5 us (3%)
  local copies, waits for them, and re-layouts  1.99 us (2%)
    pallas_call x1, Pallas kernels, resample(): pl.pallas_call(functools.partial(exchange_kernel, count, grid_cols, group...  89.7 us
    pallas_call x1, Pallas kernels, run_steps(): pl.pallas_call(stencil_kernel, out_shape=jax.ShapeDtypeStruct(tile.shape,...  9.14 us
    ppermute x1, waiting for transfers between devices, per_device(): top = lax.ppermute(high, 'space', forward)  5.93 us
    ppermute x1, starting transfers between devices, per_device(): lines_below = lax.ppermute(own_lines[..., :reach], 'space', backward)  3.84 us
    ppermute x1, starting transfers between devices, per_device(): depth_below = lax.ppermute(depth[:reach], 'space', backward)  3.63 us
  transfers between devices with their start and end apart: 6, of which 2 were waited for; matrix products, arithmetic and copies ran while one was open for 4% of the time, Pallas kernels for 73%

profile of v17, /device:TPU:24, one launch (start us, length us, event | category | flops | bytes accessed | tf_op | source)
XLA Modules:
  0.0 122.7 jit_solution(6263465339972643970)
XLA Ops:
  0.0 0.0 copy-start.2
  0.0 0.9 fusion.6
  1.0 3.6 %collective-permute-start.5 = (f32[8,1024]{1,0:T(8,128)S(1)}, f32[8,1024]{1,0:T(8,128)S(1)}, u32[]{:S(2)}, u32[]{:S(2)}) collective-permute-start(f32[8,1024]{1,0:T(8,128)S(1)} %get-tuple-element.15), channel_id=1, source_target_pairs={{1,0},{2,1},{3,2},{4,3},{5,4},{6,5},{7,6},{8,7},{9,8},{10,9},{11,1... | collective-permute-start | bytes 98312 | tf_op jit(solution)/shard_map/ppermute | solution.py:372
  4.6 0.0 collective-permute-start.4
  4.6 89.7 %shard_map.64 = (f32[13,32,1024]{2,1,0:T(8,128)}, f32[16,3,4,32]{3,2,1,0:T(4,128)}, f32[13,8,1024]{2,1,0:T(8,128)}, f32[13,8,1024]{2,1,0:T(8,128)}) custom-call(s32[16]{0:T(128)} %anc_ref.1, f32[13,32,1024]{2,1,0:T(8,128)} %bitcast.32, f32[3,4,32]{2,1,0:T(4,128)} %alt_ref.1), custom_call_target="tpu_custom_call" | custom-call | tf_op jit(solution)/shard_map/pallas_call | solution.py:233
  94.3 0.9 copy.8
  95.2 0.1 fusion.7
  95.3 0.1 collective-permute-start
  95.4 3.8 %collective-permute-start.1 = (f32[3,64,8]{2,1,0:T(8,128)S(1)}, f32[3,64,8]{2,1,0:T(8,128)S(1)}, u32[]{:S(2)}, u32[]{:S(2)}) collective-permute-start(f32[3,64,8]{2,1,0:T(8,128)S(1)} %get-tuple-element.20), channel_id=1, source_target_pairs={{1,0},{2,1},{3,2},{4,3},{5,4},{6,5},{7,6},{8,7},{9,8},{10,9},{11,1... | collective-permute-start | bytes 18440 | tf_op jit(solution)/shard_map/ppermute | solution.py:369
  99.2 0.0 collective-permute-start.2
  99.2 0.0 copy-done.2
  99.2 0.1 convert_reduce_fusion.2
  99.3 0.1 convert_reduce_fusion
  99.5 0.6 pad_maximum_fusion.7.hit_ref
  100.1 2.3 %collective-permute-done = f32[3,64,8]{2,1,0:T(8,128)S(1)} collective-permute-done((f32[3,64,8]{2,1,0:T(8,128)S(1)}, f32[3,64,8]{2,1,0:T(8,128)S(1)}, u32[]{:S(2)}, u32[]{:S(2)}) %collective-permute-start) | collective-permute-done | bytes 6176 | tf_op jit(solution)/shard_map/ppermute | solution.py:368
  102.3 1.6 %collective-permute-start.3 = (f32[13,8,1024]{2,1,0:T(8,128)}, f32[13,8,1024]{2,1,0:T(8,128)S(1)}, u32[]{:S(2)}, u32[]{:S(2)}) collective-permute-start(f32[13,8,1024]{2,1,0:T(8,128)} %get-tuple-element.12), channel_id=1, source_target_pairs={{1,0},{2,1},{3,2},{4,3},{5,4},{6,5},{7,6},{8,7},{9,8},{10,9},{11,1... | collective-permute-start | bytes 1277960 | tf_op jit(solution)/shard_map/ppermute | solution.py:364
  103.9 0.0 collective-permute-done.1
  103.9 0.1 pad_maximum_fusion.6
  104.0 0.3 convolution_bitcast_fusion
  104.4 0.3 convolution_bitcast_fusion.1
  104.7 0.3 convolution_bitcast_fusion.2
  105.1 0.9 pad_maximum_fusion.1.aux_ref
  106.0 0.0 collective-permute-done.5
  106.0 0.0 collective-permute-done.4
  106.0 0.7 fusion
  106.7 5.9 %collective-permute-done.2.top_ref = f32[13,8,1024]{2,1,0:T(8,128)S(1)} collective-permute-done((f32[13,8,1024]{2,1,0:T(8,128)}, f32[13,8,1024]{2,1,0:T(8,128)S(1)}, u32[]{:S(2)}, u32[]{:S(2)}) %collective-permute-start.2) | collective-permute-done | bytes 426016 | tf_op jit(solution)/shard_map/ppermute | solution.py:363
  112.6 0.0 copy-start
  112.6 0.0 collective-permute-done.3.bottom_ref
  112.6 0.0 copy-start.1
  112.6 0.8 copy-done
  113.4 0.2 copy-done.1
  113.6 9.1 %shard_map.65 = f32[13,32,1024]{2,1,0:T(8,128)} custom-call(f32[3,4]{1,0:T(4,128)} %coef_ref.1, f32[13,32,1024]{2,1,0:T(8,128)} %get-tuple-element.9.tile_ref, f32[4,32,1024]{2,1,0:T(8,128)} %pad_maximum_fusion.1.aux_ref, f32[13,8,1024]{2,1,0:T(8,128)} %copy-done, f32[13,8,1024]{2,1,0:T(8,128)} %copy-done.1, f32[4,8,1024]{2,1,0:T(8,128)} %get-tuple-element.14.top_aux_ref, ...), custom_call_target="tpu_custom_call" | custom-call | tf_op jit(solution)/shard_map/pallas_call | solution.py:344
  (4 shorter events, 0.1 us)
Async XLA Ops:
  0.0 99.2 %copy-start.2 = (s32[3,64]{1,0:T(4,128)S(1)}, s32[3,64]{1,0:T(4,128)}, u32[]{:S(2)}) copy-start(s32[3,64]{1,0:T(4,128)} %param.11) | copy-start | bytes 2308
  1.0 105.0 %collective-permute-start.5 = (f32[8,1024]{1,0:T(8,128)S(1)}, f32[8,1024]{1,0:T(8,128)S(1)}, u32[]{:S(2)}, u32[]{:S(2)}) collective-permute-start(f32[8,1024]{1,0:T(8,128)S(1)} %get-tuple-element.15), channel_id=1, source_target_pairs={{1,0},{2,1},{3,2},{4,3},{5,4},{6,5},{7,6},{8,7},{9,8},{10,9},{11,1... | collective-permute-start | bytes 98312 | tf_op jit(solution)/shard_map/ppermute | solution.py:372
  4.6 101.4 %collective-permute-start.4 = (f32[8,1024]{1,0:T(8,128)S(1)}, f32[8,1024]{1,0:T(8,128)S(1)}, u32[]{:S(2)}, u32[]{:S(2)}) collective-permute-start(f32[8,1024]{1,0:T(8,128)S(1)} %get-tuple-element.16), channel_id=1, source_target_pairs={{0,1},{1,2},{2,3},{3,4},{4,5},{5,6},{6,7},{7,8},{8,9},{9,10},{10,1... | collective-permute-start | bytes 98312 | tf_op jit(solution)/shard_map/ppermute | solution.py:371
  95.3 7.1 %collective-permute-start = (f32[3,64,8]{2,1,0:T(8,128)S(1)}, f32[3,64,8]{2,1,0:T(8,128)S(1)}, u32[]{:S(2)}, u32[]{:S(2)}) collective-permute-start(f32[3,64,8]{2,1,0:T(8,128)S(1)} %get-tuple-element.19), channel_id=1, source_target_pairs={{0,1},{1,2},{2,3},{3,4},{4,5},{5,6},{6,7},{7,8},{8,9},{9,10},{10,1... | collective-permute-start | bytes 18440 | tf_op jit(solution)/shard_map/ppermute | solution.py:368
  95.4 8.6 %collective-permute-start.1 = (f32[3,64,8]{2,1,0:T(8,128)S(1)}, f32[3,64,8]{2,1,0:T(8,128)S(1)}, u32[]{:S(2)}, u32[]{:S(2)}) collective-permute-start(f32[3,64,8]{2,1,0:T(8,128)S(1)} %get-tuple-element.20), channel_id=1, source_target_pairs={{1,0},{2,1},{3,2},{4,3},{5,4},{6,5},{7,6},{8,7},{9,8},{10,9},{11,1... | collective-permute-start | bytes 18440 | tf_op jit(solution)/shard_map/ppermute | solution.py:369
  99.2 13.4 %collective-permute-start.2 = (f32[13,8,1024]{2,1,0:T(8,128)}, f32[13,8,1024]{2,1,0:T(8,128)S(1)}, u32[]{:S(2)}, u32[]{:S(2)}) collective-permute-start(f32[13,8,1024]{2,1,0:T(8,128)} %get-tuple-element.11), channel_id=1, source_target_pairs={{0,1},{1,2},{2,3},{3,4},{4,5},{5,6},{6,7},{7,8},{8,9},{9,10},{10,1... | collective-permute-start | bytes 1277960 | tf_op jit(solution)/shard_map/ppermute | solution.py:363
  102.3 10.3 %collective-permute-start.3 = (f32[13,8,1024]{2,1,0:T(8,128)}, f32[13,8,1024]{2,1,0:T(8,128)S(1)}, u32[]{:S(2)}, u32[]{:S(2)}) collective-permute-start(f32[13,8,1024]{2,1,0:T(8,128)} %get-tuple-element.12), channel_id=1, source_target_pairs={{1,0},{2,1},{3,2},{4,3},{5,4},{6,5},{7,6},{8,7},{9,8},{10,9},{11,1... | collective-permute-start | bytes 1277960 | tf_op jit(solution)/shard_map/ppermute | solution.py:364
  112.6 0.8 copy-start
  112.6 0.9 copy-start.1

commit v18 on v17

--- a/solution.py
+++ b/solution.py
@@ -360,16 +360,19 @@
     count = lax.axis_size("space")
     forward = [(i, (i + 1) % count) for i in range(count)]
     backward = [(target, source) for source, target in forward]
-    top = lax.ppermute(high, "space", forward)
-    bottom = lax.ppermute(low, "space", backward)
     own_lines = jnp.moveaxis(gathered, 0, 1).reshape(
         (altimetry.shape[0], -1) + altimetry.shape[2:]
     )
     lines_above = lax.ppermute(own_lines[..., -reach:], "space", forward)
     lines_below = lax.ppermute(own_lines[..., :reach], "space", backward)
     depth = depth_levels.astype(jnp.float32)
-    depth_above = lax.ppermute(depth[-reach:], "space", forward)
-    depth_below = lax.ppermute(depth[:reach], "space", backward)
+    depth_high, depth_low, high, low = lax.optimization_barrier(
+        (depth[-reach:], depth[:reach], high, low)
+    )
+    depth_above = lax.ppermute(depth_high, "space", forward)
+    depth_below = lax.ppermute(depth_low, "space", backward)
+    top = lax.ppermute(high, "space", forward)
+    bottom = lax.ppermute(low, "space", backward)
     all_lines = jnp.concatenate([lines_above, own_lines, lines_below], axis=-1)
     columns = jnp.arange(width_y, dtype=jnp.int32)
     targets = []

time: 123 us -> 124 us (level)
  starting transfers between devices: 9.14 us -> 11.2 us
    ppermute x2, starting transfers between devices: 3.63 us -> 4.98 us  [the longest x1 4.9 us: per_device(): depth_below = lax.ppermute(depth_low, 'space', backward)]
  transfers between devices with their start and end apart: 6 -> 6, of which waited for: 2 -> 2; matrix products, arithmetic and copies ran while one was open for 4% -> 4% of each run, Pallas kernels for 73% -> 0%
where the time goes in v18:
time: 124 us
  Pallas kernels  97.9 us (79%)
  starting transfers between devices  11.2 us (9%)
  waiting for transfers between devices  8.27 us (7%)
  other arithmetic  3.5 us (3%)
  local copies, waits for them, and re-layouts  1.98 us (2%)
    pallas_call x1, Pallas kernels, resample(): pl.pallas_call(functools.partial(exchange_kernel, count, grid_cols, group...  88.8 us
    pallas_call x1, Pallas kernels, run_steps(): pl.pallas_call(stencil_kernel, out_shape=jax.ShapeDtypeStruct(tile.shape,...  9.14 us
    ppermute x1, waiting for transfers between devices, per_device(): top = lax.ppermute(high, 'space', forward)  6.71 us
    ppermute x1, starting transfers between devices, per_device(): depth_below = lax.ppermute(depth_low, 'space', backward)  4.9 us
    ppermute x1, starting transfers between devices, per_device(): lines_below = lax.ppermute(own_lines[..., :reach], 'space', backward)  3.84 us
  transfers between devices with their start and end apart: 6, of which 2 were waited for; matrix products, arithmetic and copies ran while one was open for 4% of the time, Pallas kernels for 0%

profile of v18, /device:TPU:24, one launch (start us, length us, event | category | flops | bytes accessed | tf_op | source)
XLA Modules:
  0.0 123.9 jit_solution(7464909345403029065)
XLA Ops:
  0.0 0.0 copy-start.2
  0.0 0.9 fusion.6
  1.0 88.8 %shard_map.64 = (f32[13,32,1024]{2,1,0:T(8,128)}, f32[16,3,4,32]{3,2,1,0:T(4,128)}, f32[13,8,1024]{2,1,0:T(8,128)}, f32[13,8,1024]{2,1,0:T(8,128)}) custom-call(s32[16]{0:T(128)} %anc_ref.1, f32[13,32,1024]{2,1,0:T(8,128)} %bitcast.32, f32[3,4,32]{2,1,0:T(4,128)} %alt_ref.1), custom_call_target="tpu_custom_call" | custom-call | tf_op jit(solution)/shard_map/pallas_call | solution.py:233
  89.7 0.1 collective-permute-start.4
  89.8 4.9 %collective-permute-start.5 = (f32[8,1024]{1,0:T(8,128)S(1)}, f32[8,1024]{1,0:T(8,128)S(1)}, u32[]{:S(2)}, u32[]{:S(2)}) collective-permute-start(f32[8,1024]{1,0:T(8,128)S(1)} %get-tuple-element.20), channel_id=1, source_target_pairs={{1,0},{2,1},{3,2},{4,3},{5,4},{6,5},{7,6},{8,7},{9,8},{10,9},{11,1... | collective-permute-start | bytes 98312 | tf_op jit(solution)/shard_map/ppermute | solution.py:373
  94.7 0.9 copy.8
  95.6 0.1 fusion.7
  95.7 0.1 collective-permute-start
  95.8 3.8 %collective-permute-start.1 = (f32[3,64,8]{2,1,0:T(8,128)S(1)}, f32[3,64,8]{2,1,0:T(8,128)S(1)}, u32[]{:S(2)}, u32[]{:S(2)}) collective-permute-start(f32[3,64,8]{2,1,0:T(8,128)S(1)} %get-tuple-element.28), channel_id=1, source_target_pairs={{1,0},{2,1},{3,2},{4,3},{5,4},{6,5},{7,6},{8,7},{9,8},{10,9},{11,1... | collective-permute-start | bytes 18440 | tf_op jit(solution)/shard_map/ppermute | solution.py:367
  99.6 0.0 collective-permute-start.2
  99.6 0.0 copy-done.2
  99.7 0.1 convert_reduce_fusion.2
  99.8 0.1 convert_reduce_fusion
  99.9 0.6 pad_maximum_fusion.7.hit_ref
  100.5 1.5 %collective-permute-done = f32[3,64,8]{2,1,0:T(8,128)S(1)} collective-permute-done((f32[3,64,8]{2,1,0:T(8,128)S(1)}, f32[3,64,8]{2,1,0:T(8,128)S(1)}, u32[]{:S(2)}, u32[]{:S(2)}) %collective-permute-start) | collective-permute-done | bytes 6176 | tf_op jit(solution)/shard_map/ppermute | solution.py:366
  102.1 2.3 %collective-permute-start.3 = (f32[13,8,1024]{2,1,0:T(8,128)}, f32[13,8,1024]{2,1,0:T(8,128)S(1)}, u32[]{:S(2)}, u32[]{:S(2)}) collective-permute-start(f32[13,8,1024]{2,1,0:T(8,128)} %get-tuple-element.18), channel_id=1, source_target_pairs={{1,0},{2,1},{3,2},{4,3},{5,4},{6,5},{7,6},{8,7},{9,8},{10,9},{11,1... | collective-permute-start | bytes 1277960 | tf_op jit(solution)/shard_map/ppermute | solution.py:375
  104.4 0.0 collective-permute-done.1
  104.4 0.1 pad_maximum_fusion.6
  104.5 0.3 convolution_bitcast_fusion
  104.8 0.3 convolution_bitcast_fusion.1
  105.1 0.3 convolution_bitcast_fusion.2
  105.5 0.9 pad_maximum_fusion.1.aux_ref
  106.4 0.0 collective-permute-done.4
  106.4 0.0 collective-permute-done.5
  106.4 0.7 fusion
  107.1 6.7 %collective-permute-done.2.top_ref = f32[13,8,1024]{2,1,0:T(8,128)S(1)} collective-permute-done((f32[13,8,1024]{2,1,0:T(8,128)}, f32[13,8,1024]{2,1,0:T(8,128)S(1)}, u32[]{:S(2)}, u32[]{:S(2)}) %collective-permute-start.2) | collective-permute-done | bytes 426016 | tf_op jit(solution)/shard_map/ppermute | solution.py:374
  113.8 0.0 copy-start
  113.8 0.0 collective-permute-done.3.bottom_ref
  113.8 0.0 copy-start.1
  113.8 0.8 copy-done
  114.6 0.2 copy-done.1
  114.8 9.1 %shard_map.65 = f32[13,32,1024]{2,1,0:T(8,128)} custom-call(f32[3,4]{1,0:T(4,128)} %coef_ref.1, f32[13,32,1024]{2,1,0:T(8,128)} %get-tuple-element.13.tile_ref, f32[4,32,1024]{2,1,0:T(8,128)} %pad_maximum_fusion.1.aux_ref, f32[13,8,1024]{2,1,0:T(8,128)} %copy-done, f32[13,8,1024]{2,1,0:T(8,128)} %copy-done.1, f32[4,8,1024]{2,1,0:T(8,128)} %get-tuple-element.22.top_aux_ref, ...), custom_call_target="tpu_custom_call" | custom-call | tf_op jit(solution)/shard_map/pallas_call | solution.py:344
  (4 shorter events, 0.1 us)
Async XLA Ops:
  0.0 99.7 %copy-start.2 = (s32[3,64]{1,0:T(4,128)S(1)}, s32[3,64]{1,0:T(4,128)}, u32[]{:S(2)}) copy-start(s32[3,64]{1,0:T(4,128)} %param.11) | copy-start | bytes 2308
  89.7 16.7 %collective-permute-start.4 = (f32[8,1024]{1,0:T(8,128)S(1)}, f32[8,1024]{1,0:T(8,128)S(1)}, u32[]{:S(2)}, u32[]{:S(2)}) collective-permute-start(f32[8,1024]{1,0:T(8,128)S(1)} %get-tuple-element.19), channel_id=1, source_target_pairs={{0,1},{1,2},{2,3},{3,4},{4,5},{5,6},{6,7},{7,8},{8,9},{9,10},{10,1... | collective-permute-start | bytes 98312 | tf_op jit(solution)/shard_map/ppermute | solution.py:372
  89.8 16.6 %collective-permute-start.5 = (f32[8,1024]{1,0:T(8,128)S(1)}, f32[8,1024]{1,0:T(8,128)S(1)}, u32[]{:S(2)}, u32[]{:S(2)}) collective-permute-start(f32[8,1024]{1,0:T(8,128)S(1)} %get-tuple-element.20), channel_id=1, source_target_pairs={{1,0},{2,1},{3,2},{4,3},{5,4},{6,5},{7,6},{8,7},{9,8},{10,9},{11,1... | collective-permute-start | bytes 98312 | tf_op jit(solution)/shard_map/ppermute | solution.py:373
  95.7 6.3 %collective-permute-start = (f32[3,64,8]{2,1,0:T(8,128)S(1)}, f32[3,64,8]{2,1,0:T(8,128)S(1)}, u32[]{:S(2)}, u32[]{:S(2)}) collective-permute-start(f32[3,64,8]{2,1,0:T(8,128)S(1)} %get-tuple-element.27), channel_id=1, source_target_pairs={{0,1},{1,2},{2,3},{3,4},{4,5},{5,6},{6,7},{7,8},{8,9},{9,10},{10,1... | collective-permute-start | bytes 18440 | tf_op jit(solution)/shard_map/ppermute | solution.py:366
  95.8 8.6 %collective-permute-start.1 = (f32[3,64,8]{2,1,0:T(8,128)S(1)}, f32[3,64,8]{2,1,0:T(8,128)S(1)}, u32[]{:S(2)}, u32[]{:S(2)}) collective-permute-start(f32[3,64,8]{2,1,0:T(8,128)S(1)} %get-tuple-element.28), channel_id=1, source_target_pairs={{1,0},{2,1},{3,2},{4,3},{5,4},{6,5},{7,6},{8,7},{9,8},{10,9},{11,1... | collective-permute-start | bytes 18440 | tf_op jit(solution)/shard_map/ppermute | solution.py:367
  99.6 14.2 %collective-permute-start.2 = (f32[13,8,1024]{2,1,0:T(8,128)}, f32[13,8,1024]{2,1,0:T(8,128)S(1)}, u32[]{:S(2)}, u32[]{:S(2)}) collective-permute-start(f32[13,8,1024]{2,1,0:T(8,128)} %get-tuple-element.17), channel_id=1, source_target_pairs={{0,1},{1,2},{2,3},{3,4},{4,5},{5,6},{6,7},{7,8},{8,9},{9,10},{10,1... | collective-permute-start | bytes 1277960 | tf_op jit(solution)/shard_map/ppermute | solution.py:374
  102.1 11.8 %collective-permute-start.3 = (f32[13,8,1024]{2,1,0:T(8,128)}, f32[13,8,1024]{2,1,0:T(8,128)S(1)}, u32[]{:S(2)}, u32[]{:S(2)}) collective-permute-start(f32[13,8,1024]{2,1,0:T(8,128)} %get-tuple-element.18), channel_id=1, source_target_pairs={{1,0},{2,1},{3,2},{4,3},{5,4},{6,5},{7,6},{8,7},{9,8},{10,9},{11,1... | collective-permute-start | bytes 1277960 | tf_op jit(solution)/shard_map/ppermute | solution.py:375
  113.8 0.8 copy-start
  113.8 0.9 copy-start.1

commit v19 on v15

--- a/solution.py
+++ b/solution.py
@@ -362,18 +362,15 @@
     backward = [(target, source) for source, target in forward]
     top = lax.ppermute(high, "space", forward)
     bottom = lax.ppermute(low, "space", backward)
-    all_lines = jnp.moveaxis(gathered, 0, 1).reshape(
-        (altimetry.shape[0], -1) + altimetry.shape[2:]
-    )
     columns = jnp.arange(width_y, dtype=jnp.int32)
     targets = []
     hits = []
     for step in range(STEPS):
         onehot = (obs_rows[step][:, None] == columns[None, :]).astype(jnp.float32)
         targets.append(
-            jnp.dot(
-                all_lines[step].T, onehot, precision=lax.Precision.HIGHEST,
-                preferred_element_type=jnp.float32,
+            jnp.einsum(
+                "jix,jiy->xy", gathered[:, step], onehot.reshape(gathered.shape[0], -1, width_y),
+                precision=lax.Precision.HIGHEST, preferred_element_type=jnp.float32,
             )
         )
         hits.append(jnp.sum(onehot, axis=0)[None, :])

time: 117 us -> 117 us (level)
  transfers between devices with their start and end apart: 4 -> 4, of which waited for: 1 -> 2; matrix products, arithmetic and copies ran while one was open for 2% -> 3% of each run, Pallas kernels for 0% -> 0%
where the time goes in v19:
time: 117 us; the launch traced here: 115 us
  Pallas kernels  97.8 us (84%)
  waiting for transfers between devices  7.12 us (6%)
  starting transfers between devices  6.28 us (5%)
  local copies, waits for them, and re-layouts  2.3 us (2%)
    pallas_call x1, Pallas kernels, resample(): pl.pallas_call(functools.partial(exchange_kernel, count, grid_cols, group...  88.7 us
    pallas_call x1, Pallas kernels, run_steps(): pl.pallas_call(stencil_kernel, out_shape=jax.ShapeDtypeStruct(tile.shape,...  9.14 us
    ppermute x1, waiting for transfers between devices, per_device(): bottom_aux = lax.ppermute(aux[:, :reach], 'space', backward)  6.99 us
    ppermute x1, starting transfers between devices, per_device(): bottom = lax.ppermute(low, 'space', backward)  4.9 us
  transfers between devices with their start and end apart: 4, of which 2 were waited for; matrix products, arithmetic and copies ran while one was open for 3% of the time, Pallas kernels for 0%

profile of v19, /device:TPU:24, one launch (start us, length us, event | category | flops | bytes accessed | tf_op | source)
XLA Modules:
  0.0 115.4 jit_solution(12702424695077464064)
XLA Ops:
  0.0 0.0 copy-start.6
  0.0 0.0 copy-start.5
  0.0 88.7 %shard_map.64 = (f32[13,32,1024]{2,1,0:T(8,128)}, f32[16,3,4,32]{3,2,1,0:T(4,128)}, f32[13,8,1024]{2,1,0:T(8,128)}, f32[13,8,1024]{2,1,0:T(8,128)}) custom-call(s32[16]{0:T(128)} %anc_ref.1, f32[13,32,1024]{2,1,0:T(8,128)} %bitcast.28, f32[3,4,32]{2,1,0:T(4,128)} %alt_ref.1), custom_call_target="tpu_custom_call" | custom-call | tf_op jit(solution)/shard_map/pallas_call | solution.py:233
  88.7 0.1 collective-permute-start
  88.8 4.9 %collective-permute-start.1 = (f32[13,8,1024]{2,1,0:T(8,128)}, f32[13,8,1024]{2,1,0:T(8,128)S(1)}, u32[]{:S(2)}, u32[]{:S(2)}) collective-permute-start(f32[13,8,1024]{2,1,0:T(8,128)} %get-tuple-element.12), channel_id=1, source_target_pairs={{1,0},{2,1},{3,2},{4,3},{5,4},{6,5},{7,6},{8,7},{9,8},{10,9},{11,1... | collective-permute-start | bytes 1277960 | tf_op jit(solution)/shard_map/ppermute | solution.py:364
  93.7 0.0 copy-done.6
  93.7 0.1 eq.76
  93.8 0.1 copy.21
  93.9 0.1 eq.80
  94.0 0.1 copy.23
  94.1 0.1 eq.72
  94.1 0.1 copy.19
  94.2 0.0 copy-done.5
  94.3 0.8 slice_bitcast_fusion.2
  95.1 0.3 convolution_bitcast_fusion.2
  95.4 0.3 convolution_bitcast_fusion
  95.6 0.3 convolution_bitcast_fusion.1
  96.0 0.0 copy-start
  96.0 1.3 %collective-permute-start.3 = (f32[4,8,1024]{2,1,0:T(8,128)S(1)}, f32[4,8,1024]{2,1,0:T(8,128)S(1)}, u32[]{:S(2)}, u32[]{:S(2)}) collective-permute-start(f32[4,8,1024]{2,1,0:T(8,128)S(1)} %get-tuple-element.16), channel_id=1, source_target_pairs={{1,0},{2,1},{3,2},{4,3},{5,4},{6,5},{7,6},{8,7},{9,8},{10,9},{11,1... | collective-permute-start | bytes 393224 | tf_op jit(solution)/shard_map/ppermute | solution.py:379
  97.3 0.0 collective-permute-start.2
  97.3 0.1 convert_reduce_fusion
  97.5 0.1 convert_reduce_fusion.2
  97.6 0.6 pad_maximum_fusion.1.hit_ref
  98.2 7.0 %collective-permute-done.3.bottom_aux_ref = f32[4,8,1024]{2,1,0:T(8,128)S(1)} collective-permute-done((f32[4,8,1024]{2,1,0:T(8,128)S(1)}, f32[4,8,1024]{2,1,0:T(8,128)S(1)}, u32[]{:S(2)}, u32[]{:S(2)}) %collective-permute-start.3) | collective-permute-done | bytes 131104 | tf_op jit(solution)/shard_map/ppermute | solution.py:379
  105.2 0.0 copy-start.3
  105.2 0.1 collective-permute-done.2.top_aux_ref
  105.3 0.0 copy-start.4
  105.3 0.0 collective-permute-done.top_ref
  105.3 0.0 copy-start.1
  105.3 0.0 collective-permute-done.1.bottom_ref
  105.3 0.0 copy-start.2
  105.3 0.0 copy-done
  105.3 0.5 copy-done.3
  105.8 0.1 copy-done.4
  105.9 0.2 copy-done.1
  106.1 0.1 copy-done.2
  106.3 9.1 %shard_map.65 = f32[13,32,1024]{2,1,0:T(8,128)} custom-call(f32[3,4]{1,0:T(4,128)} %coef_ref.1, f32[13,32,1024]{2,1,0:T(8,128)} %get-tuple-element.9.tile_ref, f32[4,32,1024]{2,1,0:T(8,128)} %copy-done, f32[13,8,1024]{2,1,0:T(8,128)} %copy-done.1, f32[13,8,1024]{2,1,0:T(8,128)} %copy-done.2, f32[4,8,1024]{2,1,0:T(8,128)} %copy-done.4, ...), custom_call_target="tpu_custom_call" | custom-call | tf_op jit(solution)/shard_map/pallas_call | solution.py:344
  (4 shorter events, 0.1 us)
Async XLA Ops:
  0.0 93.7 %copy-start.6 = (s32[3,64]{1,0:T(4,128)S(1)}, s32[3,64]{1,0:T(4,128)}, u32[]{:S(2)}) copy-start(s32[3,64]{1,0:T(4,128)} %param.11) | copy-start | bytes 2308
  0.0 94.2 %copy-start.5 = (s32[32,1024]{1,0:T(8,128)S(1)}, s32[32,1024]{1,0:T(8,128)}, u32[]{:S(2)}) copy-start(s32[32,1024]{1,0:T(8,128)} %param.8) | copy-start | bytes 393220
  88.7 16.6 %collective-permute-start = (f32[13,8,1024]{2,1,0:T(8,128)}, f32[13,8,1024]{2,1,0:T(8,128)S(1)}, u32[]{:S(2)}, u32[]{:S(2)}) collective-permute-start(f32[13,8,1024]{2,1,0:T(8,128)} %get-tuple-element.11), channel_id=1, source_target_pairs={{0,1},{1,2},{2,3},{3,4},{4,5},{5,6},{6,7},{7,8},{8,9},{9,10},{10,1... | collective-permute-start | bytes 1277960 | tf_op jit(solution)/shard_map/ppermute | solution.py:363
  88.8 16.5 %collective-permute-start.1 = (f32[13,8,1024]{2,1,0:T(8,128)}, f32[13,8,1024]{2,1,0:T(8,128)S(1)}, u32[]{:S(2)}, u32[]{:S(2)}) collective-permute-start(f32[13,8,1024]{2,1,0:T(8,128)} %get-tuple-element.12), channel_id=1, source_target_pairs={{1,0},{2,1},{3,2},{4,3},{5,4},{6,5},{7,6},{8,7},{9,8},{10,9},{11,1... | collective-permute-start | bytes 1277960 | tf_op jit(solution)/shard_map/ppermute | solution.py:364
  96.0 9.3 %copy-start = (f32[4,32,1024]{2,1,0:T(8,128)}, f32[4,32,1024]{2,1,0:T(8,128)S(1)}, u32[]{:S(2)}) copy-start(f32[4,32,1024]{2,1,0:T(8,128)S(1)} %pad_maximum_fusion.aux_ref) | copy-start | bytes 1572868
  96.0 9.1 %collective-permute-start.3 = (f32[4,8,1024]{2,1,0:T(8,128)S(1)}, f32[4,8,1024]{2,1,0:T(8,128)S(1)}, u32[]{:S(2)}, u32[]{:S(2)}) collective-permute-start(f32[4,8,1024]{2,1,0:T(8,128)S(1)} %get-tuple-element.16), channel_id=1, source_target_pairs={{1,0},{2,1},{3,2},{4,3},{5,4},{6,5},{7,6},{8,7},{9,8},{10,9},{11,1... | collective-permute-start | bytes 393224 | tf_op jit(solution)/shard_map/ppermute | solution.py:379
  97.3 8.0 %collective-permute-start.2 = (f32[4,8,1024]{2,1,0:T(8,128)S(1)}, f32[4,8,1024]{2,1,0:T(8,128)S(1)}, u32[]{:S(2)}, u32[]{:S(2)}) collective-permute-start(f32[4,8,1024]{2,1,0:T(8,128)S(1)} %get-tuple-element.17), channel_id=1, source_target_pairs={{0,1},{1,2},{2,3},{3,4},{4,5},{5,6},{6,7},{7,8},{8,9},{9,10},{10,1... | collective-permute-start | bytes 393224 | tf_op jit(solution)/shard_map/ppermute | solution.py:378
  105.2 0.6 copy-start.3
  105.3 0.7 copy-start.4
  105.3 0.8 copy-start.1
  105.3 1.0 copy-start.2
